TPU v7x, 256 devices: a whole 4x4x8 slice. The times are simulated.
256 devices in a mesh: context: 64 (over z, x, core), heads: 4 (over y).
Axes of the slice: x: 4, y: 4, z: 8, core: 2. Of those that a mesh axis runs over, the one named last changes fastest.
Arguments:
- residual: bfloat16 [8192, 2880], P('context'), may hold values from -6 to 6
- query_rows: bfloat16 [8192, 3584], P('context', 'heads'), may hold values from -6 to 6
- key_rows: bfloat16 [8192, 3584], P('context', 'heads'), may hold values from -6 to 6
- value_rows: bfloat16 [8192, 3584], P('context', 'heads'), may hold values from -6 to 6
- norm_gain: float32 [3584], P('heads'), may hold values from 0.1 to 1.9
- out_weight: bfloat16 [3584, 2880], P('heads'), may hold values from -0.09375 to 0.09375
- moe_gain: float32 [2880], replicated, may hold values from 0.1 to 1.9
- expert_ids: int32 [8192, 4], P('context'), may hold values from 0 to 31, all different within a row; in each aligned block of 128 rows (0 to 127, 128 to 255, ...) at most 24 rows name the same one
- gate_values: float32 [8192, 4], P('context'), may hold values from 0.2 to 1
- gate_weight: bfloat16 [64, 2880, 1440], P('context', None, 'heads'), may hold values from -0.109375 to 0.109375
- up_weight: bfloat16 [64, 2880, 1440], P('context', None, 'heads'), may hold values from -0.109375 to 0.109375
- down_weight: bfloat16 [64, 1440, 2880], P('context', 'heads'), may hold values from -0.109375 to 0.109375
Outputs:
- layer_out: bfloat16 [8192, 2880], P(('context', 'heads'))
Inputs may be any that keep to these rules, and one draw needn't show every extreme that they name: `expert_ids`: each token names 4 different experts. Among the 128 tokens of one block at most 24 name the same expert, and in every draw some expert is named by exactly 24 tokens of some block.
All inputs are finite; a program needn't handle non-finite values.
Results may differ from a plain program's by a relative error of at most 0.017.
Values may be sent and summed in bfloat16 or wider, within the bound.
No kernel may reach another device: no remote copies, remote signals or barrier semaphores. Data moves between devices by JAX's collectives and lax.ppermute only.
A program may use at most 128 MiB of HBM per device.

v0:
```python
import functools

import jax
import jax.numpy as jnp
from jax import lax
from jax.experimental import pallas as pl
from jax.experimental.pallas import tpu as pltpu
from jax.sharding import Mesh
from jax.sharding import PartitionSpec as P

HD = 64
PAIR = 2 * HD
CORES = 2
BREADTH = 4
SPARE = 48
BF = jnp.bfloat16
F32 = jnp.float32
VMEM_SPEC = pl.BlockSpec(memory_space=pltpu.VMEM)
SMEM_SPEC = pl.BlockSpec(memory_space=pltpu.SMEM)


def params(mib):
    return pltpu.CompilerParams(vmem_limit_bytes=mib << 20)


def cost(flops, moved):
    return pl.CostEstimate(flops=int(flops), bytes_accessed=int(moved), transcendentals=0)


def dot(a, b, dims=((1,), (0,))):
    return lax.dot_general(a, b, (dims, ((), ())), preferred_element_type=F32)


def state_body(core_ref, k_ref, v_ref, keep_ref, send_ref, both_ref):
    first = lax.broadcasted_iota(jnp.int32, (HD, PAIR), 1) < HD
    half = HD // 2
    for p in range(k_ref.shape[1] // PAIR):
        cols = slice(p * PAIR, (p + 1) * PAIR)
        both = dot(k_ref[:, cols], v_ref[:, cols], ((0,), (0,)))
        state = jnp.where(first, both[:HD], both[HD:]).astype(BF)
        both_ref[0, :, cols] = state[:half]
        both_ref[1, :, cols] = state[half:]
    keep_ref[...] = both_ref[core_ref[0]]
    send_ref[...] = both_ref[1 - core_ref[0]]


def inner_body(q_ref, k_ref, v_ref, o_ref):
    tokens = q_ref.shape[0]
    first = lax.broadcasted_iota(jnp.int32, (tokens, PAIR), 1) < HD
    causal = lax.broadcasted_iota(jnp.int32, (tokens, tokens), 0) >= lax.broadcasted_iota(
        jnp.int32, (tokens, tokens), 1
    )
    zero = jnp.zeros((tokens, PAIR), BF)
    for p in range(q_ref.shape[1] // PAIR):
        cols = slice(p * PAIR, (p + 1) * PAIR)
        q, k, v = q_ref[:, cols], k_ref[:, cols], v_ref[:, cols]
        inner = []
        for keep in (jnp.where(first, q, zero), jnp.where(first, zero, q)):
            scores = dot(keep, k, ((1,), (1,)))
            weights = jnp.where(causal, scores, 0.0).astype(BF)
            inner.append(dot(weights, v))
        o_ref[:, cols] = jnp.where(first, inner[0], inner[1])


def attend_body(
    place_ref, q_ref, inner_ref, mine_ref, other_ref, gain_ref, w_hbm, o0, o1, o2, o3, normed, state, w_ref, parts, sem
):
    fetch = pltpu.make_async_copy(w_hbm, w_ref, sem)
    fetch.start()
    tokens = q_ref.shape[0]
    first = lax.broadcasted_iota(jnp.int32, (tokens, PAIR), 1) < HD
    first_s = lax.broadcasted_iota(jnp.int32, (HD, PAIR), 1) < HD
    state[place_ref[1]] = mine_ref[...]
    state[1 - place_ref[1]] = other_ref[...]

    def halves_mean(x):
        a = jnp.sum(jnp.where(first, x, 0.0), axis=1, keepdims=True)
        b = jnp.sum(jnp.where(first, 0.0, x), axis=1, keepdims=True)
        return jnp.where(first, a, b) * (1.0 / HD)

    for p in range(q_ref.shape[1] // PAIR):
        cols = slice(p * PAIR, (p + 1) * PAIR)
        s = jnp.concatenate([state[0, :, cols], state[1, :, cols]], axis=0)
        s_zero = jnp.zeros_like(s)
        block = jnp.concatenate(
            [jnp.where(first_s, s, s_zero), jnp.where(first_s, s_zero, s)], axis=0
        )
        mixed = inner_ref[:, cols] + dot(q_ref[:, cols], block)
        centered = mixed - halves_mean(mixed)
        spread = halves_mean(centered * centered)
        normed[:, cols] = (centered * lax.rsqrt(spread + 1e-05) * gain_ref[:, cols]).astype(BF)
    quarter = w_ref.shape[0] // 4
    pad = jnp.zeros((tokens, o0.shape[1] - quarter), BF)
    fetch.wait()

    def project(j, carry):
        start = pl.multiple_of(lax.rem(place_ref[0] + j, 4) * quarter, quarter)
        part = dot(normed[...], w_ref[pl.ds(start, quarter), :], ((1,), (1,)))
        parts[j, :, :quarter] = part.astype(BF)
        parts[j, :, quarter:] = pad
        return carry

    lax.fori_loop(0, 4, project, 0)
    for j, o in enumerate((o0, o1, o2, o3)):
        o[...] = parts[j]


def route_body(experts, ids_ref, gates_ref, place_ref, high_ref, low_ref):
    top, tokens = ids_ref.shape
    rows = place_ref.shape[0]
    capacity = rows // experts
    expert = lax.broadcasted_iota(jnp.int32, (experts, tokens), 0)
    member = jnp.zeros((experts, tokens), F32)
    gate = jnp.zeros((experts, tokens), F32)
    for c in range(top):
        hit = ids_ref[c : c + 1, :] == expert
        member = member + jnp.where(hit, 1.0, 0.0)
        gate = gate + jnp.where(hit, gates_ref[c : c + 1, :], 0.0)
    earlier = lax.broadcasted_iota(jnp.int32, (tokens, tokens), 0) < lax.broadcasted_iota(
        jnp.int32, (tokens, tokens), 1
    )
    rank = dot(member.astype(BF), jnp.where(earlier, 1.0, 0.0).astype(BF))
    rank = jnp.where(member > 0.0, rank, -1.0)
    shape = (experts, capacity, tokens)
    slot = lax.broadcasted_iota(jnp.int32, shape, 1).astype(F32)
    placed = jnp.where(jnp.broadcast_to(rank[:, None, :], shape) == slot, 1.0, 0.0)
    weighted = (placed * jnp.broadcast_to(gate[:, None, :], shape)).reshape(rows, tokens)
    place_ref[...] = placed.reshape(rows, tokens).astype(BF)
    mix = weighted.T
    high = mix.astype(BF)
    high_ref[...] = high
    low_ref[...] = (mix - high.astype(F32)).astype(BF)


def pack_body(h_ref, p0, p1, p2, p3, res_ref, gain_ref, place_ref, packed_ref, att_ref, rows):
    quarter = att_ref.shape[1]
    start = pl.multiple_of(h_ref[0] * quarter, quarter)
    att = res_ref[pl.ds(start, quarter), :].astype(F32).T
    for p in (p0, p1, p2, p3):
        att = att + p[:, :quarter].astype(F32)
    att_ref[...] = att
    square = jnp.sum(att * att, axis=1, keepdims=True)
    high = square.astype(BF).astype(F32)
    middle = (square - high).astype(BF).astype(F32)
    low = square - high - middle
    lane = lax.broadcasted_iota(jnp.int32, (att.shape[0], SPARE), 1)
    extra = jnp.where(lane == 0, high, jnp.where(lane == 1, middle, jnp.where(lane == 2, low, 0.0)))
    rows[:, :quarter] = (att * gain_ref[...]).astype(BF)
    rows[:, quarter:] = extra.astype(BF)
    packed_ref[...] = dot(place_ref[...], rows[...]).astype(BF)


def weights_body(h_ref, gate_ref, up_ref, down_ref, mid_ref, out_ref):
    hidden, features = down_ref.shape
    quarter = features // 4
    padded = mid_ref.shape[1]
    wide = mid_ref.shape[2] // 2
    for q in range(4):
        place = lax.rem(q + 4 - h_ref[0], 4)
        cols = slice(q * quarter, (q + 1) * quarter)
        for side, ref in enumerate((gate_ref, up_ref)):
            lanes = slice(side * wide, (side + 1) * wide)
            tall = [ref[:, cols].astype(F32), jnp.zeros((wide - hidden, quarter), F32)]
            mid_ref[place, :quarter, lanes] = jnp.concatenate(tall, axis=0).T.astype(BF)
            mid_ref[place, quarter:, lanes] = jnp.zeros((padded - quarter, wide), BF)
        pad = jnp.zeros((hidden, padded - quarter), BF)
        out_ref[place] = jnp.concatenate([down_ref[:, cols], pad], axis=1)


def expert_body(features, x0, x1, x2, x3, mid0, out0, mid1, out1, t0, t1, t2, t3, held, total):
    quarter = features // 4
    hidden_count = out0.shape[1]
    wide = mid0.shape[2] // 2
    square = None
    for j, x in enumerate((x0, x1, x2, x3)):
        held[j] = x[...]
        tail = jnp.sum(x[:, quarter:].astype(F32), axis=1, keepdims=True)
        square = tail if j == 0 else square + tail
    scaling = lax.rsqrt(square * (1.0 / features) + 1e-06)
    total[...] = jnp.zeros_like(total)

    def gather(j, carry):
        row = held[j]
        total[0] += dot(row, mid0[j])
        total[1] += dot(row, mid1[j])
        return carry

    lax.fori_loop(0, 4, gather, 0)
    hidden = []
    for side in range(2):
        gate = total[side, :, :hidden_count] * scaling
        up = total[side, :, wide : wide + hidden_count] * scaling
        hidden.append((gate / (1.0 + jnp.exp(-gate)) * up).astype(BF))

    def spread(j, carry):
        held[j] = (dot(hidden[0], out0[j]) + dot(hidden[1], out1[j])).astype(BF)
        return carry

    lax.fori_loop(0, 4, spread, 0)
    for j, t in enumerate((t0, t1, t2, t3)):
        t[...] = held[j]


def mix_body(h_ref, back_ref, high_ref, low_ref, att_ref, o0, o1, o2, o3, done):
    back = back_ref[...]
    quarter = att_ref.shape[1]
    mixture = dot(high_ref[...], back) + dot(low_ref[...], back)
    done[:, :quarter] = (att_ref[...] + mixture[:, :quarter]).astype(BF)
    done[:, quarter:] = mixture[:, quarter:].astype(BF)
    share = o0.shape[0]
    for j, o in enumerate((o0, o1, o2, o3)):
        start = pl.multiple_of(lax.rem(h_ref[0] + j, 4) * share, share)
        o[...] = done[pl.ds(start, share), :]


def join_body(h_ref, r0, r1, r2, r3, o_ref, held):
    quarter = o_ref.shape[1] // 4
    for j, r in enumerate((r0, r1, r2, r3)):
        held[lax.rem(h_ref[0] + 4 - j, 4)] = r[...]
    for q in range(4):
        o_ref[:, q * quarter : (q + 1) * quarter] = held[q, :, :quarter]


def shift(x, by):
    return lax.ppermute(x, "heads", [(i, (i + by) % 4) for i in range(4)])


def swap(x):
    return lax.ppermute(x, "core", [(0, 1), (1, 0)])


def plus(*terms):
    total = terms[0].astype(F32)
    for term in terms[1:]:
        total = total + term.astype(F32)
    return total.astype(BF)


def on_device(
    residual,
    query_rows,
    key_rows,
    value_rows,
    norm_gain,
    out_weight,
    moe_gain,
    expert_ids,
    gate_values,
    gate_weight,
    up_weight,
    down_weight,
):
    tokens, width = query_rows.shape
    features = residual.shape[1]
    quarter = features // 4
    padded = quarter + SPARE
    chip = ("z", "x")
    chips = lax.axis_size("z") * lax.axis_size("x")
    h = lax.axis_index("heads").astype(jnp.int32)
    core = lax.axis_index("core").astype(jnp.int32)
    h_arr = jnp.full((1,), h, jnp.int32)
    core_arr = jnp.full((1,), core, jnp.int32)
    place_arr = jnp.stack([h, core])
    capacity = min(tokens, 3 * tokens * expert_ids.shape[1] // (2 * chips))
    rows = chips * capacity
    shape = jax.ShapeDtypeStruct

    keep, send = pl.pallas_call(
        state_body,
        out_shape=(shape((HD // 2, width), BF),) * 2,
        in_specs=[SMEM_SPEC] + [VMEM_SPEC] * 2,
        out_specs=(VMEM_SPEC,) * 2,
        scratch_shapes=[pltpu.VMEM((2, HD // 2, width), BF)],
        compiler_params=params(60),
        name="own_state",
    )(core_arr, key_rows, value_rows)
    taken = swap(send)
    inner = pl.pallas_call(
        inner_body,
        out_shape=shape((tokens, width), F32),
        in_specs=[VMEM_SPEC] * 3,
        out_specs=VMEM_SPEC,
        compiler_params=params(60),
        cost_estimate=cost(2e9, 2e6),
        name="inner",
    )(query_rows, key_rows, value_rows)
    chip_state = plus(keep, taken)
    depth, breadth = lax.axis_size("z"), lax.axis_size("x")
    beside = [
        lax.ppermute(chip_state, "x", [(i, (i + j) % breadth) for i in range(breadth)])
        for j in range(1, breadth)
    ]
    slab_state = plus(chip_state, *beside)

    def deeper(x, j):
        moved = lax.ppermute(x, "z", [(i, (i + j) % depth) for i in range(depth)])
        return jnp.where(lax.axis_index("z") >= j, moved.astype(F32), 0.0)

    near = [deeper(slab_state, 1), deeper(slab_state, 2)]
    triple = plus(slab_state, *near)
    base = jnp.zeros(keep.shape, F32)
    for term in near + [deeper(triple, j) for j in range(3, depth, 3)]:
        base = base + term
    for j, term in enumerate(beside):
        base = base + jnp.where(lax.axis_index("x") > j, term.astype(F32), 0.0)
    later = lax.axis_index("core") == 1
    mine = (base + jnp.where(later, taken.astype(F32), 0.0)).astype(BF)
    theirs = (base + jnp.where(later, 0.0, keep.astype(F32))).astype(BF)
    other = swap(theirs)

    place, mix_high, mix_low = pl.pallas_call(
        functools.partial(route_body, chips),
        out_shape=(shape((rows, tokens), BF), shape((tokens, rows), BF), shape((tokens, rows), BF)),
        in_specs=[VMEM_SPEC] * 2,
        out_specs=(VMEM_SPEC,) * 3,
        compiler_params=params(10),
        cost_estimate=cost(1e8, 1e6),
        name="route",
    )(expert_ids.T, gate_values.T)

    parts = pl.pallas_call(
        attend_body,
        out_shape=(shape((tokens, padded), BF),) * 4,
        in_specs=[SMEM_SPEC] + [VMEM_SPEC] * 5 + [pl.BlockSpec(memory_space=pltpu.HBM)],
        out_specs=(VMEM_SPEC,) * 4,
        scratch_shapes=[
            pltpu.VMEM((tokens, width), BF),
            pltpu.VMEM((2, HD // 2, width), BF),
            pltpu.VMEM((features, width), BF),
            pltpu.VMEM((4, tokens, padded), BF),
            pltpu.SemaphoreType.DMA,
        ],
        compiler_params=params(60),
        name="attend",
    )(place_arr, query_rows, inner, mine, other, norm_gain.reshape(1, width), out_weight.T)
    pieces = [parts[0]] + [shift(parts[j], j) for j in (1, 2, 3)]

    gain = lax.dynamic_index_in_dim(moe_gain.reshape(4, 1, quarter), h, 0, keepdims=False)
    packed, attended = pl.pallas_call(
        pack_body,
        out_shape=(shape((rows, padded), BF), shape((tokens, quarter), F32)),
        in_specs=[SMEM_SPEC] + [VMEM_SPEC] * 7,
        out_specs=(VMEM_SPEC,) * 2,
        scratch_shapes=[pltpu.VMEM((tokens, padded), BF)],
        compiler_params=params(12),
        name="pack",
    )(h_arr, *pieces, residual.T, gain, place)

    arrived = lax.all_to_all(
        packed.reshape(chips, capacity, padded), chip, 0, 0, tiled=True
    ).reshape(rows, padded)
    half = rows // 2
    arrived, late_h = lax.optimization_barrier((arrived, h_arr))
    low, high = arrived[:half], arrived[half:]

    minus_low, plus_low = shift(low, 1), shift(low, -1)
    hidden_count = gate_weight.shape[2]
    wide = -(-hidden_count // 128) * 128
    weights = pl.pallas_call(
        weights_body,
        out_shape=(shape((4, padded, 2 * wide), BF), shape((4, hidden_count, padded), BF)),
        in_specs=[SMEM_SPEC] + [VMEM_SPEC] * 3,
        out_specs=(VMEM_SPEC,) * 2,
        compiler_params=params(28),
        cost_estimate=cost(5e9, 13e6),
        name="weights",
    )(late_h, gate_weight[0].T, up_weight[0].T, down_weight[0])
    minus_low, plus_low, high, weights = lax.optimization_barrier(
        (minus_low, plus_low, high, weights)
    )
    other_weights = tuple(swap(x) for x in weights)

    def experts(group):
        return pl.pallas_call(
            functools.partial(expert_body, features),
            out_shape=(shape((half, padded), BF),) * 4,
            in_specs=[VMEM_SPEC] * 8,
            out_specs=(VMEM_SPEC,) * 4,
            scratch_shapes=[
                pltpu.VMEM((4, half, padded), BF),
                pltpu.VMEM((2, half, 2 * wide), F32),
            ],
            compiler_params=params(28),
            cost_estimate=cost(1e6, 1e5),
            name="experts",
        )(*group, *weights, *other_weights)

    far_low, plus_high = shift(minus_low, 1), shift(high, -1)
    far_low, plus_high, high = lax.optimization_barrier((far_low, plus_high, high))
    far_high, minus_high = shift(plus_high, -1), shift(high, 1)
    sum_low = experts((low, plus_low, far_low, minus_low))
    far_high, minus_high, sum_low = lax.optimization_barrier((far_high, minus_high, sum_low))
    via_low, got_low_plus = shift(sum_low[2], 1), shift(sum_low[3], -1)
    sum_high = experts((high, plus_high, far_high, minus_high))
    via_low, got_low_plus, sum_high = lax.optimization_barrier((via_low, got_low_plus, sum_high))
    got_low_minus = shift(plus(sum_low[1], via_low), 1)
    via_high = shift(sum_high[2], -1)
    got_low_minus, via_high, sum_high = lax.optimization_barrier((got_low_minus, via_high, sum_high))
    got_high_minus = shift(sum_high[1], 1)
    got_high_plus = shift(plus(sum_high[3], via_high), -1)
    total_low = plus(sum_low[0], got_low_minus, got_low_plus)
    total_high = plus(sum_high[0], got_high_minus, got_high_plus)
    leaving = jnp.concatenate([total_low, total_high], axis=0).reshape(chips, capacity, padded)
    returned = lax.all_to_all(leaving, chip, 0, 0, tiled=True).reshape(rows, padded)

    share = tokens // 4
    ends = pl.pallas_call(
        mix_body,
        out_shape=(shape((share, padded), BF),) * 4,
        in_specs=[SMEM_SPEC] + [VMEM_SPEC] * 4,
        out_specs=(VMEM_SPEC,) * 4,
        scratch_shapes=[pltpu.VMEM((tokens, padded), BF)],
        compiler_params=params(10),
        name="mix",
    )(h_arr, returned, mix_high, mix_low, attended)
    finals = [ends[0]] + [shift(ends[j], j) for j in (1, 2, 3)]
    return pl.pallas_call(
        join_body,
        out_shape=shape((share, features), BF),
        in_specs=[SMEM_SPEC] + [VMEM_SPEC] * 4,
        out_specs=VMEM_SPEC,
        scratch_shapes=[pltpu.VMEM((4, share, padded), BF)],
        compiler_params=params(6),
        name="join",
    )(h_arr, *finals)


def solution(mesh):
    devices = mesh.devices
    split = Mesh(
        devices.reshape(-1, BREADTH, CORES, devices.shape[1]), ("z", "x", "core", "heads")
    )
    context = ("z", "x", "core")
    in_specs = (
        P(context, None),
        P(context, "heads"),
        P(context, "heads"),
        P(context, "heads"),
        P("heads"),
        P("heads", None),
        P(),
        P(context, None),
        P(context, None),
        P(context, None, "heads"),
        P(context, None, "heads"),
        P(context, "heads", None),
    )
    return jax.shard_map(
        on_device,
        mesh=split,
        in_specs=in_specs,
        out_specs=P(("z", "x", "core", "heads"), None),
        check_vma=False,
    )
```

profile of v0, /device:TPU:8, one launch (start us, length us, event | category | flops | bytes accessed | tf_op | source)
XLA Modules:
  0.0 232.2 jit_solution(575505208632756228)
XLA Ops:
  4.2 2.8 %collective-permute-start.3 = (bf16[32,896]{1,0:T(8,128)(2,1)S(1)}, bf16[32,896]{1,0:T(8,128)(2,1)S(1)}, u32[]{:S(2)}, u32[]{:S(2)}) collective-permute-start(bf16[32,896]{1,0:T(8,128)(2,1)S(1)} %fusion.2), channel_id=1, source_target_pairs={{0,24},{8,0},{16,8},{24,16},{1,25},{9,1},{17,9},{25,17},{2,26},{10... | collective-permute-start | bytes 172040 | tf_op jit(solution)/shard_map/ppermute | solution.py:290
  9.4 3.5 %collective-permute-done.2 = bf16[32,896]{1,0:T(8,128)(2,1)S(1)} collective-permute-done((bf16[32,896]{1,0:T(8,128)(2,1)S(1)}, bf16[32,896]{1,0:T(8,128)(2,1)S(1)}, u32[]{:S(2)}, u32[]{:S(2)}) %collective-permute-start.2) | collective-permute-done | bytes 57376 | tf_op jit(solution)/shard_map/ppermute | solution.py:290
  13.6 3.3 %collective-permute-start.5 = (bf16[32,896]{1,0:T(8,128)(2,1)S(1)}, bf16[32,896]{1,0:T(8,128)(2,1)S(1)}, u32[]{:S(2)}, u32[]{:S(2)}) collective-permute-start(bf16[32,896]{1,0:T(8,128)(2,1)S(1)} %fusion.8), channel_id=1, source_target_pairs={{0,64},{32,96},{64,128},{96,160},{128,192},{160,224},{192,0},{224,... | collective-permute-start | bytes 172040 | tf_op jit(solution)/shard_map/ppermute | solution.py:296
  18.8 4.2 %inner.1.inner_ref = f32[128,896]{1,0:T(8,128)} custom-call(bf16[128,896]{1,0:T(8,128)(2,1)} %q_ref.3, bf16[128,896]{1,0:T(8,128)(2,1)} %k_ref.3, bf16[128,896]{1,0:T(8,128)(2,1)} %v_ref.3), custom_call_target="tpu_custom_call" | custom-call | flops 2000000000 | bytes 2000000 | tf_op jit(solution)/shard_map/inner/pallas_call | solution.py:278
  26.0 3.3 %collective-permute-start.6 = (bf16[32,896]{1,0:T(8,128)(2,1)S(1)}, bf16[32,896]{1,0:T(8,128)(2,1)S(1)}, u32[]{:S(2)}, u32[]{:S(2)}) collective-permute-start(bf16[32,896]{1,0:T(8,128)(2,1)S(1)} %add_convert_fusion.4), channel_id=1, source_target_pairs={{0,96},{32,128},{64,160},{96,192},{128,224},{160,0},{192,32},{224,... | collective-permute-start | bytes 172040 | tf_op jit(solution)/shard_map/ppermute | solution.py:296
  29.9 4.0 %collective-permute-done.6 = bf16[32,896]{1,0:T(8,128)(2,1)S(1)} collective-permute-done((bf16[32,896]{1,0:T(8,128)(2,1)S(1)}, bf16[32,896]{1,0:T(8,128)(2,1)S(1)}, u32[]{:S(2)}, u32[]{:S(2)}) %collective-permute-start.6) | collective-permute-done | bytes 57376 | tf_op jit(solution)/shard_map/ppermute | solution.py:296
  36.0 6.8 %attend.1 = (bf16[128,768]{1,0:T(8,128)(2,1)}, bf16[128,768]{1,0:T(8,128)(2,1)}, bf16[128,768]{1,0:T(8,128)(2,1)}, bf16[128,768]{1,0:T(8,128)(2,1)}) custom-call(s32[2]{0:T(128)} %pad_add_fusion.place_ref, bf16[128,896]{1,0:T(8,128)(2,1)} %q_ref.3, f32[128,896]{1,0:T(8,128)} %inner.1.inner_ref, bf16[32,896]{1,0:T(8,128)(2,1)} %fusion.4.mine_ref, ...), custom_call_target="tpu_custom_call" | custom-call | tf_op jit(solution)/shard_map/attend/pallas_call | solution.py:321
  50.9 3.1 %collective-permute-done.10.p2 = bf16[128,768]{1,0:T(8,128)(2,1)S(1)} collective-permute-done((bf16[128,768]{1,0:T(8,128)(2,1)}, bf16[128,768]{1,0:T(8,128)(2,1)S(1)}, u32[]{:S(2)}, u32[]{:S(2)}) %collective-permute-start.10) | collective-permute-done | bytes 196640 | tf_op jit(solution)/shard_map/ppermute | solution.py:225
  58.1 39.5 %all_to_all.10 = bf16[32,24,768]{2,1,0:T(8,128)(2,1)S(1)} all-to-all(bf16[32,24,768]{2,1,0:T(8,128)(2,1)S(1)} %bitcast.20), channel_id=1, replica_groups=mesh['z'=8,'x'=4,'core'=2,'heads'=4] {'z','x'}, dimensions={0} | all-to-all | bytes 2359296 | tf_op jit(solution)/shard_map/all_to_all | solution.py:349
  99.9 3.0 %weights.1 = (bf16[4,768,768]{2,1,0:T(8,128)(2,1)S(1)}, bf16[4,360,768]{2,1,0:T(8,128)(2,1)S(1)}) custom-call(s32[1]{0:T(128)} %bitcast.h_ref, bf16[360,2880]{1,0:T(8,128)(2,1)S(1)} %bitcast.22, bf16[360,2880]{1,0:T(8,128)(2,1)S(1)} %bitcast.23, bf16[360,2880]{1,0:T(8,128)(2,1)S(1)} %bitcast.24), custom_call_target="tpu_custom_call" | custom-call | flops 5000000000 | bytes 13000000 | tf_op jit(solution)/shard_map/weights/pallas_call | solution.py:359
  102.9 8.0 %collective-permute-done.13.x1 = bf16[384,768]{1,0:T(8,128)(2,1)S(1)} collective-permute-done((bf16[384,768]{1,0:T(8,128)(2,1)S(1)}, bf16[384,768]{1,0:T(8,128)(2,1)S(1)}, u32[]{:S(2)}, u32[]{:S(2)}) %collective-permute-start.13) | collective-permute-done | bytes 589856 | tf_op jit(solution)/shard_map/ppermute | solution.py:225
  113.5 3.0 %collective-permute-start.15 = (bf16[384,768]{1,0:T(8,128)(2,1)S(1)}, bf16[384,768]{1,0:T(8,128)(2,1)S(1)}, u32[]{:S(2)}, u32[]{:S(2)}) collective-permute-start(bf16[384,768]{1,0:T(8,128)(2,1)S(1)} %get-tuple-element.72.x0), channel_id=1, source_target_pairs={{0,3},{1,0},{2,1},{3,2},{4,7},{5,4},{6,5},{7,6},{8,11},{9,8},{10,9... | collective-permute-start | bytes 1769480 | tf_op jit(solution)/shard_map/ppermute | solution.py:225
  116.4 13.5 %collective-permute-done.14.x2 = bf16[384,768]{1,0:T(8,128)(2,1)S(1)} collective-permute-done((bf16[384,768]{1,0:T(8,128)(2,1)S(1)}, bf16[384,768]{1,0:T(8,128)(2,1)S(1)}, u32[]{:S(2)}, u32[]{:S(2)}) %collective-permute-start.14) | collective-permute-done | bytes 589856 | tf_op jit(solution)/shard_map/ppermute | solution.py:225
  129.9 3.0 %collective-permute-start.16 = (bf16[384,768]{1,0:T(8,128)(2,1)S(1)}, bf16[384,768]{1,0:T(8,128)(2,1)S(1)}, u32[]{:S(2)}, u32[]{:S(2)}) collective-permute-start(bf16[384,768]{1,0:T(8,128)(2,1)S(1)} %collective-permute-done.15.x1), channel_id=1, source_target_pairs={{0,3},{1,0},{2,1},{3,2},{4,7},{5,4},{6,5},{7,6},{8,11},{9,8},{10,9... | collective-permute-start | bytes 1769480 | tf_op jit(solution)/shard_map/ppermute | solution.py:225
  132.9 8.8 %experts.2 = (bf16[384,768]{1,0:T(8,128)(2,1)S(1)}, bf16[384,768]{1,0:T(8,128)(2,1)S(1)}, bf16[384,768]{1,0:T(8,128)(2,1)S(1)}, bf16[384,768]{1,0:T(8,128)(2,1)S(1)}) custom-call(bf16[384,768]{1,0:T(8,128)(2,1)S(1)} %get-tuple-element.112.x0, bf16[384,768]{1,0:T(8,128)(2,1)S(1)} %collective-permute-done.13.x1, ...), custom_call_target="tpu_custom_call" | custom-call | flops 1000000 | bytes 100000 | tf_op jit(solution)/shard_map/experts/pallas_call | solution.py:374
  141.7 3.2 %collective-permute-done.16.x2 = bf16[384,768]{1,0:T(8,128)(2,1)S(1)} collective-permute-done((bf16[384,768]{1,0:T(8,128)(2,1)S(1)}, bf16[384,768]{1,0:T(8,128)(2,1)S(1)}, u32[]{:S(2)}, u32[]{:S(2)}) %collective-permute-start.16) | collective-permute-done | bytes 589856 | tf_op jit(solution)/shard_map/ppermute | solution.py:225
  144.9 3.0 %collective-permute-done.17.x3 = bf16[384,768]{1,0:T(8,128)(2,1)S(1)} collective-permute-done((bf16[384,768]{1,0:T(8,128)(2,1)S(1)}, bf16[384,768]{1,0:T(8,128)(2,1)S(1)}, u32[]{:S(2)}, u32[]{:S(2)}) %collective-permute-start.17) | collective-permute-done | bytes 589856 | tf_op jit(solution)/shard_map/ppermute | solution.py:225
  147.9 3.0 %collective-permute-start.21 = (bf16[384,768]{1,0:T(8,128)(2,1)S(1)}, bf16[384,768]{1,0:T(8,128)(2,1)S(1)}, u32[]{:S(2)}, u32[]{:S(2)}) collective-permute-start(bf16[384,768]{1,0:T(8,128)(2,1)S(1)} %get-tuple-element.84), channel_id=1, source_target_pairs={{0,3},{1,0},{2,1},{3,2},{4,7},{5,4},{6,5},{7,6},{8,11},{9,8},{10,9... | collective-permute-start | bytes 1769480 | tf_op jit(solution)/shard_map/ppermute | solution.py:225
  150.8 8.8 %experts.3 = (bf16[384,768]{1,0:T(8,128)(2,1)S(1)}, bf16[384,768]{1,0:T(8,128)(2,1)S(1)}, bf16[384,768]{1,0:T(8,128)(2,1)S(1)}, bf16[384,768]{1,0:T(8,128)(2,1)S(1)}) custom-call(bf16[384,768]{1,0:T(8,128)(2,1)S(1)} %get-tuple-element.72.x0, bf16[384,768]{1,0:T(8,128)(2,1)S(1)} %collective-permute-done.15.x1, ...), custom_call_target="tpu_custom_call" | custom-call | flops 1000000 | bytes 100000 | tf_op jit(solution)/shard_map/experts/pallas_call | solution.py:374
  165.2 10.1 %collective-permute-done.22 = bf16[384,768]{1,0:T(8,128)(2,1)S(1)} collective-permute-done((bf16[384,768]{1,0:T(8,128)(2,1)S(1)}, bf16[384,768]{1,0:T(8,128)(2,1)S(1)}, u32[]{:S(2)}, u32[]{:S(2)}) %collective-permute-start.22) | collective-permute-done | bytes 589856 | tf_op jit(solution)/shard_map/ppermute | solution.py:225
  175.3 3.4 %collective-permute-done.23 = bf16[384,768]{1,0:T(8,128)(2,1)S(1)} collective-permute-done((bf16[384,768]{1,0:T(8,128)(2,1)S(1)}, bf16[384,768]{1,0:T(8,128)(2,1)S(1)}, u32[]{:S(2)}, u32[]{:S(2)}) %collective-permute-start.23) | collective-permute-done | bytes 589856 | tf_op jit(solution)/shard_map/ppermute | solution.py:225
  181.2 8.6 %collective-permute-done.25 = bf16[384,768]{1,0:T(8,128)(2,1)S(1)} collective-permute-done((bf16[384,768]{1,0:T(8,128)(2,1)S(1)}, bf16[384,768]{1,0:T(8,128)(2,1)S(1)}, u32[]{:S(2)}, u32[]{:S(2)}) %collective-permute-start.25) | collective-permute-done | bytes 589856 | tf_op jit(solution)/shard_map/ppermute | solution.py:225
  190.4 31.6 %all_to_all.11 = bf16[32,24,768]{2,1,0:T(8,128)(2,1)S(1)} all-to-all(bf16[32,24,768]{2,1,0:T(8,128)(2,1)S(1)} %bitcast.29), channel_id=1, replica_groups=mesh['z'=8,'x'=4,'core'=2,'heads'=4] {'z','x'}, dimensions={0} | all-to-all | bytes 2359296 | tf_op jit(solution)/shard_map/all_to_all | solution.py:404
  224.4 2.9 %collective-permute-start.27 = (bf16[32,768]{1,0:T(8,128)(2,1)S(1)}, bf16[32,768]{1,0:T(8,128)(2,1)S(1)}, u32[]{:S(2)}, u32[]{:S(2)}) collective-permute-start(bf16[32,768]{1,0:T(8,128)(2,1)S(1)} %get-tuple-element.107), channel_id=1, source_target_pairs={{0,2},{1,3},{2,0},{3,1},{4,6},{5,7},{6,4},{7,5},{8,10},{9,11},{10,... | collective-permute-start | bytes 147464 | tf_op jit(solution)/shard_map/ppermute | solution.py:225
  (83 shorter events, 47.7 us)
Async XLA Ops:
  7.1 5.8 %collective-permute-start.2 = (bf16[32,896]{1,0:T(8,128)(2,1)S(1)}, bf16[32,896]{1,0:T(8,128)(2,1)S(1)}, u32[]{:S(2)}, u32[]{:S(2)}) collective-permute-start(bf16[32,896]{1,0:T(8,128)(2,1)S(1)} %fusion.2), channel_id=1, source_target_pairs={{0,16},{8,24},{16,0},{24,8},{1,17},{9,25},{17,1},{25,9},{2,18},{10... | collective-permute-start | bytes 172040 | tf_op jit(solution)/shard_map/ppermute | solution.py:290
  7.9 5.6 %collective-permute-start.1 = (bf16[32,896]{1,0:T(8,128)(2,1)S(1)}, bf16[32,896]{1,0:T(8,128)(2,1)S(1)}, u32[]{:S(2)}, u32[]{:S(2)}) collective-permute-start(bf16[32,896]{1,0:T(8,128)(2,1)S(1)} %fusion.2), channel_id=1, source_target_pairs={{0,8},{8,16},{16,24},{24,0},{1,9},{9,17},{17,25},{25,1},{2,10},{10... | collective-permute-start | bytes 172040 | tf_op jit(solution)/shard_map/ppermute | solution.py:290
  13.6 10.0 %collective-permute-start.5 = (bf16[32,896]{1,0:T(8,128)(2,1)S(1)}, bf16[32,896]{1,0:T(8,128)(2,1)S(1)}, u32[]{:S(2)}, u32[]{:S(2)}) collective-permute-start(bf16[32,896]{1,0:T(8,128)(2,1)S(1)} %fusion.8), channel_id=1, source_target_pairs={{0,64},{32,96},{64,128},{96,160},{128,192},{160,224},{192,0},{224,... | collective-permute-start | bytes 172040 | tf_op jit(solution)/shard_map/ppermute | solution.py:296
  16.9 6.7 %collective-permute-start.4 = (bf16[32,896]{1,0:T(8,128)(2,1)S(1)}, bf16[32,896]{1,0:T(8,128)(2,1)S(1)}, u32[]{:S(2)}, u32[]{:S(2)}) collective-permute-start(bf16[32,896]{1,0:T(8,128)(2,1)S(1)} %fusion.8), channel_id=1, source_target_pairs={{0,32},{32,64},{64,96},{96,128},{128,160},{160,192},{192,224},{224... | collective-permute-start | bytes 172040 | tf_op jit(solution)/shard_map/ppermute | solution.py:296
  23.7 6.2 %collective-permute-start.7 = (bf16[32,896]{1,0:T(8,128)(2,1)S(1)}, bf16[32,896]{1,0:T(8,128)(2,1)S(1)}, u32[]{:S(2)}, u32[]{:S(2)}) collective-permute-start(bf16[32,896]{1,0:T(8,128)(2,1)S(1)} %add_convert_fusion.4), channel_id=1, source_target_pairs={{0,192},{32,224},{64,0},{96,32},{128,64},{160,96},{192,128},{224,1... | collective-permute-start | bytes 172040 | tf_op jit(solution)/shard_map/ppermute | solution.py:296
  26.0 8.0 %collective-permute-start.6 = (bf16[32,896]{1,0:T(8,128)(2,1)S(1)}, bf16[32,896]{1,0:T(8,128)(2,1)S(1)}, u32[]{:S(2)}, u32[]{:S(2)}) collective-permute-start(bf16[32,896]{1,0:T(8,128)(2,1)S(1)} %add_convert_fusion.4), channel_id=1, source_target_pairs={{0,96},{32,128},{64,160},{96,192},{128,224},{160,0},{192,32},{224,... | collective-permute-start | bytes 172040 | tf_op jit(solution)/shard_map/ppermute | solution.py:296
  42.8 8.0 %collective-permute-start.9 = (bf16[128,768]{1,0:T(8,128)(2,1)}, bf16[128,768]{1,0:T(8,128)(2,1)S(1)}, u32[]{:S(2)}, u32[]{:S(2)}) collective-permute-start(bf16[128,768]{1,0:T(8,128)(2,1)} %get-tuple-element.60), channel_id=1, source_target_pairs={{0,1},{1,2},{2,3},{3,0},{4,5},{5,6},{6,7},{7,4},{8,9},{9,10},{10,1... | collective-permute-start | bytes 589832 | tf_op jit(solution)/shard_map/ppermute | solution.py:225
  44.5 9.5 %collective-permute-start.10 = (bf16[128,768]{1,0:T(8,128)(2,1)}, bf16[128,768]{1,0:T(8,128)(2,1)S(1)}, u32[]{:S(2)}, u32[]{:S(2)}) collective-permute-start(bf16[128,768]{1,0:T(8,128)(2,1)} %get-tuple-element.61), channel_id=1, source_target_pairs={{0,2},{1,3},{2,0},{3,1},{4,6},{5,7},{6,4},{7,5},{8,10},{9,11},{10,... | collective-permute-start | bytes 589832 | tf_op jit(solution)/shard_map/ppermute | solution.py:225
  45.4 11.0 %collective-permute-start.11 = (bf16[128,768]{1,0:T(8,128)(2,1)}, bf16[128,768]{1,0:T(8,128)(2,1)S(1)}, u32[]{:S(2)}, u32[]{:S(2)}) collective-permute-start(bf16[128,768]{1,0:T(8,128)(2,1)} %get-tuple-element.62), channel_id=1, source_target_pairs={{0,3},{1,0},{2,1},{3,2},{4,7},{5,4},{6,5},{7,6},{8,11},{9,8},{10,9... | collective-permute-start | bytes 589832 | tf_op jit(solution)/shard_map/ppermute | solution.py:225
  97.6 13.2 %collective-permute-start.13 = (bf16[384,768]{1,0:T(8,128)(2,1)S(1)}, bf16[384,768]{1,0:T(8,128)(2,1)S(1)}, u32[]{:S(2)}, u32[]{:S(2)}) collective-permute-start(bf16[384,768]{1,0:T(8,128)(2,1)S(1)} %get-tuple-element.112.x0), channel_id=1, source_target_pairs={{0,3},{1,0},{2,1},{3,2},{4,7},{5,4},{6,5},{7,6},{8,11},{9,8},{10,9... | collective-permute-start | bytes 1769480 | tf_op jit(solution)/shard_map/ppermute | solution.py:225
  98.4 14.5 %collective-permute-start.12 = (bf16[384,768]{1,0:T(8,128)(2,1)S(1)}, bf16[384,768]{1,0:T(8,128)(2,1)S(1)}, u32[]{:S(2)}, u32[]{:S(2)}) collective-permute-start(bf16[384,768]{1,0:T(8,128)(2,1)S(1)} %get-tuple-element.112.x0), channel_id=1, source_target_pairs={{0,1},{1,2},{2,3},{3,0},{4,5},{5,6},{6,7},{7,4},{8,9},{9,10},{10,1... | collective-permute-start | bytes 1769480 | tf_op jit(solution)/shard_map/ppermute | solution.py:225
  112.9 19.9 %collective-permute-start.18 = (bf16[4,768,768]{2,1,0:T(8,128)(2,1)S(1)}, bf16[4,768,768]{2,1,0:T(8,128)(2,1)S(1)}, u32[]{:S(2)}, u32[]{:S(2)}) collective-permute-start(bf16[4,768,768]{2,1,0:T(8,128)(2,1)S(1)} %get-tuple-element.75.mid0), channel_id=1, source_target_pairs={{0,4},{4,0},{1,5},{5,1},{2,6},{6,2},{3,7},{7,3},{8,12},{12,8},{9,1... | collective-permute-start | bytes 14155784 | tf_op jit(solution)/shard_map/ppermute | solution.py:229
  112.9 19.9 %collective-permute-start.19 = (bf16[4,360,768]{2,1,0:T(8,128)(2,1)S(1)}, bf16[4,360,768]{2,1,0:T(8,128)(2,1)S(1)}, u32[]{:S(2)}, u32[]{:S(2)}) collective-permute-start(bf16[4,360,768]{2,1,0:T(8,128)(2,1)S(1)} %get-tuple-element.76.out0), channel_id=1, source_target_pairs={{0,4},{4,0},{1,5},{5,1},{2,6},{6,2},{3,7},{7,3},{8,12},{12,8},{9,1... | collective-permute-start | bytes 6635528 | tf_op jit(solution)/shard_map/ppermute | solution.py:229
  113.4 16.4 %collective-permute-start.14 = (bf16[384,768]{1,0:T(8,128)(2,1)S(1)}, bf16[384,768]{1,0:T(8,128)(2,1)S(1)}, u32[]{:S(2)}, u32[]{:S(2)}) collective-permute-start(bf16[384,768]{1,0:T(8,128)(2,1)S(1)} %collective-permute-done.12.x3), channel_id=1, source_target_pairs={{0,1},{1,2},{2,3},{3,0},{4,5},{5,6},{6,7},{7,4},{8,9},{9,10},{10,1... | collective-permute-start | bytes 1769480 | tf_op jit(solution)/shard_map/ppermute | solution.py:225
  113.5 16.4 %collective-permute-start.15 = (bf16[384,768]{1,0:T(8,128)(2,1)S(1)}, bf16[384,768]{1,0:T(8,128)(2,1)S(1)}, u32[]{:S(2)}, u32[]{:S(2)}) collective-permute-start(bf16[384,768]{1,0:T(8,128)(2,1)S(1)} %get-tuple-element.72.x0), channel_id=1, source_target_pairs={{0,3},{1,0},{2,1},{3,2},{4,7},{5,4},{6,5},{7,6},{8,11},{9,8},{10,9... | collective-permute-start | bytes 1769480 | tf_op jit(solution)/shard_map/ppermute | solution.py:225
  129.9 15.0 %collective-permute-start.16 = (bf16[384,768]{1,0:T(8,128)(2,1)S(1)}, bf16[384,768]{1,0:T(8,128)(2,1)S(1)}, u32[]{:S(2)}, u32[]{:S(2)}) collective-permute-start(bf16[384,768]{1,0:T(8,128)(2,1)S(1)} %collective-permute-done.15.x1), channel_id=1, source_target_pairs={{0,3},{1,0},{2,1},{3,2},{4,7},{5,4},{6,5},{7,6},{8,11},{9,8},{10,9... | collective-permute-start | bytes 1769480 | tf_op jit(solution)/shard_map/ppermute | solution.py:225
  132.9 15.0 %collective-permute-start.17 = (bf16[384,768]{1,0:T(8,128)(2,1)S(1)}, bf16[384,768]{1,0:T(8,128)(2,1)S(1)}, u32[]{:S(2)}, u32[]{:S(2)}) collective-permute-start(bf16[384,768]{1,0:T(8,128)(2,1)S(1)} %get-tuple-element.72.x0), channel_id=1, source_target_pairs={{0,1},{1,2},{2,3},{3,0},{4,5},{5,6},{6,7},{7,4},{8,9},{9,10},{10,1... | collective-permute-start | bytes 1769480 | tf_op jit(solution)/shard_map/ppermute | solution.py:225
  147.8 14.1 %collective-permute-start.20 = (bf16[384,768]{1,0:T(8,128)(2,1)S(1)}, bf16[384,768]{1,0:T(8,128)(2,1)S(1)}, u32[]{:S(2)}, u32[]{:S(2)}) collective-permute-start(bf16[384,768]{1,0:T(8,128)(2,1)S(1)} %get-tuple-element.83), channel_id=1, source_target_pairs={{0,1},{1,2},{2,3},{3,0},{4,5},{5,6},{6,7},{7,4},{8,9},{9,10},{10,1... | collective-permute-start | bytes 1769480 | tf_op jit(solution)/shard_map/ppermute | solution.py:225
  147.9 14.1 %collective-permute-start.21 = (bf16[384,768]{1,0:T(8,128)(2,1)S(1)}, bf16[384,768]{1,0:T(8,128)(2,1)S(1)}, u32[]{:S(2)}, u32[]{:S(2)}) collective-permute-start(bf16[384,768]{1,0:T(8,128)(2,1)S(1)} %get-tuple-element.84), channel_id=1, source_target_pairs={{0,3},{1,0},{2,1},{3,2},{4,7},{5,4},{6,5},{7,6},{8,11},{9,8},{10,9... | collective-permute-start | bytes 1769480 | tf_op jit(solution)/shard_map/ppermute | solution.py:225
  162.1 13.2 %collective-permute-start.22 = (bf16[384,768]{1,0:T(8,128)(2,1)S(1)}, bf16[384,768]{1,0:T(8,128)(2,1)S(1)}, u32[]{:S(2)}, u32[]{:S(2)}) collective-permute-start(bf16[384,768]{1,0:T(8,128)(2,1)S(1)} %add_convert_fusion.3), channel_id=1, source_target_pairs={{0,1},{1,2},{2,3},{3,0},{4,5},{5,6},{6,7},{7,4},{8,9},{9,10},{10,1... | collective-permute-start | bytes 1769480 | tf_op jit(solution)/shard_map/ppermute | solution.py:225
  164.5 14.2 %collective-permute-start.23 = (bf16[384,768]{1,0:T(8,128)(2,1)S(1)}, bf16[384,768]{1,0:T(8,128)(2,1)S(1)}, u32[]{:S(2)}, u32[]{:S(2)}) collective-permute-start(bf16[384,768]{1,0:T(8,128)(2,1)S(1)} %get-tuple-element.92), channel_id=1, source_target_pairs={{0,3},{1,0},{2,1},{3,2},{4,7},{5,4},{6,5},{7,6},{8,11},{9,8},{10,9... | collective-permute-start | bytes 1769480 | tf_op jit(solution)/shard_map/ppermute | solution.py:225
  178.8 10.9 %collective-permute-start.25 = (bf16[384,768]{1,0:T(8,128)(2,1)S(1)}, bf16[384,768]{1,0:T(8,128)(2,1)S(1)}, u32[]{:S(2)}, u32[]{:S(2)}) collective-permute-start(bf16[384,768]{1,0:T(8,128)(2,1)S(1)} %add_convert_fusion.1), channel_id=1, source_target_pairs={{0,3},{1,0},{2,1},{3,2},{4,7},{5,4},{6,5},{7,6},{8,11},{9,8},{10,9... | collective-permute-start | bytes 1769480 | tf_op jit(solution)/shard_map/ppermute | solution.py:225
  178.9 11.2 %collective-permute-start.24 = (bf16[384,768]{1,0:T(8,128)(2,1)S(1)}, bf16[384,768]{1,0:T(8,128)(2,1)S(1)}, u32[]{:S(2)}, u32[]{:S(2)}) collective-permute-start(bf16[384,768]{1,0:T(8,128)(2,1)S(1)} %get-tuple-element.99), channel_id=1, source_target_pairs={{0,1},{1,2},{2,3},{3,0},{4,5},{5,6},{6,7},{7,4},{8,9},{9,10},{10,1... | collective-permute-start | bytes 1769480 | tf_op jit(solution)/shard_map/ppermute | solution.py:225
  222.6 5.7 %collective-permute-start.26 = (bf16[32,768]{1,0:T(8,128)(2,1)S(1)}, bf16[32,768]{1,0:T(8,128)(2,1)S(1)}, u32[]{:S(2)}, u32[]{:S(2)}) collective-permute-start(bf16[32,768]{1,0:T(8,128)(2,1)S(1)} %get-tuple-element.106), channel_id=1, source_target_pairs={{0,1},{1,2},{2,3},{3,0},{4,5},{5,6},{6,7},{7,4},{8,9},{9,10},{10,1... | collective-permute-start | bytes 147464 | tf_op jit(solution)/shard_map/ppermute | solution.py:225
  (16 other events, 192.1 us)
where the time goes:
time: 233 us; the launch traced here: 232 us
  waiting for transfers between devices  76.6 us (33%)
  blocking collectives  71.1 us (31%)
  starting transfers between devices  43 us (18%)
  Pallas kernels  36 us (15%)
  other arithmetic  3.06 us (1%)
  local copies, waits for them, and re-layouts  2.35 us (1%)
    ppermute x18, waiting for transfers between devices, shift(): return lax.ppermute(x, 'heads', [(i, (i + by) % 4) for i in range(4)])  65.7 us
    all_to_all x1, blocking collectives, on_device(): lax.all_to_all(packed.reshape(chips, capacity, padded), chip, 0, 0, tiled...  39.5 us
    all_to_all x1, blocking collectives, on_device(): lax.all_to_all(leaving, chip, 0, 0, tiled=True).reshape(rows, padded)  31.6 us
    ppermute x18, starting transfers between devices, shift(): return lax.ppermute(x, 'heads', [(i, (i + by) % 4) for i in range(4)])  27 us
    pallas_call x2, Pallas kernels, experts(): pl.pallas_call(functools.partial(expert_body, features), out_shape=(shape...  17.7 us
    ppermute x4, starting transfers between devices, deeper(): moved = lax.ppermute(x, 'z', [(i, (i + j) % depth) for i in range(depth)])  10.8 us
    pallas_call x1, Pallas kernels, on_device(): pl.pallas_call(attend_body, out_shape=(shape((tokens, padded), BF),) * 4,...  6.85 us
    ppermute x3, waiting for transfers between devices, on_device(): lax.ppermute(chip_state, 'x', [(i, (i + j) % breadth) for i in range(brea...  4.74 us
  transfers between devices with their start and end apart: 29, of which 21 were waited for; matrix products, arithmetic and copies ran while one was open for 1% of the time, Pallas kernels for 11%

commit v1 on v0

--- a/solution.py
+++ b/solution.py
@@ -31,7 +31,7 @@
     return lax.dot_general(a, b, (dims, ((), ())), preferred_element_type=F32)
 
 
-def state_body(core_ref, k_ref, v_ref, keep_ref, send_ref, both_ref):
+def state_body(at_ref, k_ref, v_ref, keep_ref, send_ref, both_ref):
     first = lax.broadcasted_iota(jnp.int32, (HD, PAIR), 1) < HD
     half = HD // 2
     for p in range(k_ref.shape[1] // PAIR):
@@ -40,8 +40,29 @@
         state = jnp.where(first, both[:HD], both[HD:]).astype(BF)
         both_ref[0, :, cols] = state[:half]
         both_ref[1, :, cols] = state[half:]
-    keep_ref[...] = both_ref[core_ref[0]]
-    send_ref[...] = both_ref[1 - core_ref[0]]
+    keep_ref[...] = both_ref[at_ref[1]]
+    send_ref[...] = both_ref[1 - at_ref[1]]
+
+
+def flag(condition):
+    return jnp.where(condition, 1.0, 0.0)
+
+
+def triple_body(at_ref, slab_ref, near_ref, next_ref, o_ref):
+    z = at_ref[2]
+    total = slab_ref[...].astype(F32) + flag(z >= 1) * near_ref[...].astype(F32)
+    o_ref[...] = (total + flag(z >= 2) * next_ref[...].astype(F32)).astype(BF)
+
+
+def before_body(at_ref, keep_ref, taken_ref, *rest):
+    mine_ref, theirs_ref = rest[-2:]
+    z, x, later = at_ref[2], at_ref[3], flag(at_ref[1] == 1)
+    weights = [flag(z >= j) for j in (1, 2, 3, 6)] + [flag(x > j) for j in range(3)]
+    base = jnp.zeros(keep_ref.shape, F32)
+    for weight, ref in zip(weights, rest[:-2]):
+        base = base + weight * ref[...].astype(F32)
+    mine_ref[...] = (base + later * taken_ref[...].astype(F32)).astype(BF)
+    theirs_ref[...] = (base + (1.0 - later) * keep_ref[...].astype(F32)).astype(BF)
 
 
 def inner_body(q_ref, k_ref, v_ref, o_ref):
@@ -63,15 +84,13 @@
 
 
 def attend_body(
-    place_ref, q_ref, inner_ref, mine_ref, other_ref, gain_ref, w_hbm, o0, o1, o2, o3, normed, state, w_ref, parts, sem
+    at_ref, q_ref, inner_ref, mine_ref, other_ref, gain_ref, w_ref, o0, o1, o2, o3, normed, state
 ):
-    fetch = pltpu.make_async_copy(w_hbm, w_ref, sem)
-    fetch.start()
     tokens = q_ref.shape[0]
     first = lax.broadcasted_iota(jnp.int32, (tokens, PAIR), 1) < HD
     first_s = lax.broadcasted_iota(jnp.int32, (HD, PAIR), 1) < HD
-    state[place_ref[1]] = mine_ref[...]
-    state[1 - place_ref[1]] = other_ref[...]
+    state[at_ref[1]] = mine_ref[...]
+    state[1 - at_ref[1]] = other_ref[...]
 
     def halves_mean(x):
         a = jnp.sum(jnp.where(first, x, 0.0), axis=1, keepdims=True)
@@ -91,21 +110,14 @@
         normed[:, cols] = (centered * lax.rsqrt(spread + 1e-05) * gain_ref[:, cols]).astype(BF)
     quarter = w_ref.shape[0] // 4
     pad = jnp.zeros((tokens, o0.shape[1] - quarter), BF)
-    fetch.wait()
-
-    def project(j, carry):
-        start = pl.multiple_of(lax.rem(place_ref[0] + j, 4) * quarter, quarter)
+    for j, o in enumerate((o0, o1, o2, o3)):
+        start = pl.multiple_of(lax.rem(at_ref[0] + j, 4) * quarter, quarter)
         part = dot(normed[...], w_ref[pl.ds(start, quarter), :], ((1,), (1,)))
-        parts[j, :, :quarter] = part.astype(BF)
-        parts[j, :, quarter:] = pad
-        return carry
-
-    lax.fori_loop(0, 4, project, 0)
-    for j, o in enumerate((o0, o1, o2, o3)):
-        o[...] = parts[j]
-
-
-def route_body(experts, ids_ref, gates_ref, place_ref, high_ref, low_ref):
+        o[:, :quarter] = part.astype(BF)
+        o[:, quarter:] = pad
+
+
+def route_body(experts, ids_ref, gates_ref, place_ref, higat_ref, low_ref):
     top, tokens = ids_ref.shape
     rows = place_ref.shape[0]
     capacity = rows // experts
@@ -128,13 +140,13 @@
     place_ref[...] = placed.reshape(rows, tokens).astype(BF)
     mix = weighted.T
     high = mix.astype(BF)
-    high_ref[...] = high
+    higat_ref[...] = high
     low_ref[...] = (mix - high.astype(F32)).astype(BF)
 
 
-def pack_body(h_ref, p0, p1, p2, p3, res_ref, gain_ref, place_ref, packed_ref, att_ref, rows):
+def pack_body(at_ref, p0, p1, p2, p3, res_ref, gain_ref, place_ref, packed_ref, att_ref, rows, gains):
     quarter = att_ref.shape[1]
-    start = pl.multiple_of(h_ref[0] * quarter, quarter)
+    start = pl.multiple_of(at_ref[0] * quarter, quarter)
     att = res_ref[pl.ds(start, quarter), :].astype(F32).T
     for p in (p0, p1, p2, p3):
         att = att + p[:, :quarter].astype(F32)
@@ -145,18 +157,20 @@
     low = square - high - middle
     lane = lax.broadcasted_iota(jnp.int32, (att.shape[0], SPARE), 1)
     extra = jnp.where(lane == 0, high, jnp.where(lane == 1, middle, jnp.where(lane == 2, low, 0.0)))
-    rows[:, :quarter] = (att * gain_ref[...]).astype(BF)
+    for q in range(4):
+        gains[q] = gain_ref[:, q * quarter : (q + 1) * quarter]
+    rows[:, :quarter] = (att * gains[at_ref[0]]).astype(BF)
     rows[:, quarter:] = extra.astype(BF)
     packed_ref[...] = dot(place_ref[...], rows[...]).astype(BF)
 
 
-def weights_body(h_ref, gate_ref, up_ref, down_ref, mid_ref, out_ref):
+def weights_body(at_ref, gate_ref, up_ref, down_ref, mid_ref, out_ref):
     hidden, features = down_ref.shape
     quarter = features // 4
     padded = mid_ref.shape[1]
     wide = mid_ref.shape[2] // 2
     for q in range(4):
-        place = lax.rem(q + 4 - h_ref[0], 4)
+        place = lax.rem(q + 4 - at_ref[0], 4)
         cols = slice(q * quarter, (q + 1) * quarter)
         for side, ref in enumerate((gate_ref, up_ref)):
             lanes = slice(side * wide, (side + 1) * wide)
@@ -201,22 +215,22 @@
         t[...] = held[j]
 
 
-def mix_body(h_ref, back_ref, high_ref, low_ref, att_ref, o0, o1, o2, o3, done):
+def mix_body(at_ref, back_ref, higat_ref, low_ref, att_ref, o0, o1, o2, o3, done):
     back = back_ref[...]
     quarter = att_ref.shape[1]
-    mixture = dot(high_ref[...], back) + dot(low_ref[...], back)
+    mixture = dot(higat_ref[...], back) + dot(low_ref[...], back)
     done[:, :quarter] = (att_ref[...] + mixture[:, :quarter]).astype(BF)
     done[:, quarter:] = mixture[:, quarter:].astype(BF)
     share = o0.shape[0]
     for j, o in enumerate((o0, o1, o2, o3)):
-        start = pl.multiple_of(lax.rem(h_ref[0] + j, 4) * share, share)
+        start = pl.multiple_of(lax.rem(at_ref[0] + j, 4) * share, share)
         o[...] = done[pl.ds(start, share), :]
 
 
-def join_body(h_ref, r0, r1, r2, r3, o_ref, held):
+def join_body(at_ref, r0, r1, r2, r3, o_ref, held):
     quarter = o_ref.shape[1] // 4
     for j, r in enumerate((r0, r1, r2, r3)):
-        held[lax.rem(h_ref[0] + 4 - j, 4)] = r[...]
+        held[lax.rem(at_ref[0] + 4 - j, 4)] = r[...]
     for q in range(4):
         o_ref[:, q * quarter : (q + 1) * quarter] = held[q, :, :quarter]
 
@@ -256,11 +270,8 @@
     padded = quarter + SPARE
     chip = ("z", "x")
     chips = lax.axis_size("z") * lax.axis_size("x")
-    h = lax.axis_index("heads").astype(jnp.int32)
-    core = lax.axis_index("core").astype(jnp.int32)
-    h_arr = jnp.full((1,), h, jnp.int32)
-    core_arr = jnp.full((1,), core, jnp.int32)
-    place_arr = jnp.stack([h, core])
+    at = jnp.stack([lax.axis_index(name) for name in ("heads", "core", "z", "x")])
+    at, key_rows = lax.optimization_barrier((at.astype(jnp.int32), key_rows))
     capacity = min(tokens, 3 * tokens * expert_ids.shape[1] // (2 * chips))
     rows = chips * capacity
     shape = jax.ShapeDtypeStruct
@@ -273,14 +284,14 @@
         scratch_shapes=[pltpu.VMEM((2, HD // 2, width), BF)],
         compiler_params=params(60),
         name="own_state",
-    )(core_arr, key_rows, value_rows)
+    )(at, key_rows, value_rows)
     taken = swap(send)
     inner = pl.pallas_call(
         inner_body,
         out_shape=shape((tokens, width), F32),
         in_specs=[VMEM_SPEC] * 3,
         out_specs=VMEM_SPEC,
-        compiler_params=params(60),
+        compiler_params=params(28),
         cost_estimate=cost(2e9, 2e6),
         name="inner",
     )(query_rows, key_rows, value_rows)
@@ -293,19 +304,26 @@
     slab_state = plus(chip_state, *beside)
 
     def deeper(x, j):
-        moved = lax.ppermute(x, "z", [(i, (i + j) % depth) for i in range(depth)])
-        return jnp.where(lax.axis_index("z") >= j, moved.astype(F32), 0.0)
+        return lax.ppermute(x, "z", [(i, (i + j) % depth) for i in range(depth)])
 
     near = [deeper(slab_state, 1), deeper(slab_state, 2)]
-    triple = plus(slab_state, *near)
-    base = jnp.zeros(keep.shape, F32)
-    for term in near + [deeper(triple, j) for j in range(3, depth, 3)]:
-        base = base + term
-    for j, term in enumerate(beside):
-        base = base + jnp.where(lax.axis_index("x") > j, term.astype(F32), 0.0)
-    later = lax.axis_index("core") == 1
-    mine = (base + jnp.where(later, taken.astype(F32), 0.0)).astype(BF)
-    theirs = (base + jnp.where(later, 0.0, keep.astype(F32))).astype(BF)
+    near, inner = lax.optimization_barrier((near, inner))
+    triple = pl.pallas_call(
+        triple_body,
+        out_shape=shape(keep.shape, BF),
+        in_specs=[SMEM_SPEC] + [VMEM_SPEC] * 3,
+        out_specs=VMEM_SPEC,
+        compiler_params=params(28),
+        name="triple",
+    )(at, slab_state, *near)
+    mine, theirs = pl.pallas_call(
+        before_body,
+        out_shape=(shape(keep.shape, BF),) * 2,
+        in_specs=[SMEM_SPEC] + [VMEM_SPEC] * 9,
+        out_specs=(VMEM_SPEC,) * 2,
+        compiler_params=params(28),
+        name="before",
+    )(at, keep, taken, *near, deeper(triple, 3), deeper(triple, 6), *beside)
     other = swap(theirs)
 
     place, mix_high, mix_low = pl.pallas_call(
@@ -313,7 +331,7 @@
         out_shape=(shape((rows, tokens), BF), shape((tokens, rows), BF), shape((tokens, rows), BF)),
         in_specs=[VMEM_SPEC] * 2,
         out_specs=(VMEM_SPEC,) * 3,
-        compiler_params=params(10),
+        compiler_params=params(28),
         cost_estimate=cost(1e8, 1e6),
         name="route",
     )(expert_ids.T, gate_values.T)
@@ -321,36 +339,29 @@
     parts = pl.pallas_call(
         attend_body,
         out_shape=(shape((tokens, padded), BF),) * 4,
-        in_specs=[SMEM_SPEC] + [VMEM_SPEC] * 5 + [pl.BlockSpec(memory_space=pltpu.HBM)],
+        in_specs=[SMEM_SPEC] + [VMEM_SPEC] * 6,
         out_specs=(VMEM_SPEC,) * 4,
-        scratch_shapes=[
-            pltpu.VMEM((tokens, width), BF),
-            pltpu.VMEM((2, HD // 2, width), BF),
-            pltpu.VMEM((features, width), BF),
-            pltpu.VMEM((4, tokens, padded), BF),
-            pltpu.SemaphoreType.DMA,
-        ],
-        compiler_params=params(60),
+        scratch_shapes=[pltpu.VMEM((tokens, width), BF), pltpu.VMEM((2, HD // 2, width), BF)],
+        compiler_params=params(28),
         name="attend",
-    )(place_arr, query_rows, inner, mine, other, norm_gain.reshape(1, width), out_weight.T)
+    )(at, query_rows, inner, mine, other, norm_gain.reshape(1, width), out_weight.T)
     pieces = [parts[0]] + [shift(parts[j], j) for j in (1, 2, 3)]
 
-    gain = lax.dynamic_index_in_dim(moe_gain.reshape(4, 1, quarter), h, 0, keepdims=False)
     packed, attended = pl.pallas_call(
         pack_body,
         out_shape=(shape((rows, padded), BF), shape((tokens, quarter), F32)),
         in_specs=[SMEM_SPEC] + [VMEM_SPEC] * 7,
         out_specs=(VMEM_SPEC,) * 2,
-        scratch_shapes=[pltpu.VMEM((tokens, padded), BF)],
-        compiler_params=params(12),
+        scratch_shapes=[pltpu.VMEM((tokens, padded), BF), pltpu.VMEM((4, 1, quarter), F32)],
+        compiler_params=params(28),
         name="pack",
-    )(h_arr, *pieces, residual.T, gain, place)
+    )(at, *pieces, residual.T, moe_gain.reshape(1, features), place)
 
     arrived = lax.all_to_all(
         packed.reshape(chips, capacity, padded), chip, 0, 0, tiled=True
     ).reshape(rows, padded)
     half = rows // 2
-    arrived, late_h = lax.optimization_barrier((arrived, h_arr))
+    arrived, late_h = lax.optimization_barrier((arrived, at))
     low, high = arrived[:half], arrived[half:]
 
     minus_low, plus_low = shift(low, 1), shift(low, -1)
@@ -389,7 +400,6 @@
     far_low, plus_high, high = lax.optimization_barrier((far_low, plus_high, high))
     far_high, minus_high = shift(plus_high, -1), shift(high, 1)
     sum_low = experts((low, plus_low, far_low, minus_low))
-    far_high, minus_high, sum_low = lax.optimization_barrier((far_high, minus_high, sum_low))
     via_low, got_low_plus = shift(sum_low[2], 1), shift(sum_low[3], -1)
     sum_high = experts((high, plus_high, far_high, minus_high))
     via_low, got_low_plus, sum_high = lax.optimization_barrier((via_low, got_low_plus, sum_high))
@@ -410,9 +420,9 @@
         in_specs=[SMEM_SPEC] + [VMEM_SPEC] * 4,
         out_specs=(VMEM_SPEC,) * 4,
         scratch_shapes=[pltpu.VMEM((tokens, padded), BF)],
-        compiler_params=params(10),
+        compiler_params=params(28),
         name="mix",
-    )(h_arr, returned, mix_high, mix_low, attended)
+    )(at, returned, mix_high, mix_low, attended)
     finals = [ends[0]] + [shift(ends[j], j) for j in (1, 2, 3)]
     return pl.pallas_call(
         join_body,
@@ -420,9 +430,9 @@
         in_specs=[SMEM_SPEC] + [VMEM_SPEC] * 4,
         out_specs=VMEM_SPEC,
         scratch_shapes=[pltpu.VMEM((4, share, padded), BF)],
-        compiler_params=params(6),
+        compiler_params=params(28),
         name="join",
-    )(h_arr, *finals)
+    )(at, *finals)
 
 
 def solution(mesh):

time: 233 us -> 232 us (level)
  Pallas kernels: 36 us -> 33.4 us
    pallas_call x1, Pallas kernels: 6.85 us -> 2.77 us  [on_device(): pl.pallas_call(attend_body, out_shape=(shape((tokens, padded), BF),) * 4,...]
  transfers between devices with their start and end apart: 29 -> 29, of which waited for: 21 -> 23; matrix products, arithmetic and copies ran while one was open for 1% -> 0% of each run, Pallas kernels for 11% -> 10%
where the time goes in v1:
time: 232 us
  waiting for transfers between devices  78.3 us (34%)
  blocking collectives  73.3 us (32%)
  starting transfers between devices  41.6 us (18%)
  Pallas kernels  33.4 us (14%)
  local copies, waits for them, and re-layouts  2.96 us (1%)
    ppermute x18, waiting for transfers between devices, shift(): return lax.ppermute(x, 'heads', [(i, (i + by) % 4) for i in range(4)])  66.2 us
    all_to_all x1, blocking collectives, on_device(): lax.all_to_all(packed.reshape(chips, capacity, padded), chip, 0, 0, tiled...  39.5 us
    all_to_all x1, blocking collectives, on_device(): lax.all_to_all(leaving, chip, 0, 0, tiled=True).reshape(rows, padded)  33.7 us
    ppermute x18, starting transfers between devices, shift(): return lax.ppermute(x, 'heads', [(i, (i + by) % 4) for i in range(4)])  25.7 us
    pallas_call x2, Pallas kernels, experts(): pl.pallas_call(functools.partial(expert_body, features), out_shape=(shape...  17.7 us
    ppermute x4, starting transfers between devices, deeper(): return lax.ppermute(x, 'z', [(i, (i + j) % depth) for i in range(depth)])  10.8 us
    ppermute x3, waiting for transfers between devices, on_device(): lax.ppermute(chip_state, 'x', [(i, (i + j) % breadth) for i in range(brea...  4.74 us
    ppermute x4, waiting for transfers between devices, deeper(): return lax.ppermute(x, 'z', [(i, (i + j) % depth) for i in range(depth)])  4.69 us
  transfers between devices with their start and end apart: 29, of which 23 were waited for; matrix products, arithmetic and copies ran while one was open for 0% of the time, Pallas kernels for 10%

profile of v1, /device:TPU:8, one launch (start us, length us, event | category | flops | bytes accessed | tf_op | source)
XLA Modules:
  0.0 232.1 jit_solution(1542368338501150659)
XLA Ops:
  4.9 2.8 %collective-permute-start.3 = (bf16[32,896]{1,0:T(8,128)(2,1)S(1)}, bf16[32,896]{1,0:T(8,128)(2,1)S(1)}, u32[]{:S(2)}, u32[]{:S(2)}) collective-permute-start(bf16[32,896]{1,0:T(8,128)(2,1)S(1)} %add_convert_fusion.5), channel_id=1, source_target_pairs={{0,24},{8,0},{16,8},{24,16},{1,25},{9,1},{17,9},{25,17},{2,26},{10... | collective-permute-start | bytes 172040 | tf_op jit(solution)/shard_map/ppermute | solution.py:301
  10.1 3.5 %collective-permute-done.2.rest_5_ = bf16[32,896]{1,0:T(8,128)(2,1)S(1)} collective-permute-done((bf16[32,896]{1,0:T(8,128)(2,1)S(1)}, bf16[32,896]{1,0:T(8,128)(2,1)S(1)}, u32[]{:S(2)}, u32[]{:S(2)}) %collective-permute-start.2) | collective-permute-done | bytes 57376 | tf_op jit(solution)/shard_map/ppermute | solution.py:301
  14.2 3.3 %collective-permute-start.5 = (bf16[32,896]{1,0:T(8,128)(2,1)S(1)}, bf16[32,896]{1,0:T(8,128)(2,1)S(1)}, u32[]{:S(2)}, u32[]{:S(2)}) collective-permute-start(bf16[32,896]{1,0:T(8,128)(2,1)S(1)} %add_convert_fusion.4.slab_ref), channel_id=1, source_target_pairs={{0,64},{32,96},{64,128},{96,160},{128,192},{160,224},{192,0},{224,... | collective-permute-start | bytes 172040 | tf_op jit(solution)/shard_map/ppermute | solution.py:307
  27.5 3.3 %collective-permute-start.6 = (bf16[32,896]{1,0:T(8,128)(2,1)S(1)}, bf16[32,896]{1,0:T(8,128)(2,1)S(1)}, u32[]{:S(2)}, u32[]{:S(2)}) collective-permute-start(bf16[32,896]{1,0:T(8,128)(2,1)S(1)} %triple.1), channel_id=1, source_target_pairs={{0,96},{32,128},{64,160},{96,192},{128,224},{160,0},{192,32},{224,... | collective-permute-start | bytes 172040 | tf_op jit(solution)/shard_map/ppermute | solution.py:307
  31.1 4.3 %collective-permute-done.6.rest_2_ = bf16[32,896]{1,0:T(8,128)(2,1)S(1)} collective-permute-done((bf16[32,896]{1,0:T(8,128)(2,1)S(1)}, bf16[32,896]{1,0:T(8,128)(2,1)S(1)}, u32[]{:S(2)}, u32[]{:S(2)}) %collective-permute-start.6) | collective-permute-done | bytes 57376 | tf_op jit(solution)/shard_map/ppermute | solution.py:307
  37.5 2.8 %attend.1 = (bf16[128,768]{1,0:T(8,128)(2,1)S(1)}, bf16[128,768]{1,0:T(8,128)(2,1)S(1)}, bf16[128,768]{1,0:T(8,128)(2,1)S(1)}, bf16[128,768]{1,0:T(8,128)(2,1)S(1)}) custom-call(s32[4]{0:T(128)S(1)} %copy-done.7, bf16[128,896]{1,0:T(8,128)(2,1)S(1)} %copy-done.6, f32[128,896]{1,0:T(8,128)S(1)} %inner.1.inner_ref, ...), custom_call_target="tpu_custom_call" | custom-call | tf_op jit(solution)/shard_map/attend/pallas_call | solution.py:339
  42.8 2.4 %collective-permute-start.11 = (bf16[128,768]{1,0:T(8,128)(2,1)S(1)}, bf16[128,768]{1,0:T(8,128)(2,1)S(1)}, u32[]{:S(2)}, u32[]{:S(2)}) collective-permute-start(bf16[128,768]{1,0:T(8,128)(2,1)S(1)} %get-tuple-element.70), channel_id=1, source_target_pairs={{0,3},{1,0},{2,1},{3,2},{4,7},{5,4},{6,5},{7,6},{8,11},{9,8},{10,9... | collective-permute-start | bytes 589832 | tf_op jit(solution)/shard_map/ppermute | solution.py:239
  45.6 2.4 %collective-permute-done.9.p1 = bf16[128,768]{1,0:T(8,128)(2,1)S(1)} collective-permute-done((bf16[128,768]{1,0:T(8,128)(2,1)S(1)}, bf16[128,768]{1,0:T(8,128)(2,1)S(1)}, u32[]{:S(2)}, u32[]{:S(2)}) %collective-permute-start.9) | collective-permute-done | bytes 196640 | tf_op jit(solution)/shard_map/ppermute | solution.py:239
  48.1 3.1 %collective-permute-done.10.p2 = bf16[128,768]{1,0:T(8,128)(2,1)S(1)} collective-permute-done((bf16[128,768]{1,0:T(8,128)(2,1)S(1)}, bf16[128,768]{1,0:T(8,128)(2,1)S(1)}, u32[]{:S(2)}, u32[]{:S(2)}) %collective-permute-start.10) | collective-permute-done | bytes 196640 | tf_op jit(solution)/shard_map/ppermute | solution.py:239
  51.2 2.4 %collective-permute-done.11.p3 = bf16[128,768]{1,0:T(8,128)(2,1)S(1)} collective-permute-done((bf16[128,768]{1,0:T(8,128)(2,1)S(1)}, bf16[128,768]{1,0:T(8,128)(2,1)S(1)}, u32[]{:S(2)}, u32[]{:S(2)}) %collective-permute-start.11) | collective-permute-done | bytes 196640 | tf_op jit(solution)/shard_map/ppermute | solution.py:239
  54.9 39.5 %all_to_all.10 = bf16[32,24,768]{2,1,0:T(8,128)(2,1)S(1)} all-to-all(bf16[32,24,768]{2,1,0:T(8,128)(2,1)S(1)} %bitcast.21), channel_id=1, replica_groups=mesh['z'=8,'x'=4,'core'=2,'heads'=4] {'z','x'}, dimensions={0} | all-to-all | bytes 2359296 | tf_op jit(solution)/shard_map/all_to_all | solution.py:360
  96.7 3.5 %weights.1 = (bf16[4,768,768]{2,1,0:T(8,128)(2,1)S(1)}, bf16[4,360,768]{2,1,0:T(8,128)(2,1)S(1)}) custom-call(s32[4]{0:T(128)S(1)} %copy-done.7, bf16[360,2880]{1,0:T(8,128)(2,1)S(1)} %bitcast.23, bf16[360,2880]{1,0:T(8,128)(2,1)S(1)} %bitcast.24, bf16[360,2880]{1,0:T(8,128)(2,1)S(1)} %bitcast.25), custom_call_target="tpu_custom_call" | custom-call | flops 5000000000 | bytes 13000000 | tf_op jit(solution)/shard_map/weights/pallas_call | solution.py:370
  100.2 7.5 %collective-permute-done.13.x1 = bf16[384,768]{1,0:T(8,128)(2,1)S(1)} collective-permute-done((bf16[384,768]{1,0:T(8,128)(2,1)S(1)}, bf16[384,768]{1,0:T(8,128)(2,1)S(1)}, u32[]{:S(2)}, u32[]{:S(2)}) %collective-permute-start.13) | collective-permute-done | bytes 589856 | tf_op jit(solution)/shard_map/ppermute | solution.py:239
  110.3 3.0 %collective-permute-start.15 = (bf16[384,768]{1,0:T(8,128)(2,1)S(1)}, bf16[384,768]{1,0:T(8,128)(2,1)S(1)}, u32[]{:S(2)}, u32[]{:S(2)}) collective-permute-start(bf16[384,768]{1,0:T(8,128)(2,1)S(1)} %get-tuple-element.87.x0), channel_id=1, source_target_pairs={{0,3},{1,0},{2,1},{3,2},{4,7},{5,4},{6,5},{7,6},{8,11},{9,8},{10,9... | collective-permute-start | bytes 1769480 | tf_op jit(solution)/shard_map/ppermute | solution.py:239
  113.2 13.5 %collective-permute-done.14.x2 = bf16[384,768]{1,0:T(8,128)(2,1)S(1)} collective-permute-done((bf16[384,768]{1,0:T(8,128)(2,1)S(1)}, bf16[384,768]{1,0:T(8,128)(2,1)S(1)}, u32[]{:S(2)}, u32[]{:S(2)}) %collective-permute-start.14) | collective-permute-done | bytes 589856 | tf_op jit(solution)/shard_map/ppermute | solution.py:239
  126.7 2.3 %collective-permute-start.21 = (bf16[384,768]{1,0:T(8,128)(2,1)S(1)}, bf16[384,768]{1,0:T(8,128)(2,1)S(1)}, u32[]{:S(2)}, u32[]{:S(2)}) collective-permute-start(bf16[384,768]{1,0:T(8,128)(2,1)S(1)} %get-tuple-element.87.x0), channel_id=1, source_target_pairs={{0,1},{1,2},{2,3},{3,0},{4,5},{5,6},{6,7},{7,4},{8,9},{9,10},{10,1... | collective-permute-start | bytes 1769480 | tf_op jit(solution)/shard_map/ppermute | solution.py:239
  129.7 8.8 %experts.2 = (bf16[384,768]{1,0:T(8,128)(2,1)S(1)}, bf16[384,768]{1,0:T(8,128)(2,1)S(1)}, bf16[384,768]{1,0:T(8,128)(2,1)S(1)}, bf16[384,768]{1,0:T(8,128)(2,1)S(1)}) custom-call(bf16[384,768]{1,0:T(8,128)(2,1)S(1)} %get-tuple-element.112.x0, bf16[384,768]{1,0:T(8,128)(2,1)S(1)} %collective-permute-done.13.x1, ...), custom_call_target="tpu_custom_call" | custom-call | flops 1000000 | bytes 100000 | tf_op jit(solution)/shard_map/experts/pallas_call | solution.py:385
  138.5 2.6 %collective-permute-start.18 = (bf16[384,768]{1,0:T(8,128)(2,1)S(1)}, bf16[384,768]{1,0:T(8,128)(2,1)S(1)}, u32[]{:S(2)}, u32[]{:S(2)}) collective-permute-start(bf16[384,768]{1,0:T(8,128)(2,1)S(1)} %get-tuple-element.85), channel_id=1, source_target_pairs={{0,1},{1,2},{2,3},{3,0},{4,5},{5,6},{6,7},{7,4},{8,9},{9,10},{10,1... | collective-permute-start | bytes 1769480 | tf_op jit(solution)/shard_map/ppermute | solution.py:239
  143.1 3.0 %collective-permute-done.20.x2 = bf16[384,768]{1,0:T(8,128)(2,1)S(1)} collective-permute-done((bf16[384,768]{1,0:T(8,128)(2,1)S(1)}, bf16[384,768]{1,0:T(8,128)(2,1)S(1)}, u32[]{:S(2)}, u32[]{:S(2)}) %collective-permute-start.20) | collective-permute-done | bytes 589856 | tf_op jit(solution)/shard_map/ppermute | solution.py:239
  146.0 8.8 %experts.3 = (bf16[384,768]{1,0:T(8,128)(2,1)S(1)}, bf16[384,768]{1,0:T(8,128)(2,1)S(1)}, bf16[384,768]{1,0:T(8,128)(2,1)S(1)}, bf16[384,768]{1,0:T(8,128)(2,1)S(1)}) custom-call(bf16[384,768]{1,0:T(8,128)(2,1)S(1)} %get-tuple-element.87.x0, bf16[384,768]{1,0:T(8,128)(2,1)S(1)} %collective-permute-done.15.x1, ...), custom_call_target="tpu_custom_call" | custom-call | flops 1000000 | bytes 100000 | tf_op jit(solution)/shard_map/experts/pallas_call | solution.py:385
  159.0 11.4 %collective-permute-done.22 = bf16[384,768]{1,0:T(8,128)(2,1)S(1)} collective-permute-done((bf16[384,768]{1,0:T(8,128)(2,1)S(1)}, bf16[384,768]{1,0:T(8,128)(2,1)S(1)}, u32[]{:S(2)}, u32[]{:S(2)}) %collective-permute-start.22) | collective-permute-done | bytes 589856 | tf_op jit(solution)/shard_map/ppermute | solution.py:239
  174.4 10.1 %collective-permute-done.25 = bf16[384,768]{1,0:T(8,128)(2,1)S(1)} collective-permute-done((bf16[384,768]{1,0:T(8,128)(2,1)S(1)}, bf16[384,768]{1,0:T(8,128)(2,1)S(1)}, u32[]{:S(2)}, u32[]{:S(2)}) %collective-permute-start.25) | collective-permute-done | bytes 589856 | tf_op jit(solution)/shard_map/ppermute | solution.py:239
  187.1 33.7 %all_to_all.11 = bf16[32,24,768]{2,1,0:T(8,128)(2,1)S(1)} all-to-all(bf16[32,24,768]{2,1,0:T(8,128)(2,1)S(1)} %bitcast.29), channel_id=1, replica_groups=mesh['z'=8,'x'=4,'core'=2,'heads'=4] {'z','x'}, dimensions={0} | all-to-all | bytes 2359296 | tf_op jit(solution)/shard_map/all_to_all | solution.py:414
  221.9 4.7 %collective-permute-start.27 = (bf16[32,768]{1,0:T(8,128)(2,1)S(1)}, bf16[32,768]{1,0:T(8,128)(2,1)S(1)}, u32[]{:S(2)}, u32[]{:S(2)}) collective-permute-start(bf16[32,768]{1,0:T(8,128)(2,1)S(1)} %get-tuple-element.109), channel_id=1, source_target_pairs={{0,2},{1,3},{2,0},{3,1},{4,6},{5,7},{6,4},{7,5},{8,10},{9,11},{10,... | collective-permute-start | bytes 147464 | tf_op jit(solution)/shard_map/ppermute | solution.py:239
  (89 shorter events, 48.8 us)
Async XLA Ops:
  7.7 5.8 %collective-permute-start.2 = (bf16[32,896]{1,0:T(8,128)(2,1)S(1)}, bf16[32,896]{1,0:T(8,128)(2,1)S(1)}, u32[]{:S(2)}, u32[]{:S(2)}) collective-permute-start(bf16[32,896]{1,0:T(8,128)(2,1)S(1)} %add_convert_fusion.5), channel_id=1, source_target_pairs={{0,16},{8,24},{16,0},{24,8},{1,17},{9,25},{17,1},{25,9},{2,18},{10... | collective-permute-start | bytes 172040 | tf_op jit(solution)/shard_map/ppermute | solution.py:301
  8.5 5.6 %collective-permute-start.1 = (bf16[32,896]{1,0:T(8,128)(2,1)S(1)}, bf16[32,896]{1,0:T(8,128)(2,1)S(1)}, u32[]{:S(2)}, u32[]{:S(2)}) collective-permute-start(bf16[32,896]{1,0:T(8,128)(2,1)S(1)} %add_convert_fusion.5), channel_id=1, source_target_pairs={{0,8},{8,16},{16,24},{24,0},{1,9},{9,17},{17,25},{25,1},{2,10},{10... | collective-permute-start | bytes 172040 | tf_op jit(solution)/shard_map/ppermute | solution.py:301
  14.2 10.3 %collective-permute-start.5 = (bf16[32,896]{1,0:T(8,128)(2,1)S(1)}, bf16[32,896]{1,0:T(8,128)(2,1)S(1)}, u32[]{:S(2)}, u32[]{:S(2)}) collective-permute-start(bf16[32,896]{1,0:T(8,128)(2,1)S(1)} %add_convert_fusion.4.slab_ref), channel_id=1, source_target_pairs={{0,64},{32,96},{64,128},{96,160},{128,192},{160,224},{192,0},{224,... | collective-permute-start | bytes 172040 | tf_op jit(solution)/shard_map/ppermute | solution.py:307
  17.6 7.0 %collective-permute-start.4 = (bf16[32,896]{1,0:T(8,128)(2,1)S(1)}, bf16[32,896]{1,0:T(8,128)(2,1)S(1)}, u32[]{:S(2)}, u32[]{:S(2)}) collective-permute-start(bf16[32,896]{1,0:T(8,128)(2,1)S(1)} %add_convert_fusion.4.slab_ref), channel_id=1, source_target_pairs={{0,32},{32,64},{64,96},{96,128},{128,160},{160,192},{192,224},{224... | collective-permute-start | bytes 172040 | tf_op jit(solution)/shard_map/ppermute | solution.py:307
  25.2 5.9 %collective-permute-start.7 = (bf16[32,896]{1,0:T(8,128)(2,1)S(1)}, bf16[32,896]{1,0:T(8,128)(2,1)S(1)}, u32[]{:S(2)}, u32[]{:S(2)}) collective-permute-start(bf16[32,896]{1,0:T(8,128)(2,1)S(1)} %triple.1), channel_id=1, source_target_pairs={{0,192},{32,224},{64,0},{96,32},{128,64},{160,96},{192,128},{224,1... | collective-permute-start | bytes 172040 | tf_op jit(solution)/shard_map/ppermute | solution.py:307
  27.5 8.0 %collective-permute-start.6 = (bf16[32,896]{1,0:T(8,128)(2,1)S(1)}, bf16[32,896]{1,0:T(8,128)(2,1)S(1)}, u32[]{:S(2)}, u32[]{:S(2)}) collective-permute-start(bf16[32,896]{1,0:T(8,128)(2,1)S(1)} %triple.1), channel_id=1, source_target_pairs={{0,96},{32,128},{64,160},{96,192},{128,224},{160,0},{192,32},{224,... | collective-permute-start | bytes 172040 | tf_op jit(solution)/shard_map/ppermute | solution.py:307
  40.2 7.8 %collective-permute-start.9 = (bf16[128,768]{1,0:T(8,128)(2,1)S(1)}, bf16[128,768]{1,0:T(8,128)(2,1)S(1)}, u32[]{:S(2)}, u32[]{:S(2)}) collective-permute-start(bf16[128,768]{1,0:T(8,128)(2,1)S(1)} %get-tuple-element.68), channel_id=1, source_target_pairs={{0,1},{1,2},{2,3},{3,0},{4,5},{5,6},{6,7},{7,4},{8,9},{9,10},{10,1... | collective-permute-start | bytes 589832 | tf_op jit(solution)/shard_map/ppermute | solution.py:239
  41.9 9.3 %collective-permute-start.10 = (bf16[128,768]{1,0:T(8,128)(2,1)S(1)}, bf16[128,768]{1,0:T(8,128)(2,1)S(1)}, u32[]{:S(2)}, u32[]{:S(2)}) collective-permute-start(bf16[128,768]{1,0:T(8,128)(2,1)S(1)} %get-tuple-element.69), channel_id=1, source_target_pairs={{0,2},{1,3},{2,0},{3,1},{4,6},{5,7},{6,4},{7,5},{8,10},{9,11},{10,... | collective-permute-start | bytes 589832 | tf_op jit(solution)/shard_map/ppermute | solution.py:239
  42.8 10.8 %collective-permute-start.11 = (bf16[128,768]{1,0:T(8,128)(2,1)S(1)}, bf16[128,768]{1,0:T(8,128)(2,1)S(1)}, u32[]{:S(2)}, u32[]{:S(2)}) collective-permute-start(bf16[128,768]{1,0:T(8,128)(2,1)S(1)} %get-tuple-element.70), channel_id=1, source_target_pairs={{0,3},{1,0},{2,1},{3,2},{4,7},{5,4},{6,5},{7,6},{8,11},{9,8},{10,9... | collective-permute-start | bytes 589832 | tf_op jit(solution)/shard_map/ppermute | solution.py:239
  94.5 13.1 %collective-permute-start.13 = (bf16[384,768]{1,0:T(8,128)(2,1)S(1)}, bf16[384,768]{1,0:T(8,128)(2,1)S(1)}, u32[]{:S(2)}, u32[]{:S(2)}) collective-permute-start(bf16[384,768]{1,0:T(8,128)(2,1)S(1)} %get-tuple-element.112.x0), channel_id=1, source_target_pairs={{0,3},{1,0},{2,1},{3,2},{4,7},{5,4},{6,5},{7,6},{8,11},{9,8},{10,9... | collective-permute-start | bytes 1769480 | tf_op jit(solution)/shard_map/ppermute | solution.py:239
  95.4 14.4 %collective-permute-start.12 = (bf16[384,768]{1,0:T(8,128)(2,1)S(1)}, bf16[384,768]{1,0:T(8,128)(2,1)S(1)}, u32[]{:S(2)}, u32[]{:S(2)}) collective-permute-start(bf16[384,768]{1,0:T(8,128)(2,1)S(1)} %get-tuple-element.112.x0), channel_id=1, source_target_pairs={{0,1},{1,2},{2,3},{3,0},{4,5},{5,6},{6,7},{7,4},{8,9},{9,10},{10,1... | collective-permute-start | bytes 1769480 | tf_op jit(solution)/shard_map/ppermute | solution.py:239
  109.8 19.9 %collective-permute-start.16 = (bf16[4,768,768]{2,1,0:T(8,128)(2,1)S(1)}, bf16[4,768,768]{2,1,0:T(8,128)(2,1)S(1)}, u32[]{:S(2)}, u32[]{:S(2)}) collective-permute-start(bf16[4,768,768]{2,1,0:T(8,128)(2,1)S(1)} %get-tuple-element.81.mid0), channel_id=1, source_target_pairs={{0,4},{4,0},{1,5},{5,1},{2,6},{6,2},{3,7},{7,3},{8,12},{12,8},{9,1... | collective-permute-start | bytes 14155784 | tf_op jit(solution)/shard_map/ppermute | solution.py:243
  109.8 19.9 %collective-permute-start.17 = (bf16[4,360,768]{2,1,0:T(8,128)(2,1)S(1)}, bf16[4,360,768]{2,1,0:T(8,128)(2,1)S(1)}, u32[]{:S(2)}, u32[]{:S(2)}) collective-permute-start(bf16[4,360,768]{2,1,0:T(8,128)(2,1)S(1)} %get-tuple-element.82.out0), channel_id=1, source_target_pairs={{0,4},{4,0},{1,5},{5,1},{2,6},{6,2},{3,7},{7,3},{8,12},{12,8},{9,1... | collective-permute-start | bytes 6635528 | tf_op jit(solution)/shard_map/ppermute | solution.py:243
  110.3 16.4 %collective-permute-start.14 = (bf16[384,768]{1,0:T(8,128)(2,1)S(1)}, bf16[384,768]{1,0:T(8,128)(2,1)S(1)}, u32[]{:S(2)}, u32[]{:S(2)}) collective-permute-start(bf16[384,768]{1,0:T(8,128)(2,1)S(1)} %collective-permute-done.12.x3), channel_id=1, source_target_pairs={{0,1},{1,2},{2,3},{3,0},{4,5},{5,6},{6,7},{7,4},{8,9},{9,10},{10,1... | collective-permute-start | bytes 1769480 | tf_op jit(solution)/shard_map/ppermute | solution.py:239
  110.3 16.4 %collective-permute-start.15 = (bf16[384,768]{1,0:T(8,128)(2,1)S(1)}, bf16[384,768]{1,0:T(8,128)(2,1)S(1)}, u32[]{:S(2)}, u32[]{:S(2)}) collective-permute-start(bf16[384,768]{1,0:T(8,128)(2,1)S(1)} %get-tuple-element.87.x0), channel_id=1, source_target_pairs={{0,3},{1,0},{2,1},{3,2},{4,7},{5,4},{6,5},{7,6},{8,11},{9,8},{10,9... | collective-permute-start | bytes 1769480 | tf_op jit(solution)/shard_map/ppermute | solution.py:239
  126.7 16.3 %collective-permute-start.21 = (bf16[384,768]{1,0:T(8,128)(2,1)S(1)}, bf16[384,768]{1,0:T(8,128)(2,1)S(1)}, u32[]{:S(2)}, u32[]{:S(2)}) collective-permute-start(bf16[384,768]{1,0:T(8,128)(2,1)S(1)} %get-tuple-element.87.x0), channel_id=1, source_target_pairs={{0,1},{1,2},{2,3},{3,0},{4,5},{5,6},{6,7},{7,4},{8,9},{9,10},{10,1... | collective-permute-start | bytes 1769480 | tf_op jit(solution)/shard_map/ppermute | solution.py:239
  129.1 16.9 %collective-permute-start.20 = (bf16[384,768]{1,0:T(8,128)(2,1)S(1)}, bf16[384,768]{1,0:T(8,128)(2,1)S(1)}, u32[]{:S(2)}, u32[]{:S(2)}) collective-permute-start(bf16[384,768]{1,0:T(8,128)(2,1)S(1)} %collective-permute-done.15.x1), channel_id=1, source_target_pairs={{0,3},{1,0},{2,1},{3,2},{4,7},{5,4},{6,5},{7,6},{8,11},{9,8},{10,9... | collective-permute-start | bytes 1769480 | tf_op jit(solution)/shard_map/ppermute | solution.py:239
  138.5 16.4 %collective-permute-start.18 = (bf16[384,768]{1,0:T(8,128)(2,1)S(1)}, bf16[384,768]{1,0:T(8,128)(2,1)S(1)}, u32[]{:S(2)}, u32[]{:S(2)}) collective-permute-start(bf16[384,768]{1,0:T(8,128)(2,1)S(1)} %get-tuple-element.85), channel_id=1, source_target_pairs={{0,1},{1,2},{2,3},{3,0},{4,5},{5,6},{6,7},{7,4},{8,9},{9,10},{10,1... | collective-permute-start | bytes 1769480 | tf_op jit(solution)/shard_map/ppermute | solution.py:239
  141.2 15.5 %collective-permute-start.19 = (bf16[384,768]{1,0:T(8,128)(2,1)S(1)}, bf16[384,768]{1,0:T(8,128)(2,1)S(1)}, u32[]{:S(2)}, u32[]{:S(2)}) collective-permute-start(bf16[384,768]{1,0:T(8,128)(2,1)S(1)} %get-tuple-element.86), channel_id=1, source_target_pairs={{0,3},{1,0},{2,1},{3,2},{4,7},{5,4},{6,5},{7,6},{8,11},{9,8},{10,9... | collective-permute-start | bytes 1769480 | tf_op jit(solution)/shard_map/ppermute | solution.py:239
  156.9 13.5 %collective-permute-start.22 = (bf16[384,768]{1,0:T(8,128)(2,1)S(1)}, bf16[384,768]{1,0:T(8,128)(2,1)S(1)}, u32[]{:S(2)}, u32[]{:S(2)}) collective-permute-start(bf16[384,768]{1,0:T(8,128)(2,1)S(1)} %add_convert_fusion.3), channel_id=1, source_target_pairs={{0,1},{1,2},{2,3},{3,0},{4,5},{5,6},{6,7},{7,4},{8,9},{9,10},{10,1... | collective-permute-start | bytes 1769480 | tf_op jit(solution)/shard_map/ppermute | solution.py:239
  158.7 13.3 %collective-permute-start.23 = (bf16[384,768]{1,0:T(8,128)(2,1)S(1)}, bf16[384,768]{1,0:T(8,128)(2,1)S(1)}, u32[]{:S(2)}, u32[]{:S(2)}) collective-permute-start(bf16[384,768]{1,0:T(8,128)(2,1)S(1)} %get-tuple-element.94), channel_id=1, source_target_pairs={{0,3},{1,0},{2,1},{3,2},{4,7},{5,4},{6,5},{7,6},{8,11},{9,8},{10,9... | collective-permute-start | bytes 1769480 | tf_op jit(solution)/shard_map/ppermute | solution.py:239
  172.1 12.4 %collective-permute-start.25 = (bf16[384,768]{1,0:T(8,128)(2,1)S(1)}, bf16[384,768]{1,0:T(8,128)(2,1)S(1)}, u32[]{:S(2)}, u32[]{:S(2)}) collective-permute-start(bf16[384,768]{1,0:T(8,128)(2,1)S(1)} %add_convert_fusion.1), channel_id=1, source_target_pairs={{0,3},{1,0},{2,1},{3,2},{4,7},{5,4},{6,5},{7,6},{8,11},{9,8},{10,9... | collective-permute-start | bytes 1769480 | tf_op jit(solution)/shard_map/ppermute | solution.py:239
  173.3 13.4 %collective-permute-start.24 = (bf16[384,768]{1,0:T(8,128)(2,1)S(1)}, bf16[384,768]{1,0:T(8,128)(2,1)S(1)}, u32[]{:S(2)}, u32[]{:S(2)}) collective-permute-start(bf16[384,768]{1,0:T(8,128)(2,1)S(1)} %get-tuple-element.101), channel_id=1, source_target_pairs={{0,1},{1,2},{2,3},{3,0},{4,5},{5,6},{6,7},{7,4},{8,9},{9,10},{10,1... | collective-permute-start | bytes 1769480 | tf_op jit(solution)/shard_map/ppermute | solution.py:239
  221.9 6.8 %collective-permute-start.27 = (bf16[32,768]{1,0:T(8,128)(2,1)S(1)}, bf16[32,768]{1,0:T(8,128)(2,1)S(1)}, u32[]{:S(2)}, u32[]{:S(2)}) collective-permute-start(bf16[32,768]{1,0:T(8,128)(2,1)S(1)} %get-tuple-element.109), channel_id=1, source_target_pairs={{0,2},{1,3},{2,0},{3,1},{4,6},{5,7},{6,4},{7,5},{8,10},{9,11},{10,... | collective-permute-start | bytes 147464 | tf_op jit(solution)/shard_map/ppermute | solution.py:239
  (20 other events, 238.4 us)

commit v2 on v1

--- a/solution.py
+++ b/solution.py
@@ -40,8 +40,8 @@
         state = jnp.where(first, both[:HD], both[HD:]).astype(BF)
         both_ref[0, :, cols] = state[:half]
         both_ref[1, :, cols] = state[half:]
-    keep_ref[...] = both_ref[at_ref[1]]
-    send_ref[...] = both_ref[1 - at_ref[1]]
+    keep_ref[...] = both_ref[at_ref[0]]
+    send_ref[...] = both_ref[1 - at_ref[0]]
 
 
 def flag(condition):
@@ -49,14 +49,14 @@
 
 
 def triple_body(at_ref, slab_ref, near_ref, next_ref, o_ref):
-    z = at_ref[2]
+    z = at_ref[0]
     total = slab_ref[...].astype(F32) + flag(z >= 1) * near_ref[...].astype(F32)
     o_ref[...] = (total + flag(z >= 2) * next_ref[...].astype(F32)).astype(BF)
 
 
-def before_body(at_ref, keep_ref, taken_ref, *rest):
+def before_body(core_ref, z_ref, x_ref, keep_ref, taken_ref, *rest):
     mine_ref, theirs_ref = rest[-2:]
-    z, x, later = at_ref[2], at_ref[3], flag(at_ref[1] == 1)
+    z, x, later = z_ref[0], x_ref[0], flag(core_ref[0] == 1)
     weights = [flag(z >= j) for j in (1, 2, 3, 6)] + [flag(x > j) for j in range(3)]
     base = jnp.zeros(keep_ref.shape, F32)
     for weight, ref in zip(weights, rest[:-2]):
@@ -84,13 +84,13 @@
 
 
 def attend_body(
-    at_ref, q_ref, inner_ref, mine_ref, other_ref, gain_ref, w_ref, o0, o1, o2, o3, normed, state
+    at_ref, core_ref, q_ref, inner_ref, mine_ref, other_ref, gain_ref, w_ref, o0, o1, o2, o3, normed, state
 ):
     tokens = q_ref.shape[0]
     first = lax.broadcasted_iota(jnp.int32, (tokens, PAIR), 1) < HD
     first_s = lax.broadcasted_iota(jnp.int32, (HD, PAIR), 1) < HD
-    state[at_ref[1]] = mine_ref[...]
-    state[1 - at_ref[1]] = other_ref[...]
+    state[core_ref[0]] = mine_ref[...]
+    state[1 - core_ref[0]] = other_ref[...]
 
     def halves_mean(x):
         a = jnp.sum(jnp.where(first, x, 0.0), axis=1, keepdims=True)
@@ -270,8 +270,10 @@
     padded = quarter + SPARE
     chip = ("z", "x")
     chips = lax.axis_size("z") * lax.axis_size("x")
-    at = jnp.stack([lax.axis_index(name) for name in ("heads", "core", "z", "x")])
-    at, key_rows = lax.optimization_barrier((at.astype(jnp.int32), key_rows))
+    ids = tuple(
+        jnp.full((1,), lax.axis_index(name).astype(jnp.int32)) for name in ("heads", "core", "z", "x")
+    )
+    (h_at, core_at, z_at, x_at), key_rows = lax.optimization_barrier((ids, key_rows))
     capacity = min(tokens, 3 * tokens * expert_ids.shape[1] // (2 * chips))
     rows = chips * capacity
     shape = jax.ShapeDtypeStruct
@@ -282,16 +284,16 @@
         in_specs=[SMEM_SPEC] + [VMEM_SPEC] * 2,
         out_specs=(VMEM_SPEC,) * 2,
         scratch_shapes=[pltpu.VMEM((2, HD // 2, width), BF)],
-        compiler_params=params(60),
+        compiler_params=params(28),
         name="own_state",
-    )(at, key_rows, value_rows)
+    )(core_at, key_rows, value_rows)
     taken = swap(send)
     inner = pl.pallas_call(
         inner_body,
         out_shape=shape((tokens, width), F32),
         in_specs=[VMEM_SPEC] * 3,
         out_specs=VMEM_SPEC,
-        compiler_params=params(28),
+        compiler_params=params(60),
         cost_estimate=cost(2e9, 2e6),
         name="inner",
     )(query_rows, key_rows, value_rows)
@@ -315,15 +317,15 @@
         out_specs=VMEM_SPEC,
         compiler_params=params(28),
         name="triple",
-    )(at, slab_state, *near)
+    )(z_at, slab_state, *near)
     mine, theirs = pl.pallas_call(
         before_body,
         out_shape=(shape(keep.shape, BF),) * 2,
-        in_specs=[SMEM_SPEC] + [VMEM_SPEC] * 9,
+        in_specs=[SMEM_SPEC] * 3 + [VMEM_SPEC] * 9,
         out_specs=(VMEM_SPEC,) * 2,
         compiler_params=params(28),
         name="before",
-    )(at, keep, taken, *near, deeper(triple, 3), deeper(triple, 6), *beside)
+    )(core_at, z_at, x_at, keep, taken, *near, deeper(triple, 3), deeper(triple, 6), *beside)
     other = swap(theirs)
 
     place, mix_high, mix_low = pl.pallas_call(
@@ -339,13 +341,14 @@
     parts = pl.pallas_call(
         attend_body,
         out_shape=(shape((tokens, padded), BF),) * 4,
-        in_specs=[SMEM_SPEC] + [VMEM_SPEC] * 6,
+        in_specs=[SMEM_SPEC] * 2 + [VMEM_SPEC] * 6,
         out_specs=(VMEM_SPEC,) * 4,
         scratch_shapes=[pltpu.VMEM((tokens, width), BF), pltpu.VMEM((2, HD // 2, width), BF)],
         compiler_params=params(28),
         name="attend",
-    )(at, query_rows, inner, mine, other, norm_gain.reshape(1, width), out_weight.T)
-    pieces = [parts[0]] + [shift(parts[j], j) for j in (1, 2, 3)]
+    )(h_at, core_at, query_rows, inner, mine, other, norm_gain.reshape(1, width), out_weight.T)
+    across = shift(parts[2], 2)
+    pieces = [parts[0], shift(parts[1], 1), across, shift(parts[3], 3)]
 
     packed, attended = pl.pallas_call(
         pack_body,
@@ -355,13 +358,13 @@
         scratch_shapes=[pltpu.VMEM((tokens, padded), BF), pltpu.VMEM((4, 1, quarter), F32)],
         compiler_params=params(28),
         name="pack",
-    )(at, *pieces, residual.T, moe_gain.reshape(1, features), place)
+    )(h_at, *pieces, residual.T, moe_gain.reshape(1, features), place)
 
     arrived = lax.all_to_all(
         packed.reshape(chips, capacity, padded), chip, 0, 0, tiled=True
     ).reshape(rows, padded)
     half = rows // 2
-    arrived, late_h = lax.optimization_barrier((arrived, at))
+    arrived, late_h = lax.optimization_barrier((arrived, h_at))
     low, high = arrived[:half], arrived[half:]
 
     minus_low, plus_low = shift(low, 1), shift(low, -1)
@@ -422,8 +425,9 @@
         scratch_shapes=[pltpu.VMEM((tokens, padded), BF)],
         compiler_params=params(28),
         name="mix",
-    )(at, returned, mix_high, mix_low, attended)
-    finals = [ends[0]] + [shift(ends[j], j) for j in (1, 2, 3)]
+    )(h_at, returned, mix_high, mix_low, attended)
+    across = shift(ends[2], 2)
+    finals = [ends[0], shift(ends[1], 1), across, shift(ends[3], 3)]
     return pl.pallas_call(
         join_body,
         out_shape=shape((share, features), BF),
@@ -432,7 +436,7 @@
         scratch_shapes=[pltpu.VMEM((4, share, padded), BF)],
         compiler_params=params(28),
         name="join",
-    )(at, *finals)
+    )(h_at, *finals)
 
 
 def solution(mesh):

time: 232 us -> 230 us (level)
  Pallas kernels: 33.4 us -> 29.8 us
  local copies, waits for them, and re-layouts: 2.96 us -> 5.49 us
    unnamed x30 -> x26, local copies, waits for them, and re-layouts: 2.87 us -> 5.4 us
  transfers between devices with their start and end apart: 29 -> 29, of which waited for: 23 -> 23; matrix products, arithmetic and copies ran while one was open for 0% -> 0% of each run, Pallas kernels for 10% -> 11%
where the time goes in v2:
time: 230 us
  waiting for transfers between devices  78.8 us (34%)
  blocking collectives  73 us (32%)
  starting transfers between devices  41.7 us (18%)
  Pallas kernels  29.8 us (13%)
  local copies, waits for them, and re-layouts  5.49 us (2%)
    ppermute x18, waiting for transfers between devices, shift(): return lax.ppermute(x, 'heads', [(i, (i + by) % 4) for i in range(4)])  66.5 us
    all_to_all x1, blocking collectives, on_device(): lax.all_to_all(packed.reshape(chips, capacity, padded), chip, 0, 0, tiled...  39.2 us
    all_to_all x1, blocking collectives, on_device(): lax.all_to_all(leaving, chip, 0, 0, tiled=True).reshape(rows, padded)  33.7 us
    ppermute x18, starting transfers between devices, shift(): return lax.ppermute(x, 'heads', [(i, (i + by) % 4) for i in range(4)])  25.7 us
    pallas_call x2, Pallas kernels, experts(): pl.pallas_call(functools.partial(expert_body, features), out_shape=(shape...  17.7 us
    ppermute x4, starting transfers between devices, deeper(): return lax.ppermute(x, 'z', [(i, (i + j) % depth) for i in range(depth)])  10.8 us
    unnamed x26, local copies, waits for them, and re-layouts  5.4 us
    ppermute x4, waiting for transfers between devices, deeper(): return lax.ppermute(x, 'z', [(i, (i + j) % depth) for i in range(depth)])  5.11 us
  transfers between devices with their start and end apart: 29, of which 23 were waited for; matrix products, arithmetic and copies ran while one was open for 0% of the time, Pallas kernels for 11%

profile of v2, /device:TPU:8, one launch (start us, length us, event | category | flops | bytes accessed | tf_op | source)
XLA Modules:
  0.0 229.8 jit_solution(8882183141336279633)
XLA Ops:
  3.5 2.8 %collective-permute-start.3 = (bf16[32,896]{1,0:T(8,128)(2,1)S(1)}, bf16[32,896]{1,0:T(8,128)(2,1)S(1)}, u32[]{:S(2)}, u32[]{:S(2)}) collective-permute-start(bf16[32,896]{1,0:T(8,128)(2,1)S(1)} %add_convert_fusion.5), channel_id=1, source_target_pairs={{0,24},{8,0},{16,8},{24,16},{1,25},{9,1},{17,9},{25,17},{2,26},{10... | collective-permute-start | bytes 172040 | tf_op jit(solution)/shard_map/ppermute | solution.py:303
  8.7 3.5 %collective-permute-done.2.rest_5_ = bf16[32,896]{1,0:T(8,128)(2,1)S(1)} collective-permute-done((bf16[32,896]{1,0:T(8,128)(2,1)S(1)}, bf16[32,896]{1,0:T(8,128)(2,1)S(1)}, u32[]{:S(2)}, u32[]{:S(2)}) %collective-permute-start.2) | collective-permute-done | bytes 57376 | tf_op jit(solution)/shard_map/ppermute | solution.py:303
  12.8 3.3 %collective-permute-start.5 = (bf16[32,896]{1,0:T(8,128)(2,1)S(1)}, bf16[32,896]{1,0:T(8,128)(2,1)S(1)}, u32[]{:S(2)}, u32[]{:S(2)}) collective-permute-start(bf16[32,896]{1,0:T(8,128)(2,1)S(1)} %add_convert_fusion.4.slab_ref), channel_id=1, source_target_pairs={{0,64},{32,96},{64,128},{96,160},{128,192},{160,224},{192,0},{224,... | collective-permute-start | bytes 172040 | tf_op jit(solution)/shard_map/ppermute | solution.py:309
  18.1 4.2 %inner.1.inner_ref = f32[128,896]{1,0:T(8,128)} custom-call(bf16[128,896]{1,0:T(8,128)(2,1)} %q_ref.3, bf16[128,896]{1,0:T(8,128)(2,1)} %k_ref.1, bf16[128,896]{1,0:T(8,128)(2,1)} %v_ref.3), custom_call_target="tpu_custom_call" | custom-call | flops 2000000000 | bytes 2000000 | tf_op jit(solution)/shard_map/inner/pallas_call | solution.py:291
  22.4 2.8 %collective-permute-start.7 = (bf16[32,896]{1,0:T(8,128)(2,1)S(1)}, bf16[32,896]{1,0:T(8,128)(2,1)S(1)}, u32[]{:S(2)}, u32[]{:S(2)}) collective-permute-start(bf16[32,896]{1,0:T(8,128)(2,1)S(1)} %triple.1), channel_id=1, source_target_pairs={{0,192},{32,224},{64,0},{96,32},{128,64},{160,96},{192,128},{224,1... | collective-permute-start | bytes 172040 | tf_op jit(solution)/shard_map/ppermute | solution.py:309
  25.2 2.7 %collective-permute-start.6 = (bf16[32,896]{1,0:T(8,128)(2,1)S(1)}, bf16[32,896]{1,0:T(8,128)(2,1)S(1)}, u32[]{:S(2)}, u32[]{:S(2)}) collective-permute-start(bf16[32,896]{1,0:T(8,128)(2,1)S(1)} %triple.1), channel_id=1, source_target_pairs={{0,96},{32,128},{64,160},{96,192},{128,224},{160,0},{192,32},{224,... | collective-permute-start | bytes 172040 | tf_op jit(solution)/shard_map/ppermute | solution.py:309
  28.3 4.7 %collective-permute-done.6.rest_2_ = bf16[32,896]{1,0:T(8,128)(2,1)S(1)} collective-permute-done((bf16[32,896]{1,0:T(8,128)(2,1)S(1)}, bf16[32,896]{1,0:T(8,128)(2,1)S(1)}, u32[]{:S(2)}, u32[]{:S(2)}) %collective-permute-start.6) | collective-permute-done | bytes 57376 | tf_op jit(solution)/shard_map/ppermute | solution.py:309
  34.4 2.5 %copy-done = bf16[896,2880]{0,1:T(8,128)(2,1)S(1)} copy-done((bf16[896,2880]{0,1:T(8,128)(2,1)S(1)}, bf16[896,2880]{0,1:T(8,128)(2,1)}, u32[]{:S(2)}) %copy-start) | copy-done | bytes 5160984
  45.5 2.5 %collective-permute-done.9.p1 = bf16[128,768]{1,0:T(8,128)(2,1)S(1)} collective-permute-done((bf16[128,768]{1,0:T(8,128)(2,1)S(1)}, bf16[128,768]{1,0:T(8,128)(2,1)S(1)}, u32[]{:S(2)}, u32[]{:S(2)}) %collective-permute-start.9) | collective-permute-done | bytes 196640 | tf_op jit(solution)/shard_map/ppermute | solution.py:239
  48.0 3.1 %collective-permute-done.10.p2 = bf16[128,768]{1,0:T(8,128)(2,1)S(1)} collective-permute-done((bf16[128,768]{1,0:T(8,128)(2,1)S(1)}, bf16[128,768]{1,0:T(8,128)(2,1)S(1)}, u32[]{:S(2)}, u32[]{:S(2)}) %collective-permute-start.10) | collective-permute-done | bytes 196640 | tf_op jit(solution)/shard_map/ppermute | solution.py:239
  51.1 2.4 %collective-permute-done.11.p3 = bf16[128,768]{1,0:T(8,128)(2,1)S(1)} collective-permute-done((bf16[128,768]{1,0:T(8,128)(2,1)S(1)}, bf16[128,768]{1,0:T(8,128)(2,1)S(1)}, u32[]{:S(2)}, u32[]{:S(2)}) %collective-permute-start.11) | collective-permute-done | bytes 196640 | tf_op jit(solution)/shard_map/ppermute | solution.py:239
  54.3 39.2 %all_to_all.10 = bf16[32,24,768]{2,1,0:T(8,128)(2,1)S(1)} all-to-all(bf16[32,24,768]{2,1,0:T(8,128)(2,1)S(1)} %bitcast.21), channel_id=1, replica_groups=mesh['z'=8,'x'=4,'core'=2,'heads'=4] {'z','x'}, dimensions={0} | all-to-all | bytes 2359296 | tf_op jit(solution)/shard_map/all_to_all | solution.py:363
  95.7 3.0 %weights.1 = (bf16[4,768,768]{2,1,0:T(8,128)(2,1)S(1)}, bf16[4,360,768]{2,1,0:T(8,128)(2,1)S(1)}) custom-call(s32[1]{0:T(128)} %bitcast.at_ref, bf16[360,2880]{1,0:T(8,128)(2,1)S(1)} %bitcast.23, bf16[360,2880]{1,0:T(8,128)(2,1)S(1)} %bitcast.24, bf16[360,2880]{1,0:T(8,128)(2,1)S(1)} %bitcast.25), custom_call_target="tpu_custom_call" | custom-call | flops 5000000000 | bytes 13000000 | tf_op jit(solution)/shard_map/weights/pallas_call | solution.py:373
  98.7 8.0 %collective-permute-done.13.x1 = bf16[384,768]{1,0:T(8,128)(2,1)S(1)} collective-permute-done((bf16[384,768]{1,0:T(8,128)(2,1)S(1)}, bf16[384,768]{1,0:T(8,128)(2,1)S(1)}, u32[]{:S(2)}, u32[]{:S(2)}) %collective-permute-start.13) | collective-permute-done | bytes 589856 | tf_op jit(solution)/shard_map/ppermute | solution.py:239
  109.1 3.0 %collective-permute-start.15 = (bf16[384,768]{1,0:T(8,128)(2,1)S(1)}, bf16[384,768]{1,0:T(8,128)(2,1)S(1)}, u32[]{:S(2)}, u32[]{:S(2)}) collective-permute-start(bf16[384,768]{1,0:T(8,128)(2,1)S(1)} %get-tuple-element.93.x0), channel_id=1, source_target_pairs={{0,3},{1,0},{2,1},{3,2},{4,7},{5,4},{6,5},{7,6},{8,11},{9,8},{10,9... | collective-permute-start | bytes 1769480 | tf_op jit(solution)/shard_map/ppermute | solution.py:239
  112.1 13.5 %collective-permute-done.14.x2 = bf16[384,768]{1,0:T(8,128)(2,1)S(1)} collective-permute-done((bf16[384,768]{1,0:T(8,128)(2,1)S(1)}, bf16[384,768]{1,0:T(8,128)(2,1)S(1)}, u32[]{:S(2)}, u32[]{:S(2)}) %collective-permute-start.14) | collective-permute-done | bytes 589856 | tf_op jit(solution)/shard_map/ppermute | solution.py:239
  128.5 8.8 %experts.2 = (bf16[384,768]{1,0:T(8,128)(2,1)S(1)}, bf16[384,768]{1,0:T(8,128)(2,1)S(1)}, bf16[384,768]{1,0:T(8,128)(2,1)S(1)}, bf16[384,768]{1,0:T(8,128)(2,1)S(1)}) custom-call(bf16[384,768]{1,0:T(8,128)(2,1)S(1)} %get-tuple-element.118.x0, bf16[384,768]{1,0:T(8,128)(2,1)S(1)} %collective-permute-done.13.x1, ...), custom_call_target="tpu_custom_call" | custom-call | flops 1000000 | bytes 100000 | tf_op jit(solution)/shard_map/experts/pallas_call | solution.py:388
  137.4 2.6 %collective-permute-start.18 = (bf16[384,768]{1,0:T(8,128)(2,1)S(1)}, bf16[384,768]{1,0:T(8,128)(2,1)S(1)}, u32[]{:S(2)}, u32[]{:S(2)}) collective-permute-start(bf16[384,768]{1,0:T(8,128)(2,1)S(1)} %get-tuple-element.91), channel_id=1, source_target_pairs={{0,1},{1,2},{2,3},{3,0},{4,5},{5,6},{6,7},{7,4},{8,9},{9,10},{10,1... | collective-permute-start | bytes 1769480 | tf_op jit(solution)/shard_map/ppermute | solution.py:239
  141.9 3.0 %collective-permute-done.20.x2 = bf16[384,768]{1,0:T(8,128)(2,1)S(1)} collective-permute-done((bf16[384,768]{1,0:T(8,128)(2,1)S(1)}, bf16[384,768]{1,0:T(8,128)(2,1)S(1)}, u32[]{:S(2)}, u32[]{:S(2)}) %collective-permute-start.20) | collective-permute-done | bytes 589856 | tf_op jit(solution)/shard_map/ppermute | solution.py:239
  144.9 8.8 %experts.3 = (bf16[384,768]{1,0:T(8,128)(2,1)S(1)}, bf16[384,768]{1,0:T(8,128)(2,1)S(1)}, bf16[384,768]{1,0:T(8,128)(2,1)S(1)}, bf16[384,768]{1,0:T(8,128)(2,1)S(1)}) custom-call(bf16[384,768]{1,0:T(8,128)(2,1)S(1)} %get-tuple-element.93.x0, bf16[384,768]{1,0:T(8,128)(2,1)S(1)} %collective-permute-done.15.x1, ...), custom_call_target="tpu_custom_call" | custom-call | flops 1000000 | bytes 100000 | tf_op jit(solution)/shard_map/experts/pallas_call | solution.py:388
  157.8 11.4 %collective-permute-done.22 = bf16[384,768]{1,0:T(8,128)(2,1)S(1)} collective-permute-done((bf16[384,768]{1,0:T(8,128)(2,1)S(1)}, bf16[384,768]{1,0:T(8,128)(2,1)S(1)}, u32[]{:S(2)}, u32[]{:S(2)}) %collective-permute-start.22) | collective-permute-done | bytes 589856 | tf_op jit(solution)/shard_map/ppermute | solution.py:239
  173.3 10.1 %collective-permute-done.25 = bf16[384,768]{1,0:T(8,128)(2,1)S(1)} collective-permute-done((bf16[384,768]{1,0:T(8,128)(2,1)S(1)}, bf16[384,768]{1,0:T(8,128)(2,1)S(1)}, u32[]{:S(2)}, u32[]{:S(2)}) %collective-permute-start.25) | collective-permute-done | bytes 589856 | tf_op jit(solution)/shard_map/ppermute | solution.py:239
  185.9 33.7 %all_to_all.11 = bf16[32,24,768]{2,1,0:T(8,128)(2,1)S(1)} all-to-all(bf16[32,24,768]{2,1,0:T(8,128)(2,1)S(1)} %bitcast.29), channel_id=1, replica_groups=mesh['z'=8,'x'=4,'core'=2,'heads'=4] {'z','x'}, dimensions={0} | all-to-all | bytes 2359296 | tf_op jit(solution)/shard_map/all_to_all | solution.py:417
  220.2 4.7 %collective-permute-start.27 = (bf16[32,768]{1,0:T(8,128)(2,1)S(1)}, bf16[32,768]{1,0:T(8,128)(2,1)S(1)}, u32[]{:S(2)}, u32[]{:S(2)}) collective-permute-start(bf16[32,768]{1,0:T(8,128)(2,1)S(1)} %get-tuple-element.115), channel_id=1, source_target_pairs={{0,2},{1,3},{2,0},{3,1},{4,6},{5,7},{6,4},{7,5},{8,10},{9,11},{10,... | collective-permute-start | bytes 147464 | tf_op jit(solution)/shard_map/ppermute | solution.py:239
  (84 shorter events, 45.1 us)
Async XLA Ops:
  6.3 5.8 %collective-permute-start.2 = (bf16[32,896]{1,0:T(8,128)(2,1)S(1)}, bf16[32,896]{1,0:T(8,128)(2,1)S(1)}, u32[]{:S(2)}, u32[]{:S(2)}) collective-permute-start(bf16[32,896]{1,0:T(8,128)(2,1)S(1)} %add_convert_fusion.5), channel_id=1, source_target_pairs={{0,16},{8,24},{16,0},{24,8},{1,17},{9,25},{17,1},{25,9},{2,18},{10... | collective-permute-start | bytes 172040 | tf_op jit(solution)/shard_map/ppermute | solution.py:303
  7.1 5.6 %collective-permute-start.1 = (bf16[32,896]{1,0:T(8,128)(2,1)S(1)}, bf16[32,896]{1,0:T(8,128)(2,1)S(1)}, u32[]{:S(2)}, u32[]{:S(2)}) collective-permute-start(bf16[32,896]{1,0:T(8,128)(2,1)S(1)} %add_convert_fusion.5), channel_id=1, source_target_pairs={{0,8},{8,16},{16,24},{24,0},{1,9},{9,17},{17,25},{25,1},{2,10},{10... | collective-permute-start | bytes 172040 | tf_op jit(solution)/shard_map/ppermute | solution.py:303
  12.8 9.5 %collective-permute-start.5 = (bf16[32,896]{1,0:T(8,128)(2,1)S(1)}, bf16[32,896]{1,0:T(8,128)(2,1)S(1)}, u32[]{:S(2)}, u32[]{:S(2)}) collective-permute-start(bf16[32,896]{1,0:T(8,128)(2,1)S(1)} %add_convert_fusion.4.slab_ref), channel_id=1, source_target_pairs={{0,64},{32,96},{64,128},{96,160},{128,192},{160,224},{192,0},{224,... | collective-permute-start | bytes 172040 | tf_op jit(solution)/shard_map/ppermute | solution.py:309
  16.2 6.1 %collective-permute-start.4 = (bf16[32,896]{1,0:T(8,128)(2,1)S(1)}, bf16[32,896]{1,0:T(8,128)(2,1)S(1)}, u32[]{:S(2)}, u32[]{:S(2)}) collective-permute-start(bf16[32,896]{1,0:T(8,128)(2,1)S(1)} %add_convert_fusion.4.slab_ref), channel_id=1, source_target_pairs={{0,32},{32,64},{64,96},{96,128},{128,160},{160,192},{192,224},{224... | collective-permute-start | bytes 172040 | tf_op jit(solution)/shard_map/ppermute | solution.py:309
  22.4 5.9 %collective-permute-start.7 = (bf16[32,896]{1,0:T(8,128)(2,1)S(1)}, bf16[32,896]{1,0:T(8,128)(2,1)S(1)}, u32[]{:S(2)}, u32[]{:S(2)}) collective-permute-start(bf16[32,896]{1,0:T(8,128)(2,1)S(1)} %triple.1), channel_id=1, source_target_pairs={{0,192},{32,224},{64,0},{96,32},{128,64},{160,96},{192,128},{224,1... | collective-permute-start | bytes 172040 | tf_op jit(solution)/shard_map/ppermute | solution.py:309
  25.2 7.8 %collective-permute-start.6 = (bf16[32,896]{1,0:T(8,128)(2,1)S(1)}, bf16[32,896]{1,0:T(8,128)(2,1)S(1)}, u32[]{:S(2)}, u32[]{:S(2)}) collective-permute-start(bf16[32,896]{1,0:T(8,128)(2,1)S(1)} %triple.1), channel_id=1, source_target_pairs={{0,96},{32,128},{64,160},{96,192},{128,224},{160,0},{192,32},{224,... | collective-permute-start | bytes 172040 | tf_op jit(solution)/shard_map/ppermute | solution.py:309
  40.2 7.8 %collective-permute-start.9 = (bf16[128,768]{1,0:T(8,128)(2,1)S(1)}, bf16[128,768]{1,0:T(8,128)(2,1)S(1)}, u32[]{:S(2)}, u32[]{:S(2)}) collective-permute-start(bf16[128,768]{1,0:T(8,128)(2,1)S(1)} %get-tuple-element.74), channel_id=1, source_target_pairs={{0,1},{1,2},{2,3},{3,0},{4,5},{5,6},{6,7},{7,4},{8,9},{9,10},{10,1... | collective-permute-start | bytes 589832 | tf_op jit(solution)/shard_map/ppermute | solution.py:239
  41.8 9.3 %collective-permute-start.10 = (bf16[128,768]{1,0:T(8,128)(2,1)S(1)}, bf16[128,768]{1,0:T(8,128)(2,1)S(1)}, u32[]{:S(2)}, u32[]{:S(2)}) collective-permute-start(bf16[128,768]{1,0:T(8,128)(2,1)S(1)} %get-tuple-element.75), channel_id=1, source_target_pairs={{0,2},{1,3},{2,0},{3,1},{4,6},{5,7},{6,4},{7,5},{8,10},{9,11},{10,... | collective-permute-start | bytes 589832 | tf_op jit(solution)/shard_map/ppermute | solution.py:239
  42.8 10.8 %collective-permute-start.11 = (bf16[128,768]{1,0:T(8,128)(2,1)S(1)}, bf16[128,768]{1,0:T(8,128)(2,1)S(1)}, u32[]{:S(2)}, u32[]{:S(2)}) collective-permute-start(bf16[128,768]{1,0:T(8,128)(2,1)S(1)} %get-tuple-element.76), channel_id=1, source_target_pairs={{0,3},{1,0},{2,1},{3,2},{4,7},{5,4},{6,5},{7,6},{8,11},{9,8},{10,9... | collective-permute-start | bytes 589832 | tf_op jit(solution)/shard_map/ppermute | solution.py:239
  93.6 13.0 %collective-permute-start.13 = (bf16[384,768]{1,0:T(8,128)(2,1)S(1)}, bf16[384,768]{1,0:T(8,128)(2,1)S(1)}, u32[]{:S(2)}, u32[]{:S(2)}) collective-permute-start(bf16[384,768]{1,0:T(8,128)(2,1)S(1)} %get-tuple-element.118.x0), channel_id=1, source_target_pairs={{0,3},{1,0},{2,1},{3,2},{4,7},{5,4},{6,5},{7,6},{8,11},{9,8},{10,9... | collective-permute-start | bytes 1769480 | tf_op jit(solution)/shard_map/ppermute | solution.py:239
  93.9 14.7 %collective-permute-start.12 = (bf16[384,768]{1,0:T(8,128)(2,1)S(1)}, bf16[384,768]{1,0:T(8,128)(2,1)S(1)}, u32[]{:S(2)}, u32[]{:S(2)}) collective-permute-start(bf16[384,768]{1,0:T(8,128)(2,1)S(1)} %get-tuple-element.118.x0), channel_id=1, source_target_pairs={{0,1},{1,2},{2,3},{3,0},{4,5},{5,6},{6,7},{7,4},{8,9},{9,10},{10,1... | collective-permute-start | bytes 1769480 | tf_op jit(solution)/shard_map/ppermute | solution.py:239
  108.6 19.9 %collective-permute-start.16 = (bf16[4,768,768]{2,1,0:T(8,128)(2,1)S(1)}, bf16[4,768,768]{2,1,0:T(8,128)(2,1)S(1)}, u32[]{:S(2)}, u32[]{:S(2)}) collective-permute-start(bf16[4,768,768]{2,1,0:T(8,128)(2,1)S(1)} %get-tuple-element.87.mid0), channel_id=1, source_target_pairs={{0,4},{4,0},{1,5},{5,1},{2,6},{6,2},{3,7},{7,3},{8,12},{12,8},{9,1... | collective-permute-start | bytes 14155784 | tf_op jit(solution)/shard_map/ppermute | solution.py:243
  108.6 19.9 %collective-permute-start.17 = (bf16[4,360,768]{2,1,0:T(8,128)(2,1)S(1)}, bf16[4,360,768]{2,1,0:T(8,128)(2,1)S(1)}, u32[]{:S(2)}, u32[]{:S(2)}) collective-permute-start(bf16[4,360,768]{2,1,0:T(8,128)(2,1)S(1)} %get-tuple-element.88.out0), channel_id=1, source_target_pairs={{0,4},{4,0},{1,5},{5,1},{2,6},{6,2},{3,7},{7,3},{8,12},{12,8},{9,1... | collective-permute-start | bytes 6635528 | tf_op jit(solution)/shard_map/ppermute | solution.py:243
  109.1 16.4 %collective-permute-start.14 = (bf16[384,768]{1,0:T(8,128)(2,1)S(1)}, bf16[384,768]{1,0:T(8,128)(2,1)S(1)}, u32[]{:S(2)}, u32[]{:S(2)}) collective-permute-start(bf16[384,768]{1,0:T(8,128)(2,1)S(1)} %collective-permute-done.12.x3), channel_id=1, source_target_pairs={{0,1},{1,2},{2,3},{3,0},{4,5},{5,6},{6,7},{7,4},{8,9},{9,10},{10,1... | collective-permute-start | bytes 1769480 | tf_op jit(solution)/shard_map/ppermute | solution.py:239
  109.1 16.4 %collective-permute-start.15 = (bf16[384,768]{1,0:T(8,128)(2,1)S(1)}, bf16[384,768]{1,0:T(8,128)(2,1)S(1)}, u32[]{:S(2)}, u32[]{:S(2)}) collective-permute-start(bf16[384,768]{1,0:T(8,128)(2,1)S(1)} %get-tuple-element.93.x0), channel_id=1, source_target_pairs={{0,3},{1,0},{2,1},{3,2},{4,7},{5,4},{6,5},{7,6},{8,11},{9,8},{10,9... | collective-permute-start | bytes 1769480 | tf_op jit(solution)/shard_map/ppermute | solution.py:239
  125.6 16.3 %collective-permute-start.21 = (bf16[384,768]{1,0:T(8,128)(2,1)S(1)}, bf16[384,768]{1,0:T(8,128)(2,1)S(1)}, u32[]{:S(2)}, u32[]{:S(2)}) collective-permute-start(bf16[384,768]{1,0:T(8,128)(2,1)S(1)} %get-tuple-element.93.x0), channel_id=1, source_target_pairs={{0,1},{1,2},{2,3},{3,0},{4,5},{5,6},{6,7},{7,4},{8,9},{9,10},{10,1... | collective-permute-start | bytes 1769480 | tf_op jit(solution)/shard_map/ppermute | solution.py:239
  127.9 16.9 %collective-permute-start.20 = (bf16[384,768]{1,0:T(8,128)(2,1)S(1)}, bf16[384,768]{1,0:T(8,128)(2,1)S(1)}, u32[]{:S(2)}, u32[]{:S(2)}) collective-permute-start(bf16[384,768]{1,0:T(8,128)(2,1)S(1)} %collective-permute-done.15.x1), channel_id=1, source_target_pairs={{0,3},{1,0},{2,1},{3,2},{4,7},{5,4},{6,5},{7,6},{8,11},{9,8},{10,9... | collective-permute-start | bytes 1769480 | tf_op jit(solution)/shard_map/ppermute | solution.py:239
  137.4 16.4 %collective-permute-start.18 = (bf16[384,768]{1,0:T(8,128)(2,1)S(1)}, bf16[384,768]{1,0:T(8,128)(2,1)S(1)}, u32[]{:S(2)}, u32[]{:S(2)}) collective-permute-start(bf16[384,768]{1,0:T(8,128)(2,1)S(1)} %get-tuple-element.91), channel_id=1, source_target_pairs={{0,1},{1,2},{2,3},{3,0},{4,5},{5,6},{6,7},{7,4},{8,9},{9,10},{10,1... | collective-permute-start | bytes 1769480 | tf_op jit(solution)/shard_map/ppermute | solution.py:239
  140.0 15.5 %collective-permute-start.19 = (bf16[384,768]{1,0:T(8,128)(2,1)S(1)}, bf16[384,768]{1,0:T(8,128)(2,1)S(1)}, u32[]{:S(2)}, u32[]{:S(2)}) collective-permute-start(bf16[384,768]{1,0:T(8,128)(2,1)S(1)} %get-tuple-element.92), channel_id=1, source_target_pairs={{0,3},{1,0},{2,1},{3,2},{4,7},{5,4},{6,5},{7,6},{8,11},{9,8},{10,9... | collective-permute-start | bytes 1769480 | tf_op jit(solution)/shard_map/ppermute | solution.py:239
  155.7 13.5 %collective-permute-start.22 = (bf16[384,768]{1,0:T(8,128)(2,1)S(1)}, bf16[384,768]{1,0:T(8,128)(2,1)S(1)}, u32[]{:S(2)}, u32[]{:S(2)}) collective-permute-start(bf16[384,768]{1,0:T(8,128)(2,1)S(1)} %add_convert_fusion.3), channel_id=1, source_target_pairs={{0,1},{1,2},{2,3},{3,0},{4,5},{5,6},{6,7},{7,4},{8,9},{9,10},{10,1... | collective-permute-start | bytes 1769480 | tf_op jit(solution)/shard_map/ppermute | solution.py:239
  157.5 13.3 %collective-permute-start.23 = (bf16[384,768]{1,0:T(8,128)(2,1)S(1)}, bf16[384,768]{1,0:T(8,128)(2,1)S(1)}, u32[]{:S(2)}, u32[]{:S(2)}) collective-permute-start(bf16[384,768]{1,0:T(8,128)(2,1)S(1)} %get-tuple-element.100), channel_id=1, source_target_pairs={{0,3},{1,0},{2,1},{3,2},{4,7},{5,4},{6,5},{7,6},{8,11},{9,8},{10,9... | collective-permute-start | bytes 1769480 | tf_op jit(solution)/shard_map/ppermute | solution.py:239
  170.9 12.4 %collective-permute-start.25 = (bf16[384,768]{1,0:T(8,128)(2,1)S(1)}, bf16[384,768]{1,0:T(8,128)(2,1)S(1)}, u32[]{:S(2)}, u32[]{:S(2)}) collective-permute-start(bf16[384,768]{1,0:T(8,128)(2,1)S(1)} %add_convert_fusion.1), channel_id=1, source_target_pairs={{0,3},{1,0},{2,1},{3,2},{4,7},{5,4},{6,5},{7,6},{8,11},{9,8},{10,9... | collective-permute-start | bytes 1769480 | tf_op jit(solution)/shard_map/ppermute | solution.py:239
  172.1 13.4 %collective-permute-start.24 = (bf16[384,768]{1,0:T(8,128)(2,1)S(1)}, bf16[384,768]{1,0:T(8,128)(2,1)S(1)}, u32[]{:S(2)}, u32[]{:S(2)}) collective-permute-start(bf16[384,768]{1,0:T(8,128)(2,1)S(1)} %get-tuple-element.107), channel_id=1, source_target_pairs={{0,1},{1,2},{2,3},{3,0},{4,5},{5,6},{6,7},{7,4},{8,9},{9,10},{10,1... | collective-permute-start | bytes 1769480 | tf_op jit(solution)/shard_map/ppermute | solution.py:239
  220.2 6.8 %collective-permute-start.27 = (bf16[32,768]{1,0:T(8,128)(2,1)S(1)}, bf16[32,768]{1,0:T(8,128)(2,1)S(1)}, u32[]{:S(2)}, u32[]{:S(2)}) collective-permute-start(bf16[32,768]{1,0:T(8,128)(2,1)S(1)} %get-tuple-element.115), channel_id=1, source_target_pairs={{0,2},{1,3},{2,0},{3,1},{4,6},{5,7},{6,4},{7,5},{8,10},{9,11},{10,... | collective-permute-start | bytes 147464 | tf_op jit(solution)/shard_map/ppermute | solution.py:239
  (18 other events, 187.4 us)

commit v3 on v2

--- a/solution.py
+++ b/solution.py
@@ -31,7 +31,9 @@
     return lax.dot_general(a, b, (dims, ((), ())), preferred_element_type=F32)
 
 
-def state_body(at_ref, k_ref, v_ref, keep_ref, send_ref, both_ref):
+def state_body(at_ref, k_ref, v_ref, keep_ref, send_ref, k_out, v_out, both_ref):
+    k_out[...] = k_ref[...]
+    v_out[...] = v_ref[...]
     first = lax.broadcasted_iota(jnp.int32, (HD, PAIR), 1) < HD
     half = HD // 2
     for p in range(k_ref.shape[1] // PAIR):
@@ -278,11 +280,11 @@
     rows = chips * capacity
     shape = jax.ShapeDtypeStruct
 
-    keep, send = pl.pallas_call(
+    keep, send, key_near, value_near = pl.pallas_call(
         state_body,
-        out_shape=(shape((HD // 2, width), BF),) * 2,
+        out_shape=(shape((HD // 2, width), BF),) * 2 + (shape((tokens, width), BF),) * 2,
         in_specs=[SMEM_SPEC] + [VMEM_SPEC] * 2,
-        out_specs=(VMEM_SPEC,) * 2,
+        out_specs=(VMEM_SPEC,) * 4,
         scratch_shapes=[pltpu.VMEM((2, HD // 2, width), BF)],
         compiler_params=params(28),
         name="own_state",
@@ -293,10 +295,10 @@
         out_shape=shape((tokens, width), F32),
         in_specs=[VMEM_SPEC] * 3,
         out_specs=VMEM_SPEC,
-        compiler_params=params(60),
+        compiler_params=params(28),
         cost_estimate=cost(2e9, 2e6),
         name="inner",
-    )(query_rows, key_rows, value_rows)
+    )(query_rows, key_near, value_near)
     chip_state = plus(keep, taken)
     depth, breadth = lax.axis_size("z"), lax.axis_size("x")
     beside = [
@@ -405,10 +407,9 @@
     sum_low = experts((low, plus_low, far_low, minus_low))
     via_low, got_low_plus = shift(sum_low[2], 1), shift(sum_low[3], -1)
     sum_high = experts((high, plus_high, far_high, minus_high))
-    via_low, got_low_plus, sum_high = lax.optimization_barrier((via_low, got_low_plus, sum_high))
+    via_low, got_low_plus = lax.optimization_barrier((via_low, got_low_plus))
     got_low_minus = shift(plus(sum_low[1], via_low), 1)
     via_high = shift(sum_high[2], -1)
-    got_low_minus, via_high, sum_high = lax.optimization_barrier((got_low_minus, via_high, sum_high))
     got_high_minus = shift(sum_high[1], 1)
     got_high_plus = shift(plus(sum_high[3], via_high), -1)
     total_low = plus(sum_low[0], got_low_minus, got_low_plus)

time: 230 us -> 222 us (0.965)
  waiting for transfers between devices: 78.8 us -> 72.5 us
  local copies, waits for them, and re-layouts: 5.49 us -> 2.95 us
    ppermute x18, waiting for transfers between devices: 66.5 us -> 61.7 us  [shift(): return lax.ppermute(x, 'heads', [(i, (i + by) % 4) for i in range(4)])]
    unnamed x26, local copies, waits for them, and re-layouts: 5.4 us -> 2.86 us
  transfers between devices with their start and end apart: 29 -> 29, of which waited for: 23 -> 21; matrix products, arithmetic and copies ran while one was open for 0% -> 0% of each run, Pallas kernels for 11% -> 10%
where the time goes in v3:
time: 222 us; the launch traced here: 221 us
  blocking collectives  74.8 us (34%)
  waiting for transfers between devices  72.5 us (33%)
  starting transfers between devices  42.1 us (19%)
  Pallas kernels  27.9 us (13%)
  local copies, waits for them, and re-layouts  2.95 us (1%)
    ppermute x18, waiting for transfers between devices, shift(): return lax.ppermute(x, 'heads', [(i, (i + by) % 4) for i in range(4)])  61.7 us
    all_to_all x1, blocking collectives, on_device(): lax.all_to_all(packed.reshape(chips, capacity, padded), chip, 0, 0, tiled...  41.1 us
    all_to_all x1, blocking collectives, on_device(): lax.all_to_all(leaving, chip, 0, 0, tiled=True).reshape(rows, padded)  33.8 us
    ppermute x18, starting transfers between devices, shift(): return lax.ppermute(x, 'heads', [(i, (i + by) % 4) for i in range(4)])  25.9 us
    pallas_call x2, Pallas kernels, experts(): pl.pallas_call(functools.partial(expert_body, features), out_shape=(shape...  17.7 us
    ppermute x4, starting transfers between devices, deeper(): return lax.ppermute(x, 'z', [(i, (i + j) % depth) for i in range(depth)])  9.76 us
    ppermute x3, starting transfers between devices, on_device(): lax.ppermute(chip_state, 'x', [(i, (i + j) % breadth) for i in range(brea...  5.73 us
    ppermute x4, waiting for transfers between devices, deeper(): return lax.ppermute(x, 'z', [(i, (i + j) % depth) for i in range(depth)])  5.59 us
  transfers between devices with their start and end apart: 29, of which 21 were waited for; matrix products, arithmetic and copies ran while one was open for 0% of the time, Pallas kernels for 10%

profile of v3, /device:TPU:8, one launch (start us, length us, event | category | flops | bytes accessed | tf_op | source)
XLA Modules:
  0.0 221.3 jit_solution(16383353224290396468)
XLA Ops:
  5.1 2.7 %collective-permute-start.2 = (bf16[32,896]{1,0:T(8,128)(2,1)S(1)}, bf16[32,896]{1,0:T(8,128)(2,1)S(1)}, u32[]{:S(2)}, u32[]{:S(2)}) collective-permute-start(bf16[32,896]{1,0:T(8,128)(2,1)S(1)} %add_convert_fusion.5), channel_id=1, source_target_pairs={{0,16},{8,24},{16,0},{24,8},{1,17},{9,25},{17,1},{25,9},{2,18},{10... | collective-permute-start | bytes 172040 | tf_op jit(solution)/shard_map/ppermute | solution.py:305
  14.0 3.3 %collective-permute-start.5 = (bf16[32,896]{1,0:T(8,128)(2,1)S(1)}, bf16[32,896]{1,0:T(8,128)(2,1)S(1)}, u32[]{:S(2)}, u32[]{:S(2)}) collective-permute-start(bf16[32,896]{1,0:T(8,128)(2,1)S(1)} %add_convert_fusion.4.slab_ref), channel_id=1, source_target_pairs={{0,64},{32,96},{64,128},{96,160},{128,192},{160,224},{192,0},{224,... | collective-permute-start | bytes 172040 | tf_op jit(solution)/shard_map/ppermute | solution.py:311
  18.2 2.2 %inner.1.inner_ref = f32[128,896]{1,0:T(8,128)S(1)} custom-call(bf16[128,896]{1,0:T(8,128)(2,1)S(1)} %copy-done.4, bf16[128,896]{1,0:T(8,128)(2,1)S(1)} %get-tuple-element.59.k_ref, bf16[128,896]{1,0:T(8,128)(2,1)S(1)} %get-tuple-element.60.v_ref), custom_call_target="tpu_custom_call" | custom-call | flops 2000000000 | bytes 2000000 | tf_op jit(solution)/shard_map/inner/pallas_call | solution.py:293
  20.5 2.3 %collective-permute-done.5.next_ref.rest_1_ = bf16[32,896]{1,0:T(8,128)(2,1)S(1)} collective-permute-done((bf16[32,896]{1,0:T(8,128)(2,1)S(1)}, bf16[32,896]{1,0:T(8,128)(2,1)S(1)}, u32[]{:S(2)}, u32[]{:S(2)}) %collective-permute-start.5) | collective-permute-done | bytes 57376 | tf_op jit(solution)/shard_map/ppermute | solution.py:311
  22.8 2.3 %collective-permute-start.6 = (bf16[32,896]{1,0:T(8,128)(2,1)S(1)}, bf16[32,896]{1,0:T(8,128)(2,1)S(1)}, u32[]{:S(2)}, u32[]{:S(2)}) collective-permute-start(bf16[32,896]{1,0:T(8,128)(2,1)S(1)} %triple.1), channel_id=1, source_target_pairs={{0,96},{32,128},{64,160},{96,192},{128,224},{160,0},{192,32},{224,... | collective-permute-start | bytes 172040 | tf_op jit(solution)/shard_map/ppermute | solution.py:311
  25.1 2.2 collective-permute-start.7
  27.3 2.9 %collective-permute-done.6.rest_2_ = bf16[32,896]{1,0:T(8,128)(2,1)S(1)} collective-permute-done((bf16[32,896]{1,0:T(8,128)(2,1)S(1)}, bf16[32,896]{1,0:T(8,128)(2,1)S(1)}, u32[]{:S(2)}, u32[]{:S(2)}) %collective-permute-start.6) | collective-permute-done | bytes 57376 | tf_op jit(solution)/shard_map/ppermute | solution.py:311
  32.1 2.2 %attend.1 = (bf16[128,768]{1,0:T(8,128)(2,1)S(1)}, bf16[128,768]{1,0:T(8,128)(2,1)S(1)}, bf16[128,768]{1,0:T(8,128)(2,1)S(1)}, bf16[128,768]{1,0:T(8,128)(2,1)S(1)}) custom-call(s32[1]{0:T(128)} %bitcast.at_ref, s32[1]{0:T(128)} %bitcast.1.at_ref.core_ref, bf16[128,896]{1,0:T(8,128)(2,1)S(1)} %copy-done.5, f32[128,896]{1,0:T(8,128)S(1)} %inner.1.inner_ref, ...), custom_call_target="tpu_custom_call" | custom-call | tf_op jit(solution)/shard_map/attend/pallas_call | solution.py:343
  34.3 2.4 %collective-permute-start.10 = (bf16[128,768]{1,0:T(8,128)(2,1)S(1)}, bf16[128,768]{1,0:T(8,128)(2,1)S(1)}, u32[]{:S(2)}, u32[]{:S(2)}) collective-permute-start(bf16[128,768]{1,0:T(8,128)(2,1)S(1)} %get-tuple-element.70), channel_id=1, source_target_pairs={{0,2},{1,3},{2,0},{3,1},{4,6},{5,7},{6,4},{7,5},{8,10},{9,11},{10,... | collective-permute-start | bytes 589832 | tf_op jit(solution)/shard_map/ppermute | solution.py:241
  39.1 4.6 %collective-permute-done.10.p2 = bf16[128,768]{1,0:T(8,128)(2,1)S(1)} collective-permute-done((bf16[128,768]{1,0:T(8,128)(2,1)S(1)}, bf16[128,768]{1,0:T(8,128)(2,1)S(1)}, u32[]{:S(2)}, u32[]{:S(2)}) %collective-permute-start.10) | collective-permute-done | bytes 196640 | tf_op jit(solution)/shard_map/ppermute | solution.py:241
  43.7 3.4 %collective-permute-done.11.p3 = bf16[128,768]{1,0:T(8,128)(2,1)S(1)} collective-permute-done((bf16[128,768]{1,0:T(8,128)(2,1)S(1)}, bf16[128,768]{1,0:T(8,128)(2,1)S(1)}, u32[]{:S(2)}, u32[]{:S(2)}) %collective-permute-start.11) | collective-permute-done | bytes 196640 | tf_op jit(solution)/shard_map/ppermute | solution.py:241
  48.0 41.1 %all_to_all.10 = bf16[32,24,768]{2,1,0:T(8,128)(2,1)S(1)} all-to-all(bf16[32,24,768]{2,1,0:T(8,128)(2,1)S(1)} %bitcast.21), channel_id=1, replica_groups=mesh['z'=8,'x'=4,'core'=2,'heads'=4] {'z','x'}, dimensions={0} | all-to-all | bytes 2359296 | tf_op jit(solution)/shard_map/all_to_all | solution.py:365
  91.3 3.0 %weights.1 = (bf16[4,768,768]{2,1,0:T(8,128)(2,1)S(1)}, bf16[4,360,768]{2,1,0:T(8,128)(2,1)S(1)}) custom-call(s32[1]{0:T(128)} %bitcast.at_ref, bf16[360,2880]{1,0:T(8,128)(2,1)S(1)} %bitcast.23, bf16[360,2880]{1,0:T(8,128)(2,1)S(1)} %bitcast.24, bf16[360,2880]{1,0:T(8,128)(2,1)S(1)} %bitcast.25), custom_call_target="tpu_custom_call" | custom-call | flops 5000000000 | bytes 13000000 | tf_op jit(solution)/shard_map/weights/pallas_call | solution.py:375
  94.3 7.9 %collective-permute-done.12.x3 = bf16[384,768]{1,0:T(8,128)(2,1)S(1)} collective-permute-done((bf16[384,768]{1,0:T(8,128)(2,1)S(1)}, bf16[384,768]{1,0:T(8,128)(2,1)S(1)}, u32[]{:S(2)}, u32[]{:S(2)}) %collective-permute-start.12) | collective-permute-done | bytes 589856 | tf_op jit(solution)/shard_map/ppermute | solution.py:241
  106.6 13.2 %collective-permute-done.14.x2 = bf16[384,768]{1,0:T(8,128)(2,1)S(1)} collective-permute-done((bf16[384,768]{1,0:T(8,128)(2,1)S(1)}, bf16[384,768]{1,0:T(8,128)(2,1)S(1)}, u32[]{:S(2)}, u32[]{:S(2)}) %collective-permute-start.14) | collective-permute-done | bytes 589856 | tf_op jit(solution)/shard_map/ppermute | solution.py:241
  122.9 8.8 %experts.2 = (bf16[384,768]{1,0:T(8,128)(2,1)S(1)}, bf16[384,768]{1,0:T(8,128)(2,1)S(1)}, bf16[384,768]{1,0:T(8,128)(2,1)S(1)}, bf16[384,768]{1,0:T(8,128)(2,1)S(1)}) custom-call(bf16[384,768]{1,0:T(8,128)(2,1)S(1)} %get-tuple-element.104.x0, bf16[384,768]{1,0:T(8,128)(2,1)S(1)} %collective-permute-done.13.x1, ...), custom_call_target="tpu_custom_call" | custom-call | flops 1000000 | bytes 100000 | tf_op jit(solution)/shard_map/experts/pallas_call | solution.py:390
  134.9 3.9 %collective-permute-done.22.x3 = bf16[384,768]{1,0:T(8,128)(2,1)S(1)} collective-permute-done((bf16[384,768]{1,0:T(8,128)(2,1)S(1)}, bf16[384,768]{1,0:T(8,128)(2,1)S(1)}, u32[]{:S(2)}, u32[]{:S(2)}) %collective-permute-start.22) | collective-permute-done | bytes 589856 | tf_op jit(solution)/shard_map/ppermute | solution.py:241
  138.8 8.8 %experts.3 = (bf16[384,768]{1,0:T(8,128)(2,1)S(1)}, bf16[384,768]{1,0:T(8,128)(2,1)S(1)}, bf16[384,768]{1,0:T(8,128)(2,1)S(1)}, bf16[384,768]{1,0:T(8,128)(2,1)S(1)}) custom-call(bf16[384,768]{1,0:T(8,128)(2,1)S(1)} %get-tuple-element.90.x0, bf16[384,768]{1,0:T(8,128)(2,1)S(1)} %collective-permute-done.15.x1, ...), custom_call_target="tpu_custom_call" | custom-call | flops 1000000 | bytes 100000 | tf_op jit(solution)/shard_map/experts/pallas_call | solution.py:390
  147.6 3.3 %collective-permute-start.24 = (bf16[384,768]{1,0:T(8,128)(2,1)S(1)}, bf16[384,768]{1,0:T(8,128)(2,1)S(1)}, u32[]{:S(2)}, u32[]{:S(2)}) collective-permute-start(bf16[384,768]{1,0:T(8,128)(2,1)S(1)} %get-tuple-element.95), channel_id=1, source_target_pairs={{0,3},{1,0},{2,1},{3,2},{4,7},{5,4},{6,5},{7,6},{8,11},{9,8},{10,9... | collective-permute-start | bytes 1769480 | tf_op jit(solution)/shard_map/ppermute | solution.py:241
  154.0 6.5 %collective-permute-done.24 = bf16[384,768]{1,0:T(8,128)(2,1)S(1)} collective-permute-done((bf16[384,768]{1,0:T(8,128)(2,1)S(1)}, bf16[384,768]{1,0:T(8,128)(2,1)S(1)}, u32[]{:S(2)}, u32[]{:S(2)}) %collective-permute-start.24) | collective-permute-done | bytes 589856 | tf_op jit(solution)/shard_map/ppermute | solution.py:241
  162.0 5.5 %collective-permute-done.20 = bf16[384,768]{1,0:T(8,128)(2,1)S(1)} collective-permute-done((bf16[384,768]{1,0:T(8,128)(2,1)S(1)}, bf16[384,768]{1,0:T(8,128)(2,1)S(1)}, u32[]{:S(2)}, u32[]{:S(2)}) %collective-permute-start.20) | collective-permute-done | bytes 589856 | tf_op jit(solution)/shard_map/ppermute | solution.py:241
  167.6 8.7 %collective-permute-done.23 = bf16[384,768]{1,0:T(8,128)(2,1)S(1)} collective-permute-done((bf16[384,768]{1,0:T(8,128)(2,1)S(1)}, bf16[384,768]{1,0:T(8,128)(2,1)S(1)}, u32[]{:S(2)}, u32[]{:S(2)}) %collective-permute-start.23) | collective-permute-done | bytes 589856 | tf_op jit(solution)/shard_map/ppermute | solution.py:241
  176.7 33.8 %all_to_all.11 = bf16[32,24,768]{2,1,0:T(8,128)(2,1)S(1)} all-to-all(bf16[32,24,768]{2,1,0:T(8,128)(2,1)S(1)} %bitcast.29), channel_id=1, replica_groups=mesh['z'=8,'x'=4,'core'=2,'heads'=4] {'z','x'}, dimensions={0} | all-to-all | bytes 2359296 | tf_op jit(solution)/shard_map/all_to_all | solution.py:418
  211.0 5.4 %collective-permute-start.27 = (bf16[32,768]{1,0:T(8,128)(2,1)S(1)}, bf16[32,768]{1,0:T(8,128)(2,1)S(1)}, u32[]{:S(2)}, u32[]{:S(2)}) collective-permute-start(bf16[32,768]{1,0:T(8,128)(2,1)S(1)} %get-tuple-element.101), channel_id=1, source_target_pairs={{0,2},{1,3},{2,0},{3,1},{4,6},{5,7},{6,4},{7,5},{8,10},{9,11},{10,... | collective-permute-start | bytes 147464 | tf_op jit(solution)/shard_map/ppermute | solution.py:241
  (84 shorter events, 40.7 us)
Async XLA Ops:
  3.5 5.7 %collective-permute-start.1 = (bf16[32,896]{1,0:T(8,128)(2,1)S(1)}, bf16[32,896]{1,0:T(8,128)(2,1)S(1)}, u32[]{:S(2)}, u32[]{:S(2)}) collective-permute-start(bf16[32,896]{1,0:T(8,128)(2,1)S(1)} %add_convert_fusion.5), channel_id=1, source_target_pairs={{0,8},{8,16},{16,24},{24,0},{1,9},{9,17},{17,25},{25,1},{2,10},{10... | collective-permute-start | bytes 172040 | tf_op jit(solution)/shard_map/ppermute | solution.py:305
  5.1 5.9 %collective-permute-start.2 = (bf16[32,896]{1,0:T(8,128)(2,1)S(1)}, bf16[32,896]{1,0:T(8,128)(2,1)S(1)}, u32[]{:S(2)}, u32[]{:S(2)}) collective-permute-start(bf16[32,896]{1,0:T(8,128)(2,1)S(1)} %add_convert_fusion.5), channel_id=1, source_target_pairs={{0,16},{8,24},{16,0},{24,8},{1,17},{9,25},{17,1},{25,9},{2,18},{10... | collective-permute-start | bytes 172040 | tf_op jit(solution)/shard_map/ppermute | solution.py:305
  12.0 8.5 %collective-permute-start.4 = (bf16[32,896]{1,0:T(8,128)(2,1)S(1)}, bf16[32,896]{1,0:T(8,128)(2,1)S(1)}, u32[]{:S(2)}, u32[]{:S(2)}) collective-permute-start(bf16[32,896]{1,0:T(8,128)(2,1)S(1)} %add_convert_fusion.4.slab_ref), channel_id=1, source_target_pairs={{0,32},{32,64},{64,96},{96,128},{128,160},{160,192},{192,224},{224... | collective-permute-start | bytes 172040 | tf_op jit(solution)/shard_map/ppermute | solution.py:311
  14.0 8.8 %collective-permute-start.5 = (bf16[32,896]{1,0:T(8,128)(2,1)S(1)}, bf16[32,896]{1,0:T(8,128)(2,1)S(1)}, u32[]{:S(2)}, u32[]{:S(2)}) collective-permute-start(bf16[32,896]{1,0:T(8,128)(2,1)S(1)} %add_convert_fusion.4.slab_ref), channel_id=1, source_target_pairs={{0,64},{32,96},{64,128},{96,160},{128,192},{160,224},{192,0},{224,... | collective-permute-start | bytes 172040 | tf_op jit(solution)/shard_map/ppermute | solution.py:311
  22.8 7.4 %collective-permute-start.6 = (bf16[32,896]{1,0:T(8,128)(2,1)S(1)}, bf16[32,896]{1,0:T(8,128)(2,1)S(1)}, u32[]{:S(2)}, u32[]{:S(2)}) collective-permute-start(bf16[32,896]{1,0:T(8,128)(2,1)S(1)} %triple.1), channel_id=1, source_target_pairs={{0,96},{32,128},{64,160},{96,192},{128,224},{160,0},{192,32},{224,... | collective-permute-start | bytes 172040 | tf_op jit(solution)/shard_map/ppermute | solution.py:311
  34.3 9.4 %collective-permute-start.10 = (bf16[128,768]{1,0:T(8,128)(2,1)S(1)}, bf16[128,768]{1,0:T(8,128)(2,1)S(1)}, u32[]{:S(2)}, u32[]{:S(2)}) collective-permute-start(bf16[128,768]{1,0:T(8,128)(2,1)S(1)} %get-tuple-element.70), channel_id=1, source_target_pairs={{0,2},{1,3},{2,0},{3,1},{4,6},{5,7},{6,4},{7,5},{8,10},{9,11},{10,... | collective-permute-start | bytes 589832 | tf_op jit(solution)/shard_map/ppermute | solution.py:241
  36.7 10.4 %collective-permute-start.11 = (bf16[128,768]{1,0:T(8,128)(2,1)S(1)}, bf16[128,768]{1,0:T(8,128)(2,1)S(1)}, u32[]{:S(2)}, u32[]{:S(2)}) collective-permute-start(bf16[128,768]{1,0:T(8,128)(2,1)S(1)} %get-tuple-element.71), channel_id=1, source_target_pairs={{0,3},{1,0},{2,1},{3,2},{4,7},{5,4},{6,5},{7,6},{8,11},{9,8},{10,9... | collective-permute-start | bytes 589832 | tf_op jit(solution)/shard_map/ppermute | solution.py:241
  38.0 9.2 %collective-permute-start.9 = (bf16[128,768]{1,0:T(8,128)(2,1)S(1)}, bf16[128,768]{1,0:T(8,128)(2,1)S(1)}, u32[]{:S(2)}, u32[]{:S(2)}) collective-permute-start(bf16[128,768]{1,0:T(8,128)(2,1)S(1)} %get-tuple-element.69), channel_id=1, source_target_pairs={{0,1},{1,2},{2,3},{3,0},{4,5},{5,6},{6,7},{7,4},{8,9},{9,10},{10,1... | collective-permute-start | bytes 589832 | tf_op jit(solution)/shard_map/ppermute | solution.py:241
  89.2 13.0 %collective-permute-start.12 = (bf16[384,768]{1,0:T(8,128)(2,1)S(1)}, bf16[384,768]{1,0:T(8,128)(2,1)S(1)}, u32[]{:S(2)}, u32[]{:S(2)}) collective-permute-start(bf16[384,768]{1,0:T(8,128)(2,1)S(1)} %get-tuple-element.104.x0), channel_id=1, source_target_pairs={{0,1},{1,2},{2,3},{3,0},{4,5},{5,6},{6,7},{7,4},{8,9},{9,10},{10,1... | collective-permute-start | bytes 1769480 | tf_op jit(solution)/shard_map/ppermute | solution.py:241
  90.8 13.3 %collective-permute-start.13 = (bf16[384,768]{1,0:T(8,128)(2,1)S(1)}, bf16[384,768]{1,0:T(8,128)(2,1)S(1)}, u32[]{:S(2)}, u32[]{:S(2)}) collective-permute-start(bf16[384,768]{1,0:T(8,128)(2,1)S(1)} %get-tuple-element.104.x0), channel_id=1, source_target_pairs={{0,3},{1,0},{2,1},{3,2},{4,7},{5,4},{6,5},{7,6},{8,11},{9,8},{10,9... | collective-permute-start | bytes 1769480 | tf_op jit(solution)/shard_map/ppermute | solution.py:241
  104.1 18.8 %collective-permute-start.16 = (bf16[4,768,768]{2,1,0:T(8,128)(2,1)S(1)}, bf16[4,768,768]{2,1,0:T(8,128)(2,1)S(1)}, u32[]{:S(2)}, u32[]{:S(2)}) collective-permute-start(bf16[4,768,768]{2,1,0:T(8,128)(2,1)S(1)} %get-tuple-element.82.mid0), channel_id=1, source_target_pairs={{0,4},{4,0},{1,5},{5,1},{2,6},{6,2},{3,7},{7,3},{8,12},{12,8},{9,1... | collective-permute-start | bytes 14155784 | tf_op jit(solution)/shard_map/ppermute | solution.py:245
  104.1 18.8 %collective-permute-start.17 = (bf16[4,360,768]{2,1,0:T(8,128)(2,1)S(1)}, bf16[4,360,768]{2,1,0:T(8,128)(2,1)S(1)}, u32[]{:S(2)}, u32[]{:S(2)}) collective-permute-start(bf16[4,360,768]{2,1,0:T(8,128)(2,1)S(1)} %get-tuple-element.83.out0), channel_id=1, source_target_pairs={{0,4},{4,0},{1,5},{5,1},{2,6},{6,2},{3,7},{7,3},{8,12},{12,8},{9,1... | collective-permute-start | bytes 6635528 | tf_op jit(solution)/shard_map/ppermute | solution.py:245
  104.6 15.2 %collective-permute-start.14 = (bf16[384,768]{1,0:T(8,128)(2,1)S(1)}, bf16[384,768]{1,0:T(8,128)(2,1)S(1)}, u32[]{:S(2)}, u32[]{:S(2)}) collective-permute-start(bf16[384,768]{1,0:T(8,128)(2,1)S(1)} %collective-permute-done.12.x3), channel_id=1, source_target_pairs={{0,1},{1,2},{2,3},{3,0},{4,5},{5,6},{6,7},{7,4},{8,9},{9,10},{10,1... | collective-permute-start | bytes 1769480 | tf_op jit(solution)/shard_map/ppermute | solution.py:241
  105.9 15.0 %collective-permute-start.15 = (bf16[384,768]{1,0:T(8,128)(2,1)S(1)}, bf16[384,768]{1,0:T(8,128)(2,1)S(1)}, u32[]{:S(2)}, u32[]{:S(2)}) collective-permute-start(bf16[384,768]{1,0:T(8,128)(2,1)S(1)} %get-tuple-element.90.x0), channel_id=1, source_target_pairs={{0,3},{1,0},{2,1},{3,2},{4,7},{5,4},{6,5},{7,6},{8,11},{9,8},{10,9... | collective-permute-start | bytes 1769480 | tf_op jit(solution)/shard_map/ppermute | solution.py:241
  120.9 14.1 %collective-permute-start.21 = (bf16[384,768]{1,0:T(8,128)(2,1)S(1)}, bf16[384,768]{1,0:T(8,128)(2,1)S(1)}, u32[]{:S(2)}, u32[]{:S(2)}) collective-permute-start(bf16[384,768]{1,0:T(8,128)(2,1)S(1)} %collective-permute-done.15.x1), channel_id=1, source_target_pairs={{0,3},{1,0},{2,1},{3,2},{4,7},{5,4},{6,5},{7,6},{8,11},{9,8},{10,9... | collective-permute-start | bytes 1769480 | tf_op jit(solution)/shard_map/ppermute | solution.py:241
  121.6 17.2 %collective-permute-start.22 = (bf16[384,768]{1,0:T(8,128)(2,1)S(1)}, bf16[384,768]{1,0:T(8,128)(2,1)S(1)}, u32[]{:S(2)}, u32[]{:S(2)}) collective-permute-start(bf16[384,768]{1,0:T(8,128)(2,1)S(1)} %get-tuple-element.90.x0), channel_id=1, source_target_pairs={{0,1},{1,2},{2,3},{3,0},{4,5},{5,6},{6,7},{7,4},{8,9},{9,10},{10,1... | collective-permute-start | bytes 1769480 | tf_op jit(solution)/shard_map/ppermute | solution.py:241
  131.7 19.2 %collective-permute-start.18 = (bf16[384,768]{1,0:T(8,128)(2,1)S(1)}, bf16[384,768]{1,0:T(8,128)(2,1)S(1)}, u32[]{:S(2)}, u32[]{:S(2)}) collective-permute-start(bf16[384,768]{1,0:T(8,128)(2,1)S(1)} %get-tuple-element.86), channel_id=1, source_target_pairs={{0,1},{1,2},{2,3},{3,0},{4,5},{5,6},{6,7},{7,4},{8,9},{9,10},{10,1... | collective-permute-start | bytes 1769480 | tf_op jit(solution)/shard_map/ppermute | solution.py:241
  133.6 17.3 %collective-permute-start.19 = (bf16[384,768]{1,0:T(8,128)(2,1)S(1)}, bf16[384,768]{1,0:T(8,128)(2,1)S(1)}, u32[]{:S(2)}, u32[]{:S(2)}) collective-permute-start(bf16[384,768]{1,0:T(8,128)(2,1)S(1)} %get-tuple-element.87), channel_id=1, source_target_pairs={{0,3},{1,0},{2,1},{3,2},{4,7},{5,4},{6,5},{7,6},{8,11},{9,8},{10,9... | collective-permute-start | bytes 1769480 | tf_op jit(solution)/shard_map/ppermute | solution.py:241
  147.6 12.9 %collective-permute-start.24 = (bf16[384,768]{1,0:T(8,128)(2,1)S(1)}, bf16[384,768]{1,0:T(8,128)(2,1)S(1)}, u32[]{:S(2)}, u32[]{:S(2)}) collective-permute-start(bf16[384,768]{1,0:T(8,128)(2,1)S(1)} %get-tuple-element.95), channel_id=1, source_target_pairs={{0,3},{1,0},{2,1},{3,2},{4,7},{5,4},{6,5},{7,6},{8,11},{9,8},{10,9... | collective-permute-start | bytes 1769480 | tf_op jit(solution)/shard_map/ppermute | solution.py:241
  151.1 16.3 %collective-permute-start.20 = (bf16[384,768]{1,0:T(8,128)(2,1)S(1)}, bf16[384,768]{1,0:T(8,128)(2,1)S(1)}, u32[]{:S(2)}, u32[]{:S(2)}) collective-permute-start(bf16[384,768]{1,0:T(8,128)(2,1)S(1)} %add_convert_fusion.3), channel_id=1, source_target_pairs={{0,1},{1,2},{2,3},{3,0},{4,5},{5,6},{6,7},{7,4},{8,9},{9,10},{10,1... | collective-permute-start | bytes 1769480 | tf_op jit(solution)/shard_map/ppermute | solution.py:241
  152.4 24.0 %collective-permute-start.23 = (bf16[384,768]{1,0:T(8,128)(2,1)S(1)}, bf16[384,768]{1,0:T(8,128)(2,1)S(1)}, u32[]{:S(2)}, u32[]{:S(2)}) collective-permute-start(bf16[384,768]{1,0:T(8,128)(2,1)S(1)} %get-tuple-element.93), channel_id=1, source_target_pairs={{0,1},{1,2},{2,3},{3,0},{4,5},{5,6},{6,7},{7,4},{8,9},{9,10},{10,1... | collective-permute-start | bytes 1769480 | tf_op jit(solution)/shard_map/ppermute | solution.py:241
  160.7 15.7 %collective-permute-start.25 = (bf16[384,768]{1,0:T(8,128)(2,1)S(1)}, bf16[384,768]{1,0:T(8,128)(2,1)S(1)}, u32[]{:S(2)}, u32[]{:S(2)}) collective-permute-start(bf16[384,768]{1,0:T(8,128)(2,1)S(1)} %add_convert_fusion.1), channel_id=1, source_target_pairs={{0,3},{1,0},{2,1},{3,2},{4,7},{5,4},{6,5},{7,6},{8,11},{9,8},{10,9... | collective-permute-start | bytes 1769480 | tf_op jit(solution)/shard_map/ppermute | solution.py:241
  210.9 5.5 %collective-permute-start.26 = (bf16[32,768]{1,0:T(8,128)(2,1)S(1)}, bf16[32,768]{1,0:T(8,128)(2,1)S(1)}, u32[]{:S(2)}, u32[]{:S(2)}) collective-permute-start(bf16[32,768]{1,0:T(8,128)(2,1)S(1)} %get-tuple-element.100), channel_id=1, source_target_pairs={{0,1},{1,2},{2,3},{3,0},{4,5},{5,6},{6,7},{7,4},{8,9},{9,10},{10,1... | collective-permute-start | bytes 147464 | tf_op jit(solution)/shard_map/ppermute | solution.py:241
  211.0 7.5 %collective-permute-start.27 = (bf16[32,768]{1,0:T(8,128)(2,1)S(1)}, bf16[32,768]{1,0:T(8,128)(2,1)S(1)}, u32[]{:S(2)}, u32[]{:S(2)}) collective-permute-start(bf16[32,768]{1,0:T(8,128)(2,1)S(1)} %get-tuple-element.101), channel_id=1, source_target_pairs={{0,2},{1,3},{2,0},{3,1},{4,6},{5,7},{6,4},{7,5},{8,10},{9,11},{10,... | collective-permute-start | bytes 147464 | tf_op jit(solution)/shard_map/ppermute | solution.py:241
  (18 other events, 184.3 us)

commit v4 on v3

--- a/solution.py
+++ b/solution.py
@@ -402,7 +402,7 @@
         )(*group, *weights, *other_weights)
 
     far_low, plus_high = shift(minus_low, 1), shift(high, -1)
-    far_low, plus_high, high = lax.optimization_barrier((far_low, plus_high, high))
+    far_low, high = lax.optimization_barrier((far_low, high))
     far_high, minus_high = shift(plus_high, -1), shift(high, 1)
     sum_low = experts((low, plus_low, far_low, minus_low))
     via_low, got_low_plus = shift(sum_low[2], 1), shift(sum_low[3], -1)

time: 222 us -> 221 us (level)
  waiting for transfers between devices: 72.5 us -> 68.6 us
    ppermute x18, waiting for transfers between devices: 61.7 us -> 57.8 us  [shift(): return lax.ppermute(x, 'heads', [(i, (i + by) % 4) for i in range(4)])]
  transfers between devices with their start and end apart: 29 -> 29, of which waited for: 21 -> 21; matrix products, arithmetic and copies ran while one was open for 0% -> 0% of each run, Pallas kernels for 10% -> 11%
where the time goes in v4:
time: 221 us; the launch traced here: 220 us
  blocking collectives  75.8 us (34%)
  waiting for transfers between devices  68.6 us (31%)
  starting transfers between devices  43.9 us (20%)
  Pallas kernels  27.9 us (13%)
  local copies, waits for them, and re-layouts  2.95 us (1%)
    ppermute x18, waiting for transfers between devices, shift(): return lax.ppermute(x, 'heads', [(i, (i + by) % 4) for i in range(4)])  57.8 us
    all_to_all x1, blocking collectives, on_device(): lax.all_to_all(packed.reshape(chips, capacity, padded), chip, 0, 0, tiled...  41.1 us
    all_to_all x1, blocking collectives, on_device(): lax.all_to_all(leaving, chip, 0, 0, tiled=True).reshape(rows, padded)  34.7 us
    ppermute x18, starting transfers between devices, shift(): return lax.ppermute(x, 'heads', [(i, (i + by) % 4) for i in range(4)])  27.7 us
    pallas_call x2, Pallas kernels, experts(): pl.pallas_call(functools.partial(expert_body, features), out_shape=(shape...  17.7 us
    ppermute x4, starting transfers between devices, deeper(): return lax.ppermute(x, 'z', [(i, (i + j) % depth) for i in range(depth)])  9.76 us
    ppermute x3, starting transfers between devices, on_device(): lax.ppermute(chip_state, 'x', [(i, (i + j) % breadth) for i in range(brea...  5.73 us
    ppermute x4, waiting for transfers between devices, deeper(): return lax.ppermute(x, 'z', [(i, (i + j) % depth) for i in range(depth)])  5.59 us
  transfers between devices with their start and end apart: 29, of which 21 were waited for; matrix products, arithmetic and copies ran while one was open for 0% of the time, Pallas kernels for 11%

profile of v4, /device:TPU:8, one launch (start us, length us, event | category | flops | bytes accessed | tf_op | source)
XLA Modules:
  0.0 220.1 jit_solution(14457746623927974940)
XLA Ops:
  5.1 2.7 %collective-permute-start.2 = (bf16[32,896]{1,0:T(8,128)(2,1)S(1)}, bf16[32,896]{1,0:T(8,128)(2,1)S(1)}, u32[]{:S(2)}, u32[]{:S(2)}) collective-permute-start(bf16[32,896]{1,0:T(8,128)(2,1)S(1)} %add_convert_fusion.5), channel_id=1, source_target_pairs={{0,16},{8,24},{16,0},{24,8},{1,17},{9,25},{17,1},{25,9},{2,18},{10... | collective-permute-start | bytes 172040 | tf_op jit(solution)/shard_map/ppermute | solution.py:305
  14.0 3.3 %collective-permute-start.5 = (bf16[32,896]{1,0:T(8,128)(2,1)S(1)}, bf16[32,896]{1,0:T(8,128)(2,1)S(1)}, u32[]{:S(2)}, u32[]{:S(2)}) collective-permute-start(bf16[32,896]{1,0:T(8,128)(2,1)S(1)} %add_convert_fusion.4.slab_ref), channel_id=1, source_target_pairs={{0,64},{32,96},{64,128},{96,160},{128,192},{160,224},{192,0},{224,... | collective-permute-start | bytes 172040 | tf_op jit(solution)/shard_map/ppermute | solution.py:311
  18.2 2.2 %inner.1.inner_ref = f32[128,896]{1,0:T(8,128)S(1)} custom-call(bf16[128,896]{1,0:T(8,128)(2,1)S(1)} %copy-done.4, bf16[128,896]{1,0:T(8,128)(2,1)S(1)} %get-tuple-element.58.k_ref, bf16[128,896]{1,0:T(8,128)(2,1)S(1)} %get-tuple-element.59.v_ref), custom_call_target="tpu_custom_call" | custom-call | flops 2000000000 | bytes 2000000 | tf_op jit(solution)/shard_map/inner/pallas_call | solution.py:293
  20.5 2.3 %collective-permute-done.5.next_ref.rest_1_ = bf16[32,896]{1,0:T(8,128)(2,1)S(1)} collective-permute-done((bf16[32,896]{1,0:T(8,128)(2,1)S(1)}, bf16[32,896]{1,0:T(8,128)(2,1)S(1)}, u32[]{:S(2)}, u32[]{:S(2)}) %collective-permute-start.5) | collective-permute-done | bytes 57376 | tf_op jit(solution)/shard_map/ppermute | solution.py:311
  22.8 2.3 %collective-permute-start.6 = (bf16[32,896]{1,0:T(8,128)(2,1)S(1)}, bf16[32,896]{1,0:T(8,128)(2,1)S(1)}, u32[]{:S(2)}, u32[]{:S(2)}) collective-permute-start(bf16[32,896]{1,0:T(8,128)(2,1)S(1)} %triple.1), channel_id=1, source_target_pairs={{0,96},{32,128},{64,160},{96,192},{128,224},{160,0},{192,32},{224,... | collective-permute-start | bytes 172040 | tf_op jit(solution)/shard_map/ppermute | solution.py:311
  27.3 2.9 %collective-permute-done.6.rest_2_ = bf16[32,896]{1,0:T(8,128)(2,1)S(1)} collective-permute-done((bf16[32,896]{1,0:T(8,128)(2,1)S(1)}, bf16[32,896]{1,0:T(8,128)(2,1)S(1)}, u32[]{:S(2)}, u32[]{:S(2)}) %collective-permute-start.6) | collective-permute-done | bytes 57376 | tf_op jit(solution)/shard_map/ppermute | solution.py:311
  32.1 2.2 %attend.1 = (bf16[128,768]{1,0:T(8,128)(2,1)S(1)}, bf16[128,768]{1,0:T(8,128)(2,1)S(1)}, bf16[128,768]{1,0:T(8,128)(2,1)S(1)}, bf16[128,768]{1,0:T(8,128)(2,1)S(1)}) custom-call(s32[1]{0:T(128)} %bitcast.at_ref, s32[1]{0:T(128)} %bitcast.1.at_ref.core_ref, bf16[128,896]{1,0:T(8,128)(2,1)S(1)} %copy-done.5, f32[128,896]{1,0:T(8,128)S(1)} %inner.1.inner_ref, ...), custom_call_target="tpu_custom_call" | custom-call | tf_op jit(solution)/shard_map/attend/pallas_call | solution.py:343
  34.3 2.4 %collective-permute-start.10 = (bf16[128,768]{1,0:T(8,128)(2,1)S(1)}, bf16[128,768]{1,0:T(8,128)(2,1)S(1)}, u32[]{:S(2)}, u32[]{:S(2)}) collective-permute-start(bf16[128,768]{1,0:T(8,128)(2,1)S(1)} %get-tuple-element.69), channel_id=1, source_target_pairs={{0,2},{1,3},{2,0},{3,1},{4,6},{5,7},{6,4},{7,5},{8,10},{9,11},{10,... | collective-permute-start | bytes 589832 | tf_op jit(solution)/shard_map/ppermute | solution.py:241
  39.1 4.6 %collective-permute-done.10.p2 = bf16[128,768]{1,0:T(8,128)(2,1)S(1)} collective-permute-done((bf16[128,768]{1,0:T(8,128)(2,1)S(1)}, bf16[128,768]{1,0:T(8,128)(2,1)S(1)}, u32[]{:S(2)}, u32[]{:S(2)}) %collective-permute-start.10) | collective-permute-done | bytes 196640 | tf_op jit(solution)/shard_map/ppermute | solution.py:241
  43.7 3.4 %collective-permute-done.11.p3 = bf16[128,768]{1,0:T(8,128)(2,1)S(1)} collective-permute-done((bf16[128,768]{1,0:T(8,128)(2,1)S(1)}, bf16[128,768]{1,0:T(8,128)(2,1)S(1)}, u32[]{:S(2)}, u32[]{:S(2)}) %collective-permute-start.11) | collective-permute-done | bytes 196640 | tf_op jit(solution)/shard_map/ppermute | solution.py:241
  48.0 41.1 %all_to_all.10 = bf16[32,24,768]{2,1,0:T(8,128)(2,1)S(1)} all-to-all(bf16[32,24,768]{2,1,0:T(8,128)(2,1)S(1)} %bitcast.21), channel_id=1, replica_groups=mesh['z'=8,'x'=4,'core'=2,'heads'=4] {'z','x'}, dimensions={0} | all-to-all | bytes 2359296 | tf_op jit(solution)/shard_map/all_to_all | solution.py:365
  91.3 3.0 %weights.1 = (bf16[4,768,768]{2,1,0:T(8,128)(2,1)S(1)}, bf16[4,360,768]{2,1,0:T(8,128)(2,1)S(1)}) custom-call(s32[1]{0:T(128)} %bitcast.at_ref, bf16[360,2880]{1,0:T(8,128)(2,1)S(1)} %bitcast.23, bf16[360,2880]{1,0:T(8,128)(2,1)S(1)} %bitcast.24, bf16[360,2880]{1,0:T(8,128)(2,1)S(1)} %bitcast.25), custom_call_target="tpu_custom_call" | custom-call | flops 5000000000 | bytes 13000000 | tf_op jit(solution)/shard_map/weights/pallas_call | solution.py:375
  94.3 7.9 %collective-permute-done.12.x3 = bf16[384,768]{1,0:T(8,128)(2,1)S(1)} collective-permute-done((bf16[384,768]{1,0:T(8,128)(2,1)S(1)}, bf16[384,768]{1,0:T(8,128)(2,1)S(1)}, u32[]{:S(2)}, u32[]{:S(2)}) %collective-permute-start.12) | collective-permute-done | bytes 589856 | tf_op jit(solution)/shard_map/ppermute | solution.py:241
  106.6 13.2 %collective-permute-done.14.x2 = bf16[384,768]{1,0:T(8,128)(2,1)S(1)} collective-permute-done((bf16[384,768]{1,0:T(8,128)(2,1)S(1)}, bf16[384,768]{1,0:T(8,128)(2,1)S(1)}, u32[]{:S(2)}, u32[]{:S(2)}) %collective-permute-start.14) | collective-permute-done | bytes 589856 | tf_op jit(solution)/shard_map/ppermute | solution.py:241
  121.9 8.8 %experts.2 = (bf16[384,768]{1,0:T(8,128)(2,1)S(1)}, bf16[384,768]{1,0:T(8,128)(2,1)S(1)}, bf16[384,768]{1,0:T(8,128)(2,1)S(1)}, bf16[384,768]{1,0:T(8,128)(2,1)S(1)}) custom-call(bf16[384,768]{1,0:T(8,128)(2,1)S(1)} %get-tuple-element.102.x0, bf16[384,768]{1,0:T(8,128)(2,1)S(1)} %collective-permute-done.13.x1, ...), custom_call_target="tpu_custom_call" | custom-call | flops 1000000 | bytes 100000 | tf_op jit(solution)/shard_map/experts/pallas_call | solution.py:390
  137.2 8.8 %experts.3 = (bf16[384,768]{1,0:T(8,128)(2,1)S(1)}, bf16[384,768]{1,0:T(8,128)(2,1)S(1)}, bf16[384,768]{1,0:T(8,128)(2,1)S(1)}, bf16[384,768]{1,0:T(8,128)(2,1)S(1)}) custom-call(bf16[384,768]{1,0:T(8,128)(2,1)S(1)} %get-tuple-element.89.x0, bf16[384,768]{1,0:T(8,128)(2,1)S(1)} %collective-permute-done.20.x1, ...), custom_call_target="tpu_custom_call" | custom-call | flops 1000000 | bytes 100000 | tf_op jit(solution)/shard_map/experts/pallas_call | solution.py:390
  147.0 2.9 %collective-permute-done.18 = bf16[384,768]{1,0:T(8,128)(2,1)S(1)} collective-permute-done((bf16[384,768]{1,0:T(8,128)(2,1)S(1)}, bf16[384,768]{1,0:T(8,128)(2,1)S(1)}, u32[]{:S(2)}, u32[]{:S(2)}) %collective-permute-start.18) | collective-permute-done | bytes 589856 | tf_op jit(solution)/shard_map/ppermute | solution.py:241
  151.1 3.2 %collective-permute-start.23 = (bf16[384,768]{1,0:T(8,128)(2,1)S(1)}, bf16[384,768]{1,0:T(8,128)(2,1)S(1)}, u32[]{:S(2)}, u32[]{:S(2)}) collective-permute-start(bf16[384,768]{1,0:T(8,128)(2,1)S(1)} %get-tuple-element.91), channel_id=1, source_target_pairs={{0,1},{1,2},{2,3},{3,0},{4,5},{5,6},{6,7},{7,4},{8,9},{9,10},{10,1... | collective-permute-start | bytes 1769480 | tf_op jit(solution)/shard_map/ppermute | solution.py:241
  154.3 6.2 %collective-permute-done.24 = bf16[384,768]{1,0:T(8,128)(2,1)S(1)} collective-permute-done((bf16[384,768]{1,0:T(8,128)(2,1)S(1)}, bf16[384,768]{1,0:T(8,128)(2,1)S(1)}, u32[]{:S(2)}, u32[]{:S(2)}) %collective-permute-start.24) | collective-permute-done | bytes 589856 | tf_op jit(solution)/shard_map/ppermute | solution.py:241
  162.0 4.3 %collective-permute-done.19 = bf16[384,768]{1,0:T(8,128)(2,1)S(1)} collective-permute-done((bf16[384,768]{1,0:T(8,128)(2,1)S(1)}, bf16[384,768]{1,0:T(8,128)(2,1)S(1)}, u32[]{:S(2)}, u32[]{:S(2)}) %collective-permute-start.19) | collective-permute-done | bytes 589856 | tf_op jit(solution)/shard_map/ppermute | solution.py:241
  166.6 8.3 %collective-permute-done.23 = bf16[384,768]{1,0:T(8,128)(2,1)S(1)} collective-permute-done((bf16[384,768]{1,0:T(8,128)(2,1)S(1)}, bf16[384,768]{1,0:T(8,128)(2,1)S(1)}, u32[]{:S(2)}, u32[]{:S(2)}) %collective-permute-start.23) | collective-permute-done | bytes 589856 | tf_op jit(solution)/shard_map/ppermute | solution.py:241
  175.2 34.7 %all_to_all.11 = bf16[32,24,768]{2,1,0:T(8,128)(2,1)S(1)} all-to-all(bf16[32,24,768]{2,1,0:T(8,128)(2,1)S(1)} %bitcast.29), channel_id=1, replica_groups=mesh['z'=8,'x'=4,'core'=2,'heads'=4] {'z','x'}, dimensions={0} | all-to-all | bytes 2359296 | tf_op jit(solution)/shard_map/all_to_all | solution.py:418
  210.4 2.4 %collective-permute-start.26 = (bf16[32,768]{1,0:T(8,128)(2,1)S(1)}, bf16[32,768]{1,0:T(8,128)(2,1)S(1)}, u32[]{:S(2)}, u32[]{:S(2)}) collective-permute-start(bf16[32,768]{1,0:T(8,128)(2,1)S(1)} %get-tuple-element.98), channel_id=1, source_target_pairs={{0,1},{1,2},{2,3},{3,0},{4,5},{5,6},{6,7},{7,4},{8,9},{9,10},{10,1... | collective-permute-start | bytes 147464 | tf_op jit(solution)/shard_map/ppermute | solution.py:241
  215.0 2.5 %collective-permute-start.28 = (bf16[32,768]{1,0:T(8,128)(2,1)S(1)}, bf16[32,768]{1,0:T(8,128)(2,1)S(1)}, u32[]{:S(2)}, u32[]{:S(2)}) collective-permute-start(bf16[32,768]{1,0:T(8,128)(2,1)S(1)} %get-tuple-element.100), channel_id=1, source_target_pairs={{0,3},{1,0},{2,1},{3,2},{4,7},{5,4},{6,5},{7,6},{8,11},{9,8},{10,9... | collective-permute-start | bytes 147464 | tf_op jit(solution)/shard_map/ppermute | solution.py:241
  (84 shorter events, 44.1 us)
Async XLA Ops:
  3.5 5.7 %collective-permute-start.1 = (bf16[32,896]{1,0:T(8,128)(2,1)S(1)}, bf16[32,896]{1,0:T(8,128)(2,1)S(1)}, u32[]{:S(2)}, u32[]{:S(2)}) collective-permute-start(bf16[32,896]{1,0:T(8,128)(2,1)S(1)} %add_convert_fusion.5), channel_id=1, source_target_pairs={{0,8},{8,16},{16,24},{24,0},{1,9},{9,17},{17,25},{25,1},{2,10},{10... | collective-permute-start | bytes 172040 | tf_op jit(solution)/shard_map/ppermute | solution.py:305
  5.1 5.9 %collective-permute-start.2 = (bf16[32,896]{1,0:T(8,128)(2,1)S(1)}, bf16[32,896]{1,0:T(8,128)(2,1)S(1)}, u32[]{:S(2)}, u32[]{:S(2)}) collective-permute-start(bf16[32,896]{1,0:T(8,128)(2,1)S(1)} %add_convert_fusion.5), channel_id=1, source_target_pairs={{0,16},{8,24},{16,0},{24,8},{1,17},{9,25},{17,1},{25,9},{2,18},{10... | collective-permute-start | bytes 172040 | tf_op jit(solution)/shard_map/ppermute | solution.py:305
  12.0 8.5 %collective-permute-start.4 = (bf16[32,896]{1,0:T(8,128)(2,1)S(1)}, bf16[32,896]{1,0:T(8,128)(2,1)S(1)}, u32[]{:S(2)}, u32[]{:S(2)}) collective-permute-start(bf16[32,896]{1,0:T(8,128)(2,1)S(1)} %add_convert_fusion.4.slab_ref), channel_id=1, source_target_pairs={{0,32},{32,64},{64,96},{96,128},{128,160},{160,192},{192,224},{224... | collective-permute-start | bytes 172040 | tf_op jit(solution)/shard_map/ppermute | solution.py:311
  14.0 8.8 %collective-permute-start.5 = (bf16[32,896]{1,0:T(8,128)(2,1)S(1)}, bf16[32,896]{1,0:T(8,128)(2,1)S(1)}, u32[]{:S(2)}, u32[]{:S(2)}) collective-permute-start(bf16[32,896]{1,0:T(8,128)(2,1)S(1)} %add_convert_fusion.4.slab_ref), channel_id=1, source_target_pairs={{0,64},{32,96},{64,128},{96,160},{128,192},{160,224},{192,0},{224,... | collective-permute-start | bytes 172040 | tf_op jit(solution)/shard_map/ppermute | solution.py:311
  22.8 7.4 %collective-permute-start.6 = (bf16[32,896]{1,0:T(8,128)(2,1)S(1)}, bf16[32,896]{1,0:T(8,128)(2,1)S(1)}, u32[]{:S(2)}, u32[]{:S(2)}) collective-permute-start(bf16[32,896]{1,0:T(8,128)(2,1)S(1)} %triple.1), channel_id=1, source_target_pairs={{0,96},{32,128},{64,160},{96,192},{128,224},{160,0},{192,32},{224,... | collective-permute-start | bytes 172040 | tf_op jit(solution)/shard_map/ppermute | solution.py:311
  34.3 9.4 %collective-permute-start.10 = (bf16[128,768]{1,0:T(8,128)(2,1)S(1)}, bf16[128,768]{1,0:T(8,128)(2,1)S(1)}, u32[]{:S(2)}, u32[]{:S(2)}) collective-permute-start(bf16[128,768]{1,0:T(8,128)(2,1)S(1)} %get-tuple-element.69), channel_id=1, source_target_pairs={{0,2},{1,3},{2,0},{3,1},{4,6},{5,7},{6,4},{7,5},{8,10},{9,11},{10,... | collective-permute-start | bytes 589832 | tf_op jit(solution)/shard_map/ppermute | solution.py:241
  36.7 10.4 %collective-permute-start.11 = (bf16[128,768]{1,0:T(8,128)(2,1)S(1)}, bf16[128,768]{1,0:T(8,128)(2,1)S(1)}, u32[]{:S(2)}, u32[]{:S(2)}) collective-permute-start(bf16[128,768]{1,0:T(8,128)(2,1)S(1)} %get-tuple-element.70), channel_id=1, source_target_pairs={{0,3},{1,0},{2,1},{3,2},{4,7},{5,4},{6,5},{7,6},{8,11},{9,8},{10,9... | collective-permute-start | bytes 589832 | tf_op jit(solution)/shard_map/ppermute | solution.py:241
  38.0 9.2 %collective-permute-start.9 = (bf16[128,768]{1,0:T(8,128)(2,1)S(1)}, bf16[128,768]{1,0:T(8,128)(2,1)S(1)}, u32[]{:S(2)}, u32[]{:S(2)}) collective-permute-start(bf16[128,768]{1,0:T(8,128)(2,1)S(1)} %get-tuple-element.68), channel_id=1, source_target_pairs={{0,1},{1,2},{2,3},{3,0},{4,5},{5,6},{6,7},{7,4},{8,9},{9,10},{10,1... | collective-permute-start | bytes 589832 | tf_op jit(solution)/shard_map/ppermute | solution.py:241
  89.2 13.0 %collective-permute-start.12 = (bf16[384,768]{1,0:T(8,128)(2,1)S(1)}, bf16[384,768]{1,0:T(8,128)(2,1)S(1)}, u32[]{:S(2)}, u32[]{:S(2)}) collective-permute-start(bf16[384,768]{1,0:T(8,128)(2,1)S(1)} %get-tuple-element.102.x0), channel_id=1, source_target_pairs={{0,1},{1,2},{2,3},{3,0},{4,5},{5,6},{6,7},{7,4},{8,9},{9,10},{10,1... | collective-permute-start | bytes 1769480 | tf_op jit(solution)/shard_map/ppermute | solution.py:241
  90.8 13.3 %collective-permute-start.13 = (bf16[384,768]{1,0:T(8,128)(2,1)S(1)}, bf16[384,768]{1,0:T(8,128)(2,1)S(1)}, u32[]{:S(2)}, u32[]{:S(2)}) collective-permute-start(bf16[384,768]{1,0:T(8,128)(2,1)S(1)} %get-tuple-element.102.x0), channel_id=1, source_target_pairs={{0,3},{1,0},{2,1},{3,2},{4,7},{5,4},{6,5},{7,6},{8,11},{9,8},{10,9... | collective-permute-start | bytes 1769480 | tf_op jit(solution)/shard_map/ppermute | solution.py:241
  104.1 17.8 %collective-permute-start.15 = (bf16[4,768,768]{2,1,0:T(8,128)(2,1)S(1)}, bf16[4,768,768]{2,1,0:T(8,128)(2,1)S(1)}, u32[]{:S(2)}, u32[]{:S(2)}) collective-permute-start(bf16[4,768,768]{2,1,0:T(8,128)(2,1)S(1)} %get-tuple-element.81.mid0), channel_id=1, source_target_pairs={{0,4},{4,0},{1,5},{5,1},{2,6},{6,2},{3,7},{7,3},{8,12},{12,8},{9,1... | collective-permute-start | bytes 14155784 | tf_op jit(solution)/shard_map/ppermute | solution.py:245
  104.1 17.8 %collective-permute-start.16 = (bf16[4,360,768]{2,1,0:T(8,128)(2,1)S(1)}, bf16[4,360,768]{2,1,0:T(8,128)(2,1)S(1)}, u32[]{:S(2)}, u32[]{:S(2)}) collective-permute-start(bf16[4,360,768]{2,1,0:T(8,128)(2,1)S(1)} %get-tuple-element.82.out0), channel_id=1, source_target_pairs={{0,4},{4,0},{1,5},{5,1},{2,6},{6,2},{3,7},{7,3},{8,12},{12,8},{9,1... | collective-permute-start | bytes 6635528 | tf_op jit(solution)/shard_map/ppermute | solution.py:245
  104.6 15.2 %collective-permute-start.14 = (bf16[384,768]{1,0:T(8,128)(2,1)S(1)}, bf16[384,768]{1,0:T(8,128)(2,1)S(1)}, u32[]{:S(2)}, u32[]{:S(2)}) collective-permute-start(bf16[384,768]{1,0:T(8,128)(2,1)S(1)} %collective-permute-done.12.x3), channel_id=1, source_target_pairs={{0,1},{1,2},{2,3},{3,0},{4,5},{5,6},{6,7},{7,4},{8,9},{9,10},{10,1... | collective-permute-start | bytes 1769480 | tf_op jit(solution)/shard_map/ppermute | solution.py:241
  105.9 15.2 %collective-permute-start.20 = (bf16[384,768]{1,0:T(8,128)(2,1)S(1)}, bf16[384,768]{1,0:T(8,128)(2,1)S(1)}, u32[]{:S(2)}, u32[]{:S(2)}) collective-permute-start(bf16[384,768]{1,0:T(8,128)(2,1)S(1)} %get-tuple-element.89.x0), channel_id=1, source_target_pairs={{0,3},{1,0},{2,1},{3,2},{4,7},{5,4},{6,5},{7,6},{8,11},{9,8},{10,9... | collective-permute-start | bytes 1769480 | tf_op jit(solution)/shard_map/ppermute | solution.py:241
  119.9 15.2 %collective-permute-start.22 = (bf16[384,768]{1,0:T(8,128)(2,1)S(1)}, bf16[384,768]{1,0:T(8,128)(2,1)S(1)}, u32[]{:S(2)}, u32[]{:S(2)}) collective-permute-start(bf16[384,768]{1,0:T(8,128)(2,1)S(1)} %get-tuple-element.89.x0), channel_id=1, source_target_pairs={{0,1},{1,2},{2,3},{3,0},{4,5},{5,6},{6,7},{7,4},{8,9},{9,10},{10,1... | collective-permute-start | bytes 1769480 | tf_op jit(solution)/shard_map/ppermute | solution.py:241
  121.1 16.1 %collective-permute-start.21 = (bf16[384,768]{1,0:T(8,128)(2,1)S(1)}, bf16[384,768]{1,0:T(8,128)(2,1)S(1)}, u32[]{:S(2)}, u32[]{:S(2)}) collective-permute-start(bf16[384,768]{1,0:T(8,128)(2,1)S(1)} %collective-permute-done.20.x1), channel_id=1, source_target_pairs={{0,3},{1,0},{2,1},{3,2},{4,7},{5,4},{6,5},{7,6},{8,11},{9,8},{10,9... | collective-permute-start | bytes 1769480 | tf_op jit(solution)/shard_map/ppermute | solution.py:241
  130.7 16.2 %collective-permute-start.17 = (bf16[384,768]{1,0:T(8,128)(2,1)S(1)}, bf16[384,768]{1,0:T(8,128)(2,1)S(1)}, u32[]{:S(2)}, u32[]{:S(2)}) collective-permute-start(bf16[384,768]{1,0:T(8,128)(2,1)S(1)} %get-tuple-element.85), channel_id=1, source_target_pairs={{0,1},{1,2},{2,3},{3,0},{4,5},{5,6},{6,7},{7,4},{8,9},{9,10},{10,1... | collective-permute-start | bytes 1769480 | tf_op jit(solution)/shard_map/ppermute | solution.py:241
  132.3 17.5 %collective-permute-start.18 = (bf16[384,768]{1,0:T(8,128)(2,1)S(1)}, bf16[384,768]{1,0:T(8,128)(2,1)S(1)}, u32[]{:S(2)}, u32[]{:S(2)}) collective-permute-start(bf16[384,768]{1,0:T(8,128)(2,1)S(1)} %get-tuple-element.86), channel_id=1, source_target_pairs={{0,3},{1,0},{2,1},{3,2},{4,7},{5,4},{6,5},{7,6},{8,11},{9,8},{10,9... | collective-permute-start | bytes 1769480 | tf_op jit(solution)/shard_map/ppermute | solution.py:241
  146.0 14.5 %collective-permute-start.24 = (bf16[384,768]{1,0:T(8,128)(2,1)S(1)}, bf16[384,768]{1,0:T(8,128)(2,1)S(1)}, u32[]{:S(2)}, u32[]{:S(2)}) collective-permute-start(bf16[384,768]{1,0:T(8,128)(2,1)S(1)} %get-tuple-element.93), channel_id=1, source_target_pairs={{0,3},{1,0},{2,1},{3,2},{4,7},{5,4},{6,5},{7,6},{8,11},{9,8},{10,9... | collective-permute-start | bytes 1769480 | tf_op jit(solution)/shard_map/ppermute | solution.py:241
  150.0 16.3 %collective-permute-start.19 = (bf16[384,768]{1,0:T(8,128)(2,1)S(1)}, bf16[384,768]{1,0:T(8,128)(2,1)S(1)}, u32[]{:S(2)}, u32[]{:S(2)}) collective-permute-start(bf16[384,768]{1,0:T(8,128)(2,1)S(1)} %add_convert_fusion.3), channel_id=1, source_target_pairs={{0,1},{1,2},{2,3},{3,0},{4,5},{5,6},{6,7},{7,4},{8,9},{9,10},{10,1... | collective-permute-start | bytes 1769480 | tf_op jit(solution)/shard_map/ppermute | solution.py:241
  151.1 23.8 %collective-permute-start.23 = (bf16[384,768]{1,0:T(8,128)(2,1)S(1)}, bf16[384,768]{1,0:T(8,128)(2,1)S(1)}, u32[]{:S(2)}, u32[]{:S(2)}) collective-permute-start(bf16[384,768]{1,0:T(8,128)(2,1)S(1)} %get-tuple-element.91), channel_id=1, source_target_pairs={{0,1},{1,2},{2,3},{3,0},{4,5},{5,6},{6,7},{7,4},{8,9},{9,10},{10,1... | collective-permute-start | bytes 1769480 | tf_op jit(solution)/shard_map/ppermute | solution.py:241
  160.7 14.2 %collective-permute-start.25 = (bf16[384,768]{1,0:T(8,128)(2,1)S(1)}, bf16[384,768]{1,0:T(8,128)(2,1)S(1)}, u32[]{:S(2)}, u32[]{:S(2)}) collective-permute-start(bf16[384,768]{1,0:T(8,128)(2,1)S(1)} %add_convert_fusion.1), channel_id=1, source_target_pairs={{0,3},{1,0},{2,1},{3,2},{4,7},{5,4},{6,5},{7,6},{8,11},{9,8},{10,9... | collective-permute-start | bytes 1769480 | tf_op jit(solution)/shard_map/ppermute | solution.py:241
  210.4 7.2 %collective-permute-start.26 = (bf16[32,768]{1,0:T(8,128)(2,1)S(1)}, bf16[32,768]{1,0:T(8,128)(2,1)S(1)}, u32[]{:S(2)}, u32[]{:S(2)}) collective-permute-start(bf16[32,768]{1,0:T(8,128)(2,1)S(1)} %get-tuple-element.98), channel_id=1, source_target_pairs={{0,1},{1,2},{2,3},{3,0},{4,5},{5,6},{6,7},{7,4},{8,9},{9,10},{10,1... | collective-permute-start | bytes 147464 | tf_op jit(solution)/shard_map/ppermute | solution.py:241
  212.8 5.6 %collective-permute-start.27 = (bf16[32,768]{1,0:T(8,128)(2,1)S(1)}, bf16[32,768]{1,0:T(8,128)(2,1)S(1)}, u32[]{:S(2)}, u32[]{:S(2)}) collective-permute-start(bf16[32,768]{1,0:T(8,128)(2,1)S(1)} %get-tuple-element.99), channel_id=1, source_target_pairs={{0,2},{1,3},{2,0},{3,1},{4,6},{5,7},{6,4},{7,5},{8,10},{9,11},{10,... | collective-permute-start | bytes 147464 | tf_op jit(solution)/shard_map/ppermute | solution.py:241
  (18 other events, 184.4 us)

commit v5 on v4

--- a/solution.py
+++ b/solution.py
@@ -349,27 +349,7 @@
         compiler_params=params(28),
         name="attend",
     )(h_at, core_at, query_rows, inner, mine, other, norm_gain.reshape(1, width), out_weight.T)
-    across = shift(parts[2], 2)
-    pieces = [parts[0], shift(parts[1], 1), across, shift(parts[3], 3)]
-
-    packed, attended = pl.pallas_call(
-        pack_body,
-        out_shape=(shape((rows, padded), BF), shape((tokens, quarter), F32)),
-        in_specs=[SMEM_SPEC] + [VMEM_SPEC] * 7,
-        out_specs=(VMEM_SPEC,) * 2,
-        scratch_shapes=[pltpu.VMEM((tokens, padded), BF), pltpu.VMEM((4, 1, quarter), F32)],
-        compiler_params=params(28),
-        name="pack",
-    )(h_at, *pieces, residual.T, moe_gain.reshape(1, features), place)
-
-    arrived = lax.all_to_all(
-        packed.reshape(chips, capacity, padded), chip, 0, 0, tiled=True
-    ).reshape(rows, padded)
-    half = rows // 2
-    arrived, late_h = lax.optimization_barrier((arrived, h_at))
-    low, high = arrived[:half], arrived[half:]
-
-    minus_low, plus_low = shift(low, 1), shift(low, -1)
+    parts, late_h = lax.optimization_barrier((parts, h_at))
     hidden_count = gate_weight.shape[2]
     wide = -(-hidden_count // 128) * 128
     weights = pl.pallas_call(
@@ -381,6 +361,27 @@
         cost_estimate=cost(5e9, 13e6),
         name="weights",
     )(late_h, gate_weight[0].T, up_weight[0].T, down_weight[0])
+    across = shift(parts[2], 2)
+    pieces = [parts[0], shift(parts[1], 1), across, shift(parts[3], 3)]
+    pieces, weights = lax.optimization_barrier((pieces, weights))
+
+    packed, attended = pl.pallas_call(
+        pack_body,
+        out_shape=(shape((rows, padded), BF), shape((tokens, quarter), F32)),
+        in_specs=[SMEM_SPEC] + [VMEM_SPEC] * 7,
+        out_specs=(VMEM_SPEC,) * 2,
+        scratch_shapes=[pltpu.VMEM((tokens, padded), BF), pltpu.VMEM((4, 1, quarter), F32)],
+        compiler_params=params(28),
+        name="pack",
+    )(h_at, *pieces, residual.T, moe_gain.reshape(1, features), place)
+
+    arrived = lax.all_to_all(
+        packed.reshape(chips, capacity, padded), chip, 0, 0, tiled=True
+    ).reshape(rows, padded)
+    half = rows // 2
+    arrived, weights = lax.optimization_barrier((arrived, weights))
+    low, high = arrived[:half], arrived[half:]
+    minus_low, plus_low = shift(low, 1), shift(low, -1)
     minus_low, plus_low, high, weights = lax.optimization_barrier(
         (minus_low, plus_low, high, weights)
     )

time: 221 us -> 221 us (level)
  no operation moved by 1% of the time
where the time goes in v5:
time: 221 us; the launch traced here: 220 us
  blocking collectives  74.9 us (34%)
  waiting for transfers between devices  69.5 us (31%)
  starting transfers between devices  43.3 us (20%)
  Pallas kernels  27.9 us (13%)
  local copies, waits for them, and re-layouts  2.96 us (1%)
    ppermute x18, waiting for transfers between devices, shift(): return lax.ppermute(x, 'heads', [(i, (i + by) % 4) for i in range(4)])  59.2 us
    all_to_all x1, blocking collectives, on_device(): lax.all_to_all(packed.reshape(chips, capacity, padded), chip, 0, 0, tiled...  41 us
    all_to_all x1, blocking collectives, on_device(): lax.all_to_all(leaving, chip, 0, 0, tiled=True).reshape(rows, padded)  33.9 us
    ppermute x18, starting transfers between devices, shift(): return lax.ppermute(x, 'heads', [(i, (i + by) % 4) for i in range(4)])  27.1 us
    pallas_call x2, Pallas kernels, experts(): pl.pallas_call(functools.partial(expert_body, features), out_shape=(shape...  17.7 us
    ppermute x4, starting transfers between devices, deeper(): return lax.ppermute(x, 'z', [(i, (i + j) % depth) for i in range(depth)])  9.79 us
    ppermute x3, starting transfers between devices, on_device(): lax.ppermute(chip_state, 'x', [(i, (i + j) % breadth) for i in range(brea...  5.73 us
    ppermute x4, waiting for transfers between devices, deeper(): return lax.ppermute(x, 'z', [(i, (i + j) % depth) for i in range(depth)])  5.47 us
  transfers between devices with their start and end apart: 29, of which 21 were waited for; matrix products, arithmetic and copies ran while one was open for 0% of the time, Pallas kernels for 11%

profile of v5, /device:TPU:8, one launch (start us, length us, event | category | flops | bytes accessed | tf_op | source)
XLA Modules:
  0.0 219.7 jit_solution(13341484661682155094)
XLA Ops:
  5.1 2.7 %collective-permute-start.2 = (bf16[32,896]{1,0:T(8,128)(2,1)S(1)}, bf16[32,896]{1,0:T(8,128)(2,1)S(1)}, u32[]{:S(2)}, u32[]{:S(2)}) collective-permute-start(bf16[32,896]{1,0:T(8,128)(2,1)S(1)} %add_convert_fusion.5), channel_id=1, source_target_pairs={{0,16},{8,24},{16,0},{24,8},{1,17},{9,25},{17,1},{25,9},{2,18},{10... | collective-permute-start | bytes 172040 | tf_op jit(solution)/shard_map/ppermute | solution.py:305
  14.0 3.3 %collective-permute-start.5 = (bf16[32,896]{1,0:T(8,128)(2,1)S(1)}, bf16[32,896]{1,0:T(8,128)(2,1)S(1)}, u32[]{:S(2)}, u32[]{:S(2)}) collective-permute-start(bf16[32,896]{1,0:T(8,128)(2,1)S(1)} %add_convert_fusion.4.slab_ref), channel_id=1, source_target_pairs={{0,64},{32,96},{64,128},{96,160},{128,192},{160,224},{192,0},{224,... | collective-permute-start | bytes 172040 | tf_op jit(solution)/shard_map/ppermute | solution.py:311
  18.2 2.3 %inner.1.inner_ref = f32[128,896]{1,0:T(8,128)S(1)} custom-call(bf16[128,896]{1,0:T(8,128)(2,1)S(1)} %copy-done.3, bf16[128,896]{1,0:T(8,128)(2,1)S(1)} %get-tuple-element.70.k_ref, bf16[128,896]{1,0:T(8,128)(2,1)S(1)} %get-tuple-element.71.v_ref), custom_call_target="tpu_custom_call" | custom-call | flops 2000000000 | bytes 2000000 | tf_op jit(solution)/shard_map/inner/pallas_call | solution.py:293
  20.5 2.3 %collective-permute-done.5.next_ref.rest_1_ = bf16[32,896]{1,0:T(8,128)(2,1)S(1)} collective-permute-done((bf16[32,896]{1,0:T(8,128)(2,1)S(1)}, bf16[32,896]{1,0:T(8,128)(2,1)S(1)}, u32[]{:S(2)}, u32[]{:S(2)}) %collective-permute-start.5) | collective-permute-done | bytes 57376 | tf_op jit(solution)/shard_map/ppermute | solution.py:311
  22.8 2.3 %collective-permute-start.6 = (bf16[32,896]{1,0:T(8,128)(2,1)S(1)}, bf16[32,896]{1,0:T(8,128)(2,1)S(1)}, u32[]{:S(2)}, u32[]{:S(2)}) collective-permute-start(bf16[32,896]{1,0:T(8,128)(2,1)S(1)} %triple.1), channel_id=1, source_target_pairs={{0,96},{32,128},{64,160},{96,192},{128,224},{160,0},{192,32},{224,... | collective-permute-start | bytes 172040 | tf_op jit(solution)/shard_map/ppermute | solution.py:311
  25.1 2.2 %collective-permute-start.7 = (bf16[32,896]{1,0:T(8,128)(2,1)S(1)}, bf16[32,896]{1,0:T(8,128)(2,1)S(1)}, u32[]{:S(2)}, u32[]{:S(2)}) collective-permute-start(bf16[32,896]{1,0:T(8,128)(2,1)S(1)} %triple.1), channel_id=1, source_target_pairs={{0,192},{32,224},{64,0},{96,32},{128,64},{160,96},{192,128},{224,1... | collective-permute-start | bytes 172040 | tf_op jit(solution)/shard_map/ppermute | solution.py:311
  27.4 2.8 %collective-permute-done.6.rest_2_ = bf16[32,896]{1,0:T(8,128)(2,1)S(1)} collective-permute-done((bf16[32,896]{1,0:T(8,128)(2,1)S(1)}, bf16[32,896]{1,0:T(8,128)(2,1)S(1)}, u32[]{:S(2)}, u32[]{:S(2)}) %collective-permute-start.6) | collective-permute-done | bytes 57376 | tf_op jit(solution)/shard_map/ppermute | solution.py:311
  32.0 2.2 %attend.1 = (bf16[128,768]{1,0:T(8,128)(2,1)S(1)}, bf16[128,768]{1,0:T(8,128)(2,1)S(1)}, bf16[128,768]{1,0:T(8,128)(2,1)S(1)}, bf16[128,768]{1,0:T(8,128)(2,1)S(1)}) custom-call(s32[1]{0:T(128)} %bitcast.at_ref, s32[1]{0:T(128)} %bitcast.1.at_ref.core_ref, bf16[128,896]{1,0:T(8,128)(2,1)S(1)} %copy-done.4, f32[128,896]{1,0:T(8,128)S(1)} %inner.1.inner_ref, ...), custom_call_target="tpu_custom_call" | custom-call | tf_op jit(solution)/shard_map/attend/pallas_call | solution.py:343
  34.3 2.4 %collective-permute-start.10 = (bf16[128,768]{1,0:T(8,128)(2,1)S(1)}, bf16[128,768]{1,0:T(8,128)(2,1)S(1)}, u32[]{:S(2)}, u32[]{:S(2)}) collective-permute-start(bf16[128,768]{1,0:T(8,128)(2,1)S(1)} %get-tuple-element.85), channel_id=1, source_target_pairs={{0,2},{1,3},{2,0},{3,1},{4,6},{5,7},{6,4},{7,5},{8,10},{9,11},{10,... | collective-permute-start | bytes 589832 | tf_op jit(solution)/shard_map/ppermute | solution.py:241
  38.7 3.0 %weights.1 = (bf16[4,768,768]{2,1,0:T(8,128)(2,1)S(1)}, bf16[4,360,768]{2,1,0:T(8,128)(2,1)S(1)}) custom-call(s32[1]{0:T(128)} %bitcast.at_ref, bf16[360,2880]{1,0:T(8,128)(2,1)S(1)} %bitcast.25, bf16[360,2880]{1,0:T(8,128)(2,1)S(1)} %bitcast.26, bf16[360,2880]{1,0:T(8,128)(2,1)S(1)} %bitcast.27), custom_call_target="tpu_custom_call" | custom-call | flops 5000000000 | bytes 13000000 | tf_op jit(solution)/shard_map/weights/pallas_call | solution.py:355
  43.7 3.4 %collective-permute-done.11.p3 = bf16[128,768]{1,0:T(8,128)(2,1)S(1)} collective-permute-done((bf16[128,768]{1,0:T(8,128)(2,1)S(1)}, bf16[128,768]{1,0:T(8,128)(2,1)S(1)}, u32[]{:S(2)}, u32[]{:S(2)}) %collective-permute-start.11) | collective-permute-done | bytes 196640 | tf_op jit(solution)/shard_map/ppermute | solution.py:241
  48.0 41.0 %all_to_all.10 = bf16[32,24,768]{2,1,0:T(8,128)(2,1)S(1)} all-to-all(bf16[32,24,768]{2,1,0:T(8,128)(2,1)S(1)} %bitcast.23), channel_id=1, replica_groups=mesh['z'=8,'x'=4,'core'=2,'heads'=4] {'z','x'}, dimensions={0} | all-to-all | bytes 2359296 | tf_op jit(solution)/shard_map/all_to_all | solution.py:378
  91.2 10.9 %collective-permute-done.12.x3 = bf16[384,768]{1,0:T(8,128)(2,1)S(1)} collective-permute-done((bf16[384,768]{1,0:T(8,128)(2,1)S(1)}, bf16[384,768]{1,0:T(8,128)(2,1)S(1)}, u32[]{:S(2)}, u32[]{:S(2)}) %collective-permute-start.12) | collective-permute-done | bytes 589856 | tf_op jit(solution)/shard_map/ppermute | solution.py:241
  106.5 13.2 %collective-permute-done.14.x2 = bf16[384,768]{1,0:T(8,128)(2,1)S(1)} collective-permute-done((bf16[384,768]{1,0:T(8,128)(2,1)S(1)}, bf16[384,768]{1,0:T(8,128)(2,1)S(1)}, u32[]{:S(2)}, u32[]{:S(2)}) %collective-permute-start.14) | collective-permute-done | bytes 589856 | tf_op jit(solution)/shard_map/ppermute | solution.py:241
  121.8 8.8 %experts.2 = (bf16[384,768]{1,0:T(8,128)(2,1)S(1)}, bf16[384,768]{1,0:T(8,128)(2,1)S(1)}, bf16[384,768]{1,0:T(8,128)(2,1)S(1)}, bf16[384,768]{1,0:T(8,128)(2,1)S(1)}) custom-call(bf16[384,768]{1,0:T(8,128)(2,1)S(1)} %get-tuple-element.126.x0, bf16[384,768]{1,0:T(8,128)(2,1)S(1)} %collective-permute-done.13.x1, ...), custom_call_target="tpu_custom_call" | custom-call | flops 1000000 | bytes 100000 | tf_op jit(solution)/shard_map/experts/pallas_call | solution.py:391
  137.3 8.8 %experts.3 = (bf16[384,768]{1,0:T(8,128)(2,1)S(1)}, bf16[384,768]{1,0:T(8,128)(2,1)S(1)}, bf16[384,768]{1,0:T(8,128)(2,1)S(1)}, bf16[384,768]{1,0:T(8,128)(2,1)S(1)}) custom-call(bf16[384,768]{1,0:T(8,128)(2,1)S(1)} %get-tuple-element.113.x0, bf16[384,768]{1,0:T(8,128)(2,1)S(1)} %collective-permute-done.20.x1, ...), custom_call_target="tpu_custom_call" | custom-call | flops 1000000 | bytes 100000 | tf_op jit(solution)/shard_map/experts/pallas_call | solution.py:391
  147.1 2.9 %collective-permute-done.18 = bf16[384,768]{1,0:T(8,128)(2,1)S(1)} collective-permute-done((bf16[384,768]{1,0:T(8,128)(2,1)S(1)}, bf16[384,768]{1,0:T(8,128)(2,1)S(1)}, u32[]{:S(2)}, u32[]{:S(2)}) %collective-permute-start.18) | collective-permute-done | bytes 589856 | tf_op jit(solution)/shard_map/ppermute | solution.py:241
  150.7 3.3 %collective-permute-start.23 = (bf16[384,768]{1,0:T(8,128)(2,1)S(1)}, bf16[384,768]{1,0:T(8,128)(2,1)S(1)}, u32[]{:S(2)}, u32[]{:S(2)}) collective-permute-start(bf16[384,768]{1,0:T(8,128)(2,1)S(1)} %get-tuple-element.115), channel_id=1, source_target_pairs={{0,1},{1,2},{2,3},{3,0},{4,5},{5,6},{6,7},{7,4},{8,9},{9,10},{10,1... | collective-permute-start | bytes 1769480 | tf_op jit(solution)/shard_map/ppermute | solution.py:241
  154.0 6.5 %collective-permute-done.24 = bf16[384,768]{1,0:T(8,128)(2,1)S(1)} collective-permute-done((bf16[384,768]{1,0:T(8,128)(2,1)S(1)}, bf16[384,768]{1,0:T(8,128)(2,1)S(1)}, u32[]{:S(2)}, u32[]{:S(2)}) %collective-permute-start.24) | collective-permute-done | bytes 589856 | tf_op jit(solution)/shard_map/ppermute | solution.py:241
  161.9 4.5 %collective-permute-done.19 = bf16[384,768]{1,0:T(8,128)(2,1)S(1)} collective-permute-done((bf16[384,768]{1,0:T(8,128)(2,1)S(1)}, bf16[384,768]{1,0:T(8,128)(2,1)S(1)}, u32[]{:S(2)}, u32[]{:S(2)}) %collective-permute-start.19) | collective-permute-done | bytes 589856 | tf_op jit(solution)/shard_map/ppermute | solution.py:241
  166.6 8.3 %collective-permute-done.23 = bf16[384,768]{1,0:T(8,128)(2,1)S(1)} collective-permute-done((bf16[384,768]{1,0:T(8,128)(2,1)S(1)}, bf16[384,768]{1,0:T(8,128)(2,1)S(1)}, u32[]{:S(2)}, u32[]{:S(2)}) %collective-permute-start.23) | collective-permute-done | bytes 589856 | tf_op jit(solution)/shard_map/ppermute | solution.py:241
  175.3 33.9 %all_to_all.11 = bf16[32,24,768]{2,1,0:T(8,128)(2,1)S(1)} all-to-all(bf16[32,24,768]{2,1,0:T(8,128)(2,1)S(1)} %bitcast.31), channel_id=1, replica_groups=mesh['z'=8,'x'=4,'core'=2,'heads'=4] {'z','x'}, dimensions={0} | all-to-all | bytes 2359296 | tf_op jit(solution)/shard_map/all_to_all | solution.py:419
  209.7 2.4 %collective-permute-start.26 = (bf16[32,768]{1,0:T(8,128)(2,1)S(1)}, bf16[32,768]{1,0:T(8,128)(2,1)S(1)}, u32[]{:S(2)}, u32[]{:S(2)}) collective-permute-start(bf16[32,768]{1,0:T(8,128)(2,1)S(1)} %get-tuple-element.122), channel_id=1, source_target_pairs={{0,1},{1,2},{2,3},{3,0},{4,5},{5,6},{6,7},{7,4},{8,9},{9,10},{10,1... | collective-permute-start | bytes 147464 | tf_op jit(solution)/shard_map/ppermute | solution.py:241
  212.2 2.6 %collective-permute-start.27 = (bf16[32,768]{1,0:T(8,128)(2,1)S(1)}, bf16[32,768]{1,0:T(8,128)(2,1)S(1)}, u32[]{:S(2)}, u32[]{:S(2)}) collective-permute-start(bf16[32,768]{1,0:T(8,128)(2,1)S(1)} %get-tuple-element.123), channel_id=1, source_target_pairs={{0,2},{1,3},{2,0},{3,1},{4,6},{5,7},{6,4},{7,5},{8,10},{9,11},{10,... | collective-permute-start | bytes 147464 | tf_op jit(solution)/shard_map/ppermute | solution.py:241
  (87 shorter events, 43.4 us)
Async XLA Ops:
  3.5 5.7 %collective-permute-start.1 = (bf16[32,896]{1,0:T(8,128)(2,1)S(1)}, bf16[32,896]{1,0:T(8,128)(2,1)S(1)}, u32[]{:S(2)}, u32[]{:S(2)}) collective-permute-start(bf16[32,896]{1,0:T(8,128)(2,1)S(1)} %add_convert_fusion.5), channel_id=1, source_target_pairs={{0,8},{8,16},{16,24},{24,0},{1,9},{9,17},{17,25},{25,1},{2,10},{10... | collective-permute-start | bytes 172040 | tf_op jit(solution)/shard_map/ppermute | solution.py:305
  5.1 5.9 %collective-permute-start.2 = (bf16[32,896]{1,0:T(8,128)(2,1)S(1)}, bf16[32,896]{1,0:T(8,128)(2,1)S(1)}, u32[]{:S(2)}, u32[]{:S(2)}) collective-permute-start(bf16[32,896]{1,0:T(8,128)(2,1)S(1)} %add_convert_fusion.5), channel_id=1, source_target_pairs={{0,16},{8,24},{16,0},{24,8},{1,17},{9,25},{17,1},{25,9},{2,18},{10... | collective-permute-start | bytes 172040 | tf_op jit(solution)/shard_map/ppermute | solution.py:305
  12.0 8.5 %collective-permute-start.4 = (bf16[32,896]{1,0:T(8,128)(2,1)S(1)}, bf16[32,896]{1,0:T(8,128)(2,1)S(1)}, u32[]{:S(2)}, u32[]{:S(2)}) collective-permute-start(bf16[32,896]{1,0:T(8,128)(2,1)S(1)} %add_convert_fusion.4.slab_ref), channel_id=1, source_target_pairs={{0,32},{32,64},{64,96},{96,128},{128,160},{160,192},{192,224},{224... | collective-permute-start | bytes 172040 | tf_op jit(solution)/shard_map/ppermute | solution.py:311
  14.0 8.8 %collective-permute-start.5 = (bf16[32,896]{1,0:T(8,128)(2,1)S(1)}, bf16[32,896]{1,0:T(8,128)(2,1)S(1)}, u32[]{:S(2)}, u32[]{:S(2)}) collective-permute-start(bf16[32,896]{1,0:T(8,128)(2,1)S(1)} %add_convert_fusion.4.slab_ref), channel_id=1, source_target_pairs={{0,64},{32,96},{64,128},{96,160},{128,192},{160,224},{192,0},{224,... | collective-permute-start | bytes 172040 | tf_op jit(solution)/shard_map/ppermute | solution.py:311
  22.8 7.4 %collective-permute-start.6 = (bf16[32,896]{1,0:T(8,128)(2,1)S(1)}, bf16[32,896]{1,0:T(8,128)(2,1)S(1)}, u32[]{:S(2)}, u32[]{:S(2)}) collective-permute-start(bf16[32,896]{1,0:T(8,128)(2,1)S(1)} %triple.1), channel_id=1, source_target_pairs={{0,96},{32,128},{64,160},{96,192},{128,224},{160,0},{192,32},{224,... | collective-permute-start | bytes 172040 | tf_op jit(solution)/shard_map/ppermute | solution.py:311
  34.3 9.4 %collective-permute-start.10 = (bf16[128,768]{1,0:T(8,128)(2,1)S(1)}, bf16[128,768]{1,0:T(8,128)(2,1)S(1)}, u32[]{:S(2)}, u32[]{:S(2)}) collective-permute-start(bf16[128,768]{1,0:T(8,128)(2,1)S(1)} %get-tuple-element.85), channel_id=1, source_target_pairs={{0,2},{1,3},{2,0},{3,1},{4,6},{5,7},{6,4},{7,5},{8,10},{9,11},{10,... | collective-permute-start | bytes 589832 | tf_op jit(solution)/shard_map/ppermute | solution.py:241
  36.7 10.4 %collective-permute-start.11 = (bf16[128,768]{1,0:T(8,128)(2,1)S(1)}, bf16[128,768]{1,0:T(8,128)(2,1)S(1)}, u32[]{:S(2)}, u32[]{:S(2)}) collective-permute-start(bf16[128,768]{1,0:T(8,128)(2,1)S(1)} %get-tuple-element.86), channel_id=1, source_target_pairs={{0,3},{1,0},{2,1},{3,2},{4,7},{5,4},{6,5},{7,6},{8,11},{9,8},{10,9... | collective-permute-start | bytes 589832 | tf_op jit(solution)/shard_map/ppermute | solution.py:241
  38.0 9.2 %collective-permute-start.9 = (bf16[128,768]{1,0:T(8,128)(2,1)S(1)}, bf16[128,768]{1,0:T(8,128)(2,1)S(1)}, u32[]{:S(2)}, u32[]{:S(2)}) collective-permute-start(bf16[128,768]{1,0:T(8,128)(2,1)S(1)} %get-tuple-element.84), channel_id=1, source_target_pairs={{0,1},{1,2},{2,3},{3,0},{4,5},{5,6},{6,7},{7,4},{8,9},{9,10},{10,1... | collective-permute-start | bytes 589832 | tf_op jit(solution)/shard_map/ppermute | solution.py:241
  89.1 13.0 %collective-permute-start.12 = (bf16[384,768]{1,0:T(8,128)(2,1)S(1)}, bf16[384,768]{1,0:T(8,128)(2,1)S(1)}, u32[]{:S(2)}, u32[]{:S(2)}) collective-permute-start(bf16[384,768]{1,0:T(8,128)(2,1)S(1)} %get-tuple-element.126.x0), channel_id=1, source_target_pairs={{0,1},{1,2},{2,3},{3,0},{4,5},{5,6},{6,7},{7,4},{8,9},{9,10},{10,1... | collective-permute-start | bytes 1769480 | tf_op jit(solution)/shard_map/ppermute | solution.py:241
  90.7 13.3 %collective-permute-start.13 = (bf16[384,768]{1,0:T(8,128)(2,1)S(1)}, bf16[384,768]{1,0:T(8,128)(2,1)S(1)}, u32[]{:S(2)}, u32[]{:S(2)}) collective-permute-start(bf16[384,768]{1,0:T(8,128)(2,1)S(1)} %get-tuple-element.126.x0), channel_id=1, source_target_pairs={{0,3},{1,0},{2,1},{3,2},{4,7},{5,4},{6,5},{7,6},{8,11},{9,8},{10,9... | collective-permute-start | bytes 1769480 | tf_op jit(solution)/shard_map/ppermute | solution.py:241
  104.0 17.8 %collective-permute-start.15 = (bf16[4,768,768]{2,1,0:T(8,128)(2,1)S(1)}, bf16[4,768,768]{2,1,0:T(8,128)(2,1)S(1)}, u32[]{:S(2)}, u32[]{:S(2)}) collective-permute-start(bf16[4,768,768]{2,1,0:T(8,128)(2,1)S(1)} %get-tuple-element.105.mid0), channel_id=1, source_target_pairs={{0,4},{4,0},{1,5},{5,1},{2,6},{6,2},{3,7},{7,3},{8,12},{12,8},{9,1... | collective-permute-start | bytes 14155784 | tf_op jit(solution)/shard_map/ppermute | solution.py:245
  104.0 17.8 %collective-permute-start.16 = (bf16[4,360,768]{2,1,0:T(8,128)(2,1)S(1)}, bf16[4,360,768]{2,1,0:T(8,128)(2,1)S(1)}, u32[]{:S(2)}, u32[]{:S(2)}) collective-permute-start(bf16[4,360,768]{2,1,0:T(8,128)(2,1)S(1)} %get-tuple-element.106.out0), channel_id=1, source_target_pairs={{0,4},{4,0},{1,5},{5,1},{2,6},{6,2},{3,7},{7,3},{8,12},{12,8},{9,1... | collective-permute-start | bytes 6635528 | tf_op jit(solution)/shard_map/ppermute | solution.py:245
  104.5 15.2 %collective-permute-start.14 = (bf16[384,768]{1,0:T(8,128)(2,1)S(1)}, bf16[384,768]{1,0:T(8,128)(2,1)S(1)}, u32[]{:S(2)}, u32[]{:S(2)}) collective-permute-start(bf16[384,768]{1,0:T(8,128)(2,1)S(1)} %collective-permute-done.12.x3), channel_id=1, source_target_pairs={{0,1},{1,2},{2,3},{3,0},{4,5},{5,6},{6,7},{7,4},{8,9},{9,10},{10,1... | collective-permute-start | bytes 1769480 | tf_op jit(solution)/shard_map/ppermute | solution.py:241
  105.8 15.2 %collective-permute-start.20 = (bf16[384,768]{1,0:T(8,128)(2,1)S(1)}, bf16[384,768]{1,0:T(8,128)(2,1)S(1)}, u32[]{:S(2)}, u32[]{:S(2)}) collective-permute-start(bf16[384,768]{1,0:T(8,128)(2,1)S(1)} %get-tuple-element.113.x0), channel_id=1, source_target_pairs={{0,3},{1,0},{2,1},{3,2},{4,7},{5,4},{6,5},{7,6},{8,11},{9,8},{10,9... | collective-permute-start | bytes 1769480 | tf_op jit(solution)/shard_map/ppermute | solution.py:241
  119.7 15.5 %collective-permute-start.22 = (bf16[384,768]{1,0:T(8,128)(2,1)S(1)}, bf16[384,768]{1,0:T(8,128)(2,1)S(1)}, u32[]{:S(2)}, u32[]{:S(2)}) collective-permute-start(bf16[384,768]{1,0:T(8,128)(2,1)S(1)} %get-tuple-element.113.x0), channel_id=1, source_target_pairs={{0,1},{1,2},{2,3},{3,0},{4,5},{5,6},{6,7},{7,4},{8,9},{9,10},{10,1... | collective-permute-start | bytes 1769480 | tf_op jit(solution)/shard_map/ppermute | solution.py:241
  121.0 16.3 %collective-permute-start.21 = (bf16[384,768]{1,0:T(8,128)(2,1)S(1)}, bf16[384,768]{1,0:T(8,128)(2,1)S(1)}, u32[]{:S(2)}, u32[]{:S(2)}) collective-permute-start(bf16[384,768]{1,0:T(8,128)(2,1)S(1)} %collective-permute-done.20.x1), channel_id=1, source_target_pairs={{0,3},{1,0},{2,1},{3,2},{4,7},{5,4},{6,5},{7,6},{8,11},{9,8},{10,9... | collective-permute-start | bytes 1769480 | tf_op jit(solution)/shard_map/ppermute | solution.py:241
  130.6 16.5 %collective-permute-start.17 = (bf16[384,768]{1,0:T(8,128)(2,1)S(1)}, bf16[384,768]{1,0:T(8,128)(2,1)S(1)}, u32[]{:S(2)}, u32[]{:S(2)}) collective-permute-start(bf16[384,768]{1,0:T(8,128)(2,1)S(1)} %get-tuple-element.109), channel_id=1, source_target_pairs={{0,1},{1,2},{2,3},{3,0},{4,5},{5,6},{6,7},{7,4},{8,9},{9,10},{10,1... | collective-permute-start | bytes 1769480 | tf_op jit(solution)/shard_map/ppermute | solution.py:241
  132.0 17.9 %collective-permute-start.18 = (bf16[384,768]{1,0:T(8,128)(2,1)S(1)}, bf16[384,768]{1,0:T(8,128)(2,1)S(1)}, u32[]{:S(2)}, u32[]{:S(2)}) collective-permute-start(bf16[384,768]{1,0:T(8,128)(2,1)S(1)} %get-tuple-element.110), channel_id=1, source_target_pairs={{0,3},{1,0},{2,1},{3,2},{4,7},{5,4},{6,5},{7,6},{8,11},{9,8},{10,9... | collective-permute-start | bytes 1769480 | tf_op jit(solution)/shard_map/ppermute | solution.py:241
  146.1 14.3 %collective-permute-start.24 = (bf16[384,768]{1,0:T(8,128)(2,1)S(1)}, bf16[384,768]{1,0:T(8,128)(2,1)S(1)}, u32[]{:S(2)}, u32[]{:S(2)}) collective-permute-start(bf16[384,768]{1,0:T(8,128)(2,1)S(1)} %get-tuple-element.117), channel_id=1, source_target_pairs={{0,3},{1,0},{2,1},{3,2},{4,7},{5,4},{6,5},{7,6},{8,11},{9,8},{10,9... | collective-permute-start | bytes 1769480 | tf_op jit(solution)/shard_map/ppermute | solution.py:241
  150.1 16.3 %collective-permute-start.19 = (bf16[384,768]{1,0:T(8,128)(2,1)S(1)}, bf16[384,768]{1,0:T(8,128)(2,1)S(1)}, u32[]{:S(2)}, u32[]{:S(2)}) collective-permute-start(bf16[384,768]{1,0:T(8,128)(2,1)S(1)} %add_convert_fusion.3), channel_id=1, source_target_pairs={{0,1},{1,2},{2,3},{3,0},{4,5},{5,6},{6,7},{7,4},{8,9},{9,10},{10,1... | collective-permute-start | bytes 1769480 | tf_op jit(solution)/shard_map/ppermute | solution.py:241
  150.7 24.3 %collective-permute-start.23 = (bf16[384,768]{1,0:T(8,128)(2,1)S(1)}, bf16[384,768]{1,0:T(8,128)(2,1)S(1)}, u32[]{:S(2)}, u32[]{:S(2)}) collective-permute-start(bf16[384,768]{1,0:T(8,128)(2,1)S(1)} %get-tuple-element.115), channel_id=1, source_target_pairs={{0,1},{1,2},{2,3},{3,0},{4,5},{5,6},{6,7},{7,4},{8,9},{9,10},{10,1... | collective-permute-start | bytes 1769480 | tf_op jit(solution)/shard_map/ppermute | solution.py:241
  160.6 14.4 %collective-permute-start.25 = (bf16[384,768]{1,0:T(8,128)(2,1)S(1)}, bf16[384,768]{1,0:T(8,128)(2,1)S(1)}, u32[]{:S(2)}, u32[]{:S(2)}) collective-permute-start(bf16[384,768]{1,0:T(8,128)(2,1)S(1)} %add_convert_fusion.1), channel_id=1, source_target_pairs={{0,3},{1,0},{2,1},{3,2},{4,7},{5,4},{6,5},{7,6},{8,11},{9,8},{10,9... | collective-permute-start | bytes 1769480 | tf_op jit(solution)/shard_map/ppermute | solution.py:241
  209.7 7.2 %collective-permute-start.26 = (bf16[32,768]{1,0:T(8,128)(2,1)S(1)}, bf16[32,768]{1,0:T(8,128)(2,1)S(1)}, u32[]{:S(2)}, u32[]{:S(2)}) collective-permute-start(bf16[32,768]{1,0:T(8,128)(2,1)S(1)} %get-tuple-element.122), channel_id=1, source_target_pairs={{0,1},{1,2},{2,3},{3,0},{4,5},{5,6},{6,7},{7,4},{8,9},{9,10},{10,1... | collective-permute-start | bytes 147464 | tf_op jit(solution)/shard_map/ppermute | solution.py:241
  212.2 5.6 %collective-permute-start.27 = (bf16[32,768]{1,0:T(8,128)(2,1)S(1)}, bf16[32,768]{1,0:T(8,128)(2,1)S(1)}, u32[]{:S(2)}, u32[]{:S(2)}) collective-permute-start(bf16[32,768]{1,0:T(8,128)(2,1)S(1)} %get-tuple-element.123), channel_id=1, source_target_pairs={{0,2},{1,3},{2,0},{3,1},{4,6},{5,7},{6,4},{7,5},{8,10},{9,11},{10,... | collective-permute-start | bytes 147464 | tf_op jit(solution)/shard_map/ppermute | solution.py:241
  (19 other events, 155.0 us)

commit v6 on v5

--- a/solution.py
+++ b/solution.py
@@ -382,10 +382,10 @@
     arrived, weights = lax.optimization_barrier((arrived, weights))
     low, high = arrived[:half], arrived[half:]
     minus_low, plus_low = shift(low, 1), shift(low, -1)
-    minus_low, plus_low, high, weights = lax.optimization_barrier(
-        (minus_low, plus_low, high, weights)
-    )
     other_weights = tuple(swap(x) for x in weights)
+    minus_low, plus_low, high, other_weights = lax.optimization_barrier(
+        (minus_low, plus_low, high, other_weights)
+    )
 
     def experts(group):
         return pl.pallas_call(

time: 221 us -> 220 us (level)
  starting transfers between devices: 43.3 us -> 51.3 us
  waiting for transfers between devices: 69.5 us -> 64.1 us
  blocking collectives: 74.9 us -> 71.2 us
    ppermute x18, starting transfers between devices: 27.1 us -> 36.3 us  [shift(): return lax.ppermute(x, 'heads', [(i, (i + by) % 4) for i in range(4)])]
    ppermute x18, waiting for transfers between devices: 59.2 us -> 50.9 us  [shift(): return lax.ppermute(x, 'heads', [(i, (i + by) % 4) for i in range(4)])]
    all_to_all x1, blocking collectives: 41 us -> 38.5 us  [on_device(): lax.all_to_all(packed.reshape(chips, capacity, padded), chip, 0, 0, tiled...]
where the time goes in v6:
time: 220 us; the launch traced here: 219 us
  blocking collectives  71.2 us (32%)
  waiting for transfers between devices  64.1 us (29%)
  starting transfers between devices  51.3 us (23%)
  Pallas kernels  27.9 us (13%)
  local copies, waits for them, and re-layouts  2.96 us (1%)
    ppermute x18, waiting for transfers between devices, shift(): return lax.ppermute(x, 'heads', [(i, (i + by) % 4) for i in range(4)])  50.9 us
    all_to_all x1, blocking collectives, on_device(): lax.all_to_all(packed.reshape(chips, capacity, padded), chip, 0, 0, tiled...  38.5 us
    ppermute x18, starting transfers between devices, shift(): return lax.ppermute(x, 'heads', [(i, (i + by) % 4) for i in range(4)])  36.3 us
    all_to_all x1, blocking collectives, on_device(): lax.all_to_all(leaving, chip, 0, 0, tiled=True).reshape(rows, padded)  32.6 us
    pallas_call x2, Pallas kernels, experts(): pl.pallas_call(functools.partial(expert_body, features), out_shape=(shape...  17.7 us
    ppermute x4, starting transfers between devices, deeper(): return lax.ppermute(x, 'z', [(i, (i + j) % depth) for i in range(depth)])  9.88 us
    ppermute x4, waiting for transfers between devices, deeper(): return lax.ppermute(x, 'z', [(i, (i + j) % depth) for i in range(depth)])  6.43 us
    ppermute x3, waiting for transfers between devices, on_device(): lax.ppermute(chip_state, 'x', [(i, (i + j) % breadth) for i in range(brea...  4.75 us
  transfers between devices with their start and end apart: 29, of which 21 were waited for; matrix products, arithmetic and copies ran while one was open for 0% of the time, Pallas kernels for 11%

profile of v6, /device:TPU:8, one launch (start us, length us, event | category | flops | bytes accessed | tf_op | source)
XLA Modules:
  0.0 218.6 jit_solution(10728359235673304090)
XLA Ops:
  3.5 2.8 %collective-permute-start.3 = (bf16[32,896]{1,0:T(8,128)(2,1)S(1)}, bf16[32,896]{1,0:T(8,128)(2,1)S(1)}, u32[]{:S(2)}, u32[]{:S(2)}) collective-permute-start(bf16[32,896]{1,0:T(8,128)(2,1)S(1)} %add_convert_fusion.5), channel_id=1, source_target_pairs={{0,24},{8,0},{16,8},{24,16},{1,25},{9,1},{17,9},{25,17},{2,26},{10... | collective-permute-start | bytes 172040 | tf_op jit(solution)/shard_map/ppermute | solution.py:305
  8.7 3.5 %collective-permute-done.2.rest_5_ = bf16[32,896]{1,0:T(8,128)(2,1)S(1)} collective-permute-done((bf16[32,896]{1,0:T(8,128)(2,1)S(1)}, bf16[32,896]{1,0:T(8,128)(2,1)S(1)}, u32[]{:S(2)}, u32[]{:S(2)}) %collective-permute-start.2) | collective-permute-done | bytes 57376 | tf_op jit(solution)/shard_map/ppermute | solution.py:305
  12.8 3.3 %collective-permute-start.5 = (bf16[32,896]{1,0:T(8,128)(2,1)S(1)}, bf16[32,896]{1,0:T(8,128)(2,1)S(1)}, u32[]{:S(2)}, u32[]{:S(2)}) collective-permute-start(bf16[32,896]{1,0:T(8,128)(2,1)S(1)} %add_convert_fusion.4.slab_ref), channel_id=1, source_target_pairs={{0,64},{32,96},{64,128},{96,160},{128,192},{160,224},{192,0},{224,... | collective-permute-start | bytes 172040 | tf_op jit(solution)/shard_map/ppermute | solution.py:311
  22.3 2.8 %collective-permute-start.7 = (bf16[32,896]{1,0:T(8,128)(2,1)S(1)}, bf16[32,896]{1,0:T(8,128)(2,1)S(1)}, u32[]{:S(2)}, u32[]{:S(2)}) collective-permute-start(bf16[32,896]{1,0:T(8,128)(2,1)S(1)} %triple.1), channel_id=1, source_target_pairs={{0,192},{32,224},{64,0},{96,32},{128,64},{160,96},{192,128},{224,1... | collective-permute-start | bytes 172040 | tf_op jit(solution)/shard_map/ppermute | solution.py:311
  27.5 4.9 %collective-permute-done.6.rest_2_ = bf16[32,896]{1,0:T(8,128)(2,1)S(1)} collective-permute-done((bf16[32,896]{1,0:T(8,128)(2,1)S(1)}, bf16[32,896]{1,0:T(8,128)(2,1)S(1)}, u32[]{:S(2)}, u32[]{:S(2)}) %collective-permute-start.6) | collective-permute-done | bytes 57376 | tf_op jit(solution)/shard_map/ppermute | solution.py:311
  41.1 3.0 %weights.1 = (bf16[4,768,768]{2,1,0:T(8,128)(2,1)S(1)}, bf16[4,360,768]{2,1,0:T(8,128)(2,1)S(1)}) custom-call(s32[1]{0:T(128)} %bitcast.at_ref, bf16[360,2880]{1,0:T(8,128)(2,1)S(1)} %bitcast.25, bf16[360,2880]{1,0:T(8,128)(2,1)S(1)} %bitcast.26, bf16[360,2880]{1,0:T(8,128)(2,1)S(1)} %bitcast.27), custom_call_target="tpu_custom_call" | custom-call | flops 5000000000 | bytes 13000000 | tf_op jit(solution)/shard_map/weights/pallas_call | solution.py:355
  44.1 2.9 %collective-permute-done.10.p2 = bf16[128,768]{1,0:T(8,128)(2,1)S(1)} collective-permute-done((bf16[128,768]{1,0:T(8,128)(2,1)S(1)}, bf16[128,768]{1,0:T(8,128)(2,1)S(1)}, u32[]{:S(2)}, u32[]{:S(2)}) %collective-permute-start.10) | collective-permute-done | bytes 196640 | tf_op jit(solution)/shard_map/ppermute | solution.py:241
  50.2 38.5 %all_to_all.10 = bf16[32,24,768]{2,1,0:T(8,128)(2,1)S(1)} all-to-all(bf16[32,24,768]{2,1,0:T(8,128)(2,1)S(1)} %bitcast.23), channel_id=1, replica_groups=mesh['z'=8,'x'=4,'core'=2,'heads'=4] {'z','x'}, dimensions={0} | all-to-all | bytes 2359296 | tf_op jit(solution)/shard_map/all_to_all | solution.py:378
  91.5 13.2 %collective-permute-done.13.x1 = bf16[384,768]{1,0:T(8,128)(2,1)S(1)} collective-permute-done((bf16[384,768]{1,0:T(8,128)(2,1)S(1)}, bf16[384,768]{1,0:T(8,128)(2,1)S(1)}, u32[]{:S(2)}, u32[]{:S(2)}) %collective-permute-start.13) | collective-permute-done | bytes 589856 | tf_op jit(solution)/shard_map/ppermute | solution.py:241
  106.4 3.0 %collective-permute-start.20 = (bf16[384,768]{1,0:T(8,128)(2,1)S(1)}, bf16[384,768]{1,0:T(8,128)(2,1)S(1)}, u32[]{:S(2)}, u32[]{:S(2)}) collective-permute-start(bf16[384,768]{1,0:T(8,128)(2,1)S(1)} %get-tuple-element.113.x0), channel_id=1, source_target_pairs={{0,3},{1,0},{2,1},{3,2},{4,7},{5,4},{6,5},{7,6},{8,11},{9,8},{10,9... | collective-permute-start | bytes 1769480 | tf_op jit(solution)/shard_map/ppermute | solution.py:241
  109.4 12.2 %collective-permute-done.16.x2 = bf16[384,768]{1,0:T(8,128)(2,1)S(1)} collective-permute-done((bf16[384,768]{1,0:T(8,128)(2,1)S(1)}, bf16[384,768]{1,0:T(8,128)(2,1)S(1)}, u32[]{:S(2)}, u32[]{:S(2)}) %collective-permute-start.16) | collective-permute-done | bytes 589856 | tf_op jit(solution)/shard_map/ppermute | solution.py:241
  121.6 3.0 %collective-permute-start.21 = (bf16[384,768]{1,0:T(8,128)(2,1)S(1)}, bf16[384,768]{1,0:T(8,128)(2,1)S(1)}, u32[]{:S(2)}, u32[]{:S(2)}) collective-permute-start(bf16[384,768]{1,0:T(8,128)(2,1)S(1)} %collective-permute-done.20.x1), channel_id=1, source_target_pairs={{0,3},{1,0},{2,1},{3,2},{4,7},{5,4},{6,5},{7,6},{8,11},{9,8},{10,9... | collective-permute-start | bytes 1769480 | tf_op jit(solution)/shard_map/ppermute | solution.py:241
  124.6 8.8 %experts.2 = (bf16[384,768]{1,0:T(8,128)(2,1)S(1)}, bf16[384,768]{1,0:T(8,128)(2,1)S(1)}, bf16[384,768]{1,0:T(8,128)(2,1)S(1)}, bf16[384,768]{1,0:T(8,128)(2,1)S(1)}) custom-call(bf16[384,768]{1,0:T(8,128)(2,1)S(1)} %get-tuple-element.126.x0, bf16[384,768]{1,0:T(8,128)(2,1)S(1)} %collective-permute-done.13.x1, ...), custom_call_target="tpu_custom_call" | custom-call | flops 1000000 | bytes 100000 | tf_op jit(solution)/shard_map/experts/pallas_call | solution.py:391
  133.5 3.3 %collective-permute-start.18 = (bf16[384,768]{1,0:T(8,128)(2,1)S(1)}, bf16[384,768]{1,0:T(8,128)(2,1)S(1)}, u32[]{:S(2)}, u32[]{:S(2)}) collective-permute-start(bf16[384,768]{1,0:T(8,128)(2,1)S(1)} %get-tuple-element.110), channel_id=1, source_target_pairs={{0,3},{1,0},{2,1},{3,2},{4,7},{5,4},{6,5},{7,6},{8,11},{9,8},{10,9... | collective-permute-start | bytes 1769480 | tf_op jit(solution)/shard_map/ppermute | solution.py:241
  137.0 8.8 %experts.3 = (bf16[384,768]{1,0:T(8,128)(2,1)S(1)}, bf16[384,768]{1,0:T(8,128)(2,1)S(1)}, bf16[384,768]{1,0:T(8,128)(2,1)S(1)}, bf16[384,768]{1,0:T(8,128)(2,1)S(1)}) custom-call(bf16[384,768]{1,0:T(8,128)(2,1)S(1)} %get-tuple-element.113.x0, bf16[384,768]{1,0:T(8,128)(2,1)S(1)} %collective-permute-done.20.x1, ...), custom_call_target="tpu_custom_call" | custom-call | flops 1000000 | bytes 100000 | tf_op jit(solution)/shard_map/experts/pallas_call | solution.py:391
  145.8 3.1 %collective-permute-start.24 = (bf16[384,768]{1,0:T(8,128)(2,1)S(1)}, bf16[384,768]{1,0:T(8,128)(2,1)S(1)}, u32[]{:S(2)}, u32[]{:S(2)}) collective-permute-start(bf16[384,768]{1,0:T(8,128)(2,1)S(1)} %get-tuple-element.117), channel_id=1, source_target_pairs={{0,3},{1,0},{2,1},{3,2},{4,7},{5,4},{6,5},{7,6},{8,11},{9,8},{10,9... | collective-permute-start | bytes 1769480 | tf_op jit(solution)/shard_map/ppermute | solution.py:241
  150.5 3.3 %collective-permute-start.19 = (bf16[384,768]{1,0:T(8,128)(2,1)S(1)}, bf16[384,768]{1,0:T(8,128)(2,1)S(1)}, u32[]{:S(2)}, u32[]{:S(2)}) collective-permute-start(bf16[384,768]{1,0:T(8,128)(2,1)S(1)} %add_convert_fusion.3), channel_id=1, source_target_pairs={{0,1},{1,2},{2,3},{3,0},{4,5},{5,6},{6,7},{7,4},{8,9},{9,10},{10,1... | collective-permute-start | bytes 1769480 | tf_op jit(solution)/shard_map/ppermute | solution.py:241
  153.8 3.2 %collective-permute-start.23 = (bf16[384,768]{1,0:T(8,128)(2,1)S(1)}, bf16[384,768]{1,0:T(8,128)(2,1)S(1)}, u32[]{:S(2)}, u32[]{:S(2)}) collective-permute-start(bf16[384,768]{1,0:T(8,128)(2,1)S(1)} %get-tuple-element.115), channel_id=1, source_target_pairs={{0,1},{1,2},{2,3},{3,0},{4,5},{5,6},{6,7},{7,4},{8,9},{9,10},{10,1... | collective-permute-start | bytes 1769480 | tf_op jit(solution)/shard_map/ppermute | solution.py:241
  157.1 3.6 %collective-permute-done.24 = bf16[384,768]{1,0:T(8,128)(2,1)S(1)} collective-permute-done((bf16[384,768]{1,0:T(8,128)(2,1)S(1)}, bf16[384,768]{1,0:T(8,128)(2,1)S(1)}, u32[]{:S(2)}, u32[]{:S(2)}) %collective-permute-start.24) | collective-permute-done | bytes 589856 | tf_op jit(solution)/shard_map/ppermute | solution.py:241
  160.8 2.9 %collective-permute-start.25 = (bf16[384,768]{1,0:T(8,128)(2,1)S(1)}, bf16[384,768]{1,0:T(8,128)(2,1)S(1)}, u32[]{:S(2)}, u32[]{:S(2)}) collective-permute-start(bf16[384,768]{1,0:T(8,128)(2,1)S(1)} %add_convert_fusion.1), channel_id=1, source_target_pairs={{0,3},{1,0},{2,1},{3,2},{4,7},{5,4},{6,5},{7,6},{8,11},{9,8},{10,9... | collective-permute-start | bytes 1769480 | tf_op jit(solution)/shard_map/ppermute | solution.py:241
  163.7 4.5 %collective-permute-done.19 = bf16[384,768]{1,0:T(8,128)(2,1)S(1)} collective-permute-done((bf16[384,768]{1,0:T(8,128)(2,1)S(1)}, bf16[384,768]{1,0:T(8,128)(2,1)S(1)}, u32[]{:S(2)}, u32[]{:S(2)}) %collective-permute-start.19) | collective-permute-done | bytes 589856 | tf_op jit(solution)/shard_map/ppermute | solution.py:241
  168.4 7.0 %collective-permute-done.23 = bf16[384,768]{1,0:T(8,128)(2,1)S(1)} collective-permute-done((bf16[384,768]{1,0:T(8,128)(2,1)S(1)}, bf16[384,768]{1,0:T(8,128)(2,1)S(1)}, u32[]{:S(2)}, u32[]{:S(2)}) %collective-permute-start.23) | collective-permute-done | bytes 589856 | tf_op jit(solution)/shard_map/ppermute | solution.py:241
  175.7 32.6 %all_to_all.11 = bf16[32,24,768]{2,1,0:T(8,128)(2,1)S(1)} all-to-all(bf16[32,24,768]{2,1,0:T(8,128)(2,1)S(1)} %bitcast.31), channel_id=1, replica_groups=mesh['z'=8,'x'=4,'core'=2,'heads'=4] {'z','x'}, dimensions={0} | all-to-all | bytes 2359296 | tf_op jit(solution)/shard_map/all_to_all | solution.py:419
  213.5 2.5 %collective-permute-start.28 = (bf16[32,768]{1,0:T(8,128)(2,1)S(1)}, bf16[32,768]{1,0:T(8,128)(2,1)S(1)}, u32[]{:S(2)}, u32[]{:S(2)}) collective-permute-start(bf16[32,768]{1,0:T(8,128)(2,1)S(1)} %get-tuple-element.124), channel_id=1, source_target_pairs={{0,3},{1,0},{2,1},{3,2},{4,7},{5,4},{6,5},{7,6},{8,11},{9,8},{10,9... | collective-permute-start | bytes 147464 | tf_op jit(solution)/shard_map/ppermute | solution.py:241
  (87 shorter events, 41.4 us)
Async XLA Ops:
  6.3 5.8 %collective-permute-start.2 = (bf16[32,896]{1,0:T(8,128)(2,1)S(1)}, bf16[32,896]{1,0:T(8,128)(2,1)S(1)}, u32[]{:S(2)}, u32[]{:S(2)}) collective-permute-start(bf16[32,896]{1,0:T(8,128)(2,1)S(1)} %add_convert_fusion.5), channel_id=1, source_target_pairs={{0,16},{8,24},{16,0},{24,8},{1,17},{9,25},{17,1},{25,9},{2,18},{10... | collective-permute-start | bytes 172040 | tf_op jit(solution)/shard_map/ppermute | solution.py:305
  7.1 5.6 %collective-permute-start.1 = (bf16[32,896]{1,0:T(8,128)(2,1)S(1)}, bf16[32,896]{1,0:T(8,128)(2,1)S(1)}, u32[]{:S(2)}, u32[]{:S(2)}) collective-permute-start(bf16[32,896]{1,0:T(8,128)(2,1)S(1)} %add_convert_fusion.5), channel_id=1, source_target_pairs={{0,8},{8,16},{16,24},{24,0},{1,9},{9,17},{17,25},{25,1},{2,10},{10... | collective-permute-start | bytes 172040 | tf_op jit(solution)/shard_map/ppermute | solution.py:305
  12.8 9.1 %collective-permute-start.5 = (bf16[32,896]{1,0:T(8,128)(2,1)S(1)}, bf16[32,896]{1,0:T(8,128)(2,1)S(1)}, u32[]{:S(2)}, u32[]{:S(2)}) collective-permute-start(bf16[32,896]{1,0:T(8,128)(2,1)S(1)} %add_convert_fusion.4.slab_ref), channel_id=1, source_target_pairs={{0,64},{32,96},{64,128},{96,160},{128,192},{160,224},{192,0},{224,... | collective-permute-start | bytes 172040 | tf_op jit(solution)/shard_map/ppermute | solution.py:311
  16.2 6.1 %collective-permute-start.4 = (bf16[32,896]{1,0:T(8,128)(2,1)S(1)}, bf16[32,896]{1,0:T(8,128)(2,1)S(1)}, u32[]{:S(2)}, u32[]{:S(2)}) collective-permute-start(bf16[32,896]{1,0:T(8,128)(2,1)S(1)} %add_convert_fusion.4.slab_ref), channel_id=1, source_target_pairs={{0,32},{32,64},{64,96},{96,128},{128,160},{160,192},{192,224},{224... | collective-permute-start | bytes 172040 | tf_op jit(solution)/shard_map/ppermute | solution.py:311
  25.2 7.2 %collective-permute-start.6 = (bf16[32,896]{1,0:T(8,128)(2,1)S(1)}, bf16[32,896]{1,0:T(8,128)(2,1)S(1)}, u32[]{:S(2)}, u32[]{:S(2)}) collective-permute-start(bf16[32,896]{1,0:T(8,128)(2,1)S(1)} %triple.1), channel_id=1, source_target_pairs={{0,96},{32,128},{64,160},{96,192},{128,224},{160,0},{192,32},{224,... | collective-permute-start | bytes 172040 | tf_op jit(solution)/shard_map/ppermute | solution.py:311
  36.1 8.0 %collective-permute-start.9 = (bf16[128,768]{1,0:T(8,128)(2,1)S(1)}, bf16[128,768]{1,0:T(8,128)(2,1)S(1)}, u32[]{:S(2)}, u32[]{:S(2)}) collective-permute-start(bf16[128,768]{1,0:T(8,128)(2,1)S(1)} %get-tuple-element.84), channel_id=1, source_target_pairs={{0,1},{1,2},{2,3},{3,0},{4,5},{5,6},{6,7},{7,4},{8,9},{9,10},{10,1... | collective-permute-start | bytes 589832 | tf_op jit(solution)/shard_map/ppermute | solution.py:241
  37.8 9.3 %collective-permute-start.10 = (bf16[128,768]{1,0:T(8,128)(2,1)S(1)}, bf16[128,768]{1,0:T(8,128)(2,1)S(1)}, u32[]{:S(2)}, u32[]{:S(2)}) collective-permute-start(bf16[128,768]{1,0:T(8,128)(2,1)S(1)} %get-tuple-element.85), channel_id=1, source_target_pairs={{0,2},{1,3},{2,0},{3,1},{4,6},{5,7},{6,4},{7,5},{8,10},{9,11},{10,... | collective-permute-start | bytes 589832 | tf_op jit(solution)/shard_map/ppermute | solution.py:241
  38.7 10.8 %collective-permute-start.11 = (bf16[128,768]{1,0:T(8,128)(2,1)S(1)}, bf16[128,768]{1,0:T(8,128)(2,1)S(1)}, u32[]{:S(2)}, u32[]{:S(2)}) collective-permute-start(bf16[128,768]{1,0:T(8,128)(2,1)S(1)} %get-tuple-element.86), channel_id=1, source_target_pairs={{0,3},{1,0},{2,1},{3,2},{4,7},{5,4},{6,5},{7,6},{8,11},{9,8},{10,9... | collective-permute-start | bytes 589832 | tf_op jit(solution)/shard_map/ppermute | solution.py:241
  88.8 17.6 %collective-permute-start.14 = (bf16[4,768,768]{2,1,0:T(8,128)(2,1)S(1)}, bf16[4,768,768]{2,1,0:T(8,128)(2,1)S(1)}, u32[]{:S(2)}, u32[]{:S(2)}) collective-permute-start(bf16[4,768,768]{2,1,0:T(8,128)(2,1)S(1)} %get-tuple-element.99.mid0), channel_id=1, source_target_pairs={{0,4},{4,0},{1,5},{5,1},{2,6},{6,2},{3,7},{7,3},{8,12},{12,8},{9,1... | collective-permute-start | bytes 14155784 | tf_op jit(solution)/shard_map/ppermute | solution.py:245
  88.8 17.6 %collective-permute-start.15 = (bf16[4,360,768]{2,1,0:T(8,128)(2,1)S(1)}, bf16[4,360,768]{2,1,0:T(8,128)(2,1)S(1)}, u32[]{:S(2)}, u32[]{:S(2)}) collective-permute-start(bf16[4,360,768]{2,1,0:T(8,128)(2,1)S(1)} %get-tuple-element.100.out0), channel_id=1, source_target_pairs={{0,4},{4,0},{1,5},{5,1},{2,6},{6,2},{3,7},{7,3},{8,12},{12,8},{9,1... | collective-permute-start | bytes 6635528 | tf_op jit(solution)/shard_map/ppermute | solution.py:245
  89.4 15.3 %collective-permute-start.13 = (bf16[384,768]{1,0:T(8,128)(2,1)S(1)}, bf16[384,768]{1,0:T(8,128)(2,1)S(1)}, u32[]{:S(2)}, u32[]{:S(2)}) collective-permute-start(bf16[384,768]{1,0:T(8,128)(2,1)S(1)} %get-tuple-element.126.x0), channel_id=1, source_target_pairs={{0,3},{1,0},{2,1},{3,2},{4,7},{5,4},{6,5},{7,6},{8,11},{9,8},{10,9... | collective-permute-start | bytes 1769480 | tf_op jit(solution)/shard_map/ppermute | solution.py:241
  90.3 16.1 %collective-permute-start.12 = (bf16[384,768]{1,0:T(8,128)(2,1)S(1)}, bf16[384,768]{1,0:T(8,128)(2,1)S(1)}, u32[]{:S(2)}, u32[]{:S(2)}) collective-permute-start(bf16[384,768]{1,0:T(8,128)(2,1)S(1)} %get-tuple-element.126.x0), channel_id=1, source_target_pairs={{0,1},{1,2},{2,3},{3,0},{4,5},{5,6},{6,7},{7,4},{8,9},{9,10},{10,1... | collective-permute-start | bytes 1769480 | tf_op jit(solution)/shard_map/ppermute | solution.py:241
  106.3 15.3 %collective-permute-start.16 = (bf16[384,768]{1,0:T(8,128)(2,1)S(1)}, bf16[384,768]{1,0:T(8,128)(2,1)S(1)}, u32[]{:S(2)}, u32[]{:S(2)}) collective-permute-start(bf16[384,768]{1,0:T(8,128)(2,1)S(1)} %collective-permute-done.12.x3), channel_id=1, source_target_pairs={{0,1},{1,2},{2,3},{3,0},{4,5},{5,6},{6,7},{7,4},{8,9},{9,10},{10,1... | collective-permute-start | bytes 1769480 | tf_op jit(solution)/shard_map/ppermute | solution.py:241
  106.4 15.2 %collective-permute-start.20 = (bf16[384,768]{1,0:T(8,128)(2,1)S(1)}, bf16[384,768]{1,0:T(8,128)(2,1)S(1)}, u32[]{:S(2)}, u32[]{:S(2)}) collective-permute-start(bf16[384,768]{1,0:T(8,128)(2,1)S(1)} %get-tuple-element.113.x0), channel_id=1, source_target_pairs={{0,3},{1,0},{2,1},{3,2},{4,7},{5,4},{6,5},{7,6},{8,11},{9,8},{10,9... | collective-permute-start | bytes 1769480 | tf_op jit(solution)/shard_map/ppermute | solution.py:241
  121.6 15.3 %collective-permute-start.22 = (bf16[384,768]{1,0:T(8,128)(2,1)S(1)}, bf16[384,768]{1,0:T(8,128)(2,1)S(1)}, u32[]{:S(2)}, u32[]{:S(2)}) collective-permute-start(bf16[384,768]{1,0:T(8,128)(2,1)S(1)} %get-tuple-element.113.x0), channel_id=1, source_target_pairs={{0,1},{1,2},{2,3},{3,0},{4,5},{5,6},{6,7},{7,4},{8,9},{9,10},{10,1... | collective-permute-start | bytes 1769480 | tf_op jit(solution)/shard_map/ppermute | solution.py:241
  121.6 15.3 %collective-permute-start.21 = (bf16[384,768]{1,0:T(8,128)(2,1)S(1)}, bf16[384,768]{1,0:T(8,128)(2,1)S(1)}, u32[]{:S(2)}, u32[]{:S(2)}) collective-permute-start(bf16[384,768]{1,0:T(8,128)(2,1)S(1)} %collective-permute-done.20.x1), channel_id=1, source_target_pairs={{0,3},{1,0},{2,1},{3,2},{4,7},{5,4},{6,5},{7,6},{8,11},{9,8},{10,9... | collective-permute-start | bytes 1769480 | tf_op jit(solution)/shard_map/ppermute | solution.py:241
  133.4 15.5 %collective-permute-start.17 = (bf16[384,768]{1,0:T(8,128)(2,1)S(1)}, bf16[384,768]{1,0:T(8,128)(2,1)S(1)}, u32[]{:S(2)}, u32[]{:S(2)}) collective-permute-start(bf16[384,768]{1,0:T(8,128)(2,1)S(1)} %get-tuple-element.109), channel_id=1, source_target_pairs={{0,1},{1,2},{2,3},{3,0},{4,5},{5,6},{6,7},{7,4},{8,9},{9,10},{10,1... | collective-permute-start | bytes 1769480 | tf_op jit(solution)/shard_map/ppermute | solution.py:241
  133.5 16.9 %collective-permute-start.18 = (bf16[384,768]{1,0:T(8,128)(2,1)S(1)}, bf16[384,768]{1,0:T(8,128)(2,1)S(1)}, u32[]{:S(2)}, u32[]{:S(2)}) collective-permute-start(bf16[384,768]{1,0:T(8,128)(2,1)S(1)} %get-tuple-element.110), channel_id=1, source_target_pairs={{0,3},{1,0},{2,1},{3,2},{4,7},{5,4},{6,5},{7,6},{8,11},{9,8},{10,9... | collective-permute-start | bytes 1769480 | tf_op jit(solution)/shard_map/ppermute | solution.py:241
  145.8 14.9 %collective-permute-start.24 = (bf16[384,768]{1,0:T(8,128)(2,1)S(1)}, bf16[384,768]{1,0:T(8,128)(2,1)S(1)}, u32[]{:S(2)}, u32[]{:S(2)}) collective-permute-start(bf16[384,768]{1,0:T(8,128)(2,1)S(1)} %get-tuple-element.117), channel_id=1, source_target_pairs={{0,3},{1,0},{2,1},{3,2},{4,7},{5,4},{6,5},{7,6},{8,11},{9,8},{10,9... | collective-permute-start | bytes 1769480 | tf_op jit(solution)/shard_map/ppermute | solution.py:241
  150.5 17.7 %collective-permute-start.19 = (bf16[384,768]{1,0:T(8,128)(2,1)S(1)}, bf16[384,768]{1,0:T(8,128)(2,1)S(1)}, u32[]{:S(2)}, u32[]{:S(2)}) collective-permute-start(bf16[384,768]{1,0:T(8,128)(2,1)S(1)} %add_convert_fusion.3), channel_id=1, source_target_pairs={{0,1},{1,2},{2,3},{3,0},{4,5},{5,6},{6,7},{7,4},{8,9},{9,10},{10,1... | collective-permute-start | bytes 1769480 | tf_op jit(solution)/shard_map/ppermute | solution.py:241
  153.8 21.6 %collective-permute-start.23 = (bf16[384,768]{1,0:T(8,128)(2,1)S(1)}, bf16[384,768]{1,0:T(8,128)(2,1)S(1)}, u32[]{:S(2)}, u32[]{:S(2)}) collective-permute-start(bf16[384,768]{1,0:T(8,128)(2,1)S(1)} %get-tuple-element.115), channel_id=1, source_target_pairs={{0,1},{1,2},{2,3},{3,0},{4,5},{5,6},{6,7},{7,4},{8,9},{9,10},{10,1... | collective-permute-start | bytes 1769480 | tf_op jit(solution)/shard_map/ppermute | solution.py:241
  160.8 14.6 %collective-permute-start.25 = (bf16[384,768]{1,0:T(8,128)(2,1)S(1)}, bf16[384,768]{1,0:T(8,128)(2,1)S(1)}, u32[]{:S(2)}, u32[]{:S(2)}) collective-permute-start(bf16[384,768]{1,0:T(8,128)(2,1)S(1)} %add_convert_fusion.1), channel_id=1, source_target_pairs={{0,3},{1,0},{2,1},{3,2},{4,7},{5,4},{6,5},{7,6},{8,11},{9,8},{10,9... | collective-permute-start | bytes 1769480 | tf_op jit(solution)/shard_map/ppermute | solution.py:241
  208.8 7.2 %collective-permute-start.26 = (bf16[32,768]{1,0:T(8,128)(2,1)S(1)}, bf16[32,768]{1,0:T(8,128)(2,1)S(1)}, u32[]{:S(2)}, u32[]{:S(2)}) collective-permute-start(bf16[32,768]{1,0:T(8,128)(2,1)S(1)} %get-tuple-element.122), channel_id=1, source_target_pairs={{0,1},{1,2},{2,3},{3,0},{4,5},{5,6},{6,7},{7,4},{8,9},{9,10},{10,1... | collective-permute-start | bytes 147464 | tf_op jit(solution)/shard_map/ppermute | solution.py:241
  211.3 5.6 %collective-permute-start.27 = (bf16[32,768]{1,0:T(8,128)(2,1)S(1)}, bf16[32,768]{1,0:T(8,128)(2,1)S(1)}, u32[]{:S(2)}, u32[]{:S(2)}) collective-permute-start(bf16[32,768]{1,0:T(8,128)(2,1)S(1)} %get-tuple-element.123), channel_id=1, source_target_pairs={{0,2},{1,3},{2,0},{3,1},{4,6},{5,7},{6,4},{7,5},{8,10},{9,11},{10,... | collective-permute-start | bytes 147464 | tf_op jit(solution)/shard_map/ppermute | solution.py:241
  (19 other events, 165.6 us)
